TPU v7x, 32 devices: a whole 2x2x4 slice. The times are simulated.
32 devices in a mesh: freq: 2 (over x), tile: 16 (over z, y, core).
Axes of the slice: x: 2, y: 2, z: 4, core: 2. Of those that a mesh axis runs over, the one named last changes fastest.
Arguments:
- data: float32 [4, 2048, 256], P('freq', 'tile'), parts along dimension 0, may hold values from -6 to 6
- x_init: float32 [4, 8192, 256], P('freq', 'tile'), parts along dimension 0, may hold values from -6 to 6
- ufac: bfloat16 [4, 2048, 256], P('freq', 'tile'), parts along dimension 0, may hold values from -0.1875 to 0.1875
- vfac: bfloat16 [4, 4, 16, 8192], P('freq', None, None, 'tile'), parts along dimension 0, may hold values from -0.25 to 0.25
Outputs:
- solution: float32 [4, 8192, 256], P('freq', 'tile'), parts along dimension 0
- residual: float32 [4, 2048, 256], P('freq', 'tile'), parts along dimension 0
There are 2 independent parts, one for each index of `freq`. A program takes and returns all parts, laid end to end along the dimension named above; each array names one. Nothing has to cross between parts.
All inputs are finite; a program needn't handle non-finite values.
Results may differ from a plain program's by a relative error of at most 0.0058.
Values may be sent and summed in bfloat16 or wider, within the bound.
No kernel may reach another device: no remote copies, remote signals or barrier semaphores. Data moves between devices by JAX's collectives and lax.ppermute only.
A program may use at most 64 MiB of HBM per device.

v0:
```python
import functools

import jax
import jax.numpy as jnp
from jax import lax
from jax.experimental import pallas as pl
from jax.experimental.pallas import tpu as pltpu
from jax.sharding import PartitionSpec as P


ITERS = 2
STEP = 0.4
THRESHOLD = 0.4
VMEM_LIMIT = 24 << 20
PIECES = 4

f32 = jnp.float32
bf16 = jnp.bfloat16


def dot(a, b, dims=((1,), (0,))):
    return lax.dot_general(a, b, (dims, ((), ())), preferred_element_type=f32)


def swap_halves(a):
    return pltpu.roll(a, a.shape[1] // 2, 1)


def left_half(a):
    return lax.broadcasted_iota(jnp.int32, a.shape, 1) < a.shape[1] // 2


def times_i(a):
    s = swap_halves(a)
    return jnp.where(left_half(a), -s, s)


def interleave(re, im):
    low = left_half(re)
    return (
        jnp.where(low, re, swap_halves(im)),
        jnp.where(low, swap_halves(re), im),
    )


def slices_of(re, im, width):
    out = []
    for k in range(re.shape[1] // (2 * width)):
        cut = slice(2 * width * k, 2 * width * (k + 1))
        out.extend(interleave(re[:, cut], im[:, cut]))
    return out


def group_index(group):
    return lax.rem(lax.axis_index("tile"), group)


def split(block):
    high = block.astype(bf16)
    low = (block - high.astype(f32)).astype(bf16)
    return high, low


def send_coeffs(vcat, xr, xi, out, *, group, width):
    half = vcat.shape[0] // 2
    t1 = dot(vcat, xr)
    t2 = dot(vcat, xi)
    cr = t1[:half] + t2[half:]
    ci = t2[:half] - t1[half:]
    rank = out.shape[1]
    blocks = slices_of(cr, ci, width)
    for i in range(half // rank):
        for q in range(group):
            out[i * group + q] = blocks[q][i * rank:(i + 1) * rank].astype(bf16)


def flat_factors(vfac, cut=slice(None)):
    parts, rows, rank, _ = vfac.shape
    return vfac[:, :, :, cut].reshape(parts * rows * rank, -1)


def first_kernel(data, x, ufac, vfac, to_far, to_near, own, u_own, x_own, v_own, out, *, group, width):
    rows = data.shape[1]
    folds = ufac.shape[2] // (4 * width)
    step = rows // folds
    q = group_index(group)

    def run(waves, scratch, sems):
        wave_copy = pltpu.make_async_copy(data, waves, sems.at[0])
        v_copy = pltpu.make_async_copy(vfac, v_own, sems.at[1])
        u_copy = pltpu.make_async_copy(ufac, u_own, sems.at[2])
        x_copy = pltpu.make_async_copy(x, x_own, sems.at[3])
        for copy in (wave_copy, u_copy, v_copy, x_copy):
            copy.start()
        wave_copy.wait()
        for s, block in enumerate(slices_of(waves[0], waves[1], width)):
            scratch[jnp.bitwise_xor(q, s)] = block
        own[...] = scratch[0]
        for ref, base, b in ((to_near, 0, 1), (to_far, 0, 2), (to_far, step, 3)):
            high, low = split(scratch[b])
            for g in range(folds):
                cut = slice(g * step, (g + 1) * step)
                lane = 4 * width * g
                ref[base:base + step, lane:lane + 2 * width] = high[cut]
                ref[base:base + step, lane + 2 * width:lane + 4 * width] = low[cut]
        u_copy.wait()
        for part in range(2):
            to_near[step + rows * part:step + rows * (part + 1)] = u_own[part]
            to_far[2 * step + rows * part:2 * step + rows * (part + 1)] = u_own[part]
        v_copy.wait()
        x_copy.wait()
        send_coeffs(
            flat_factors(v_own), x_own[0].astype(bf16), x_own[1].astype(bf16), out, group=group, width=width
        )

    pl.run_scoped(
        run,
        pltpu.VMEM(data.shape, f32),
        pltpu.VMEM((group, rows, 2 * width), f32),
        pltpu.SemaphoreType.DMA((4,)),
    )


def row_kernel(coeffs, own, ufac, near, far, far_near, adjoint, *maybe_misfit, width):
    lanes = 2 * width
    rows = own.shape[0]
    c = coeffs[...].reshape(-1, lanes)
    ci = times_i(c.astype(f32)).astype(bf16)

    folds = ufac.shape[2] // (2 * lanes)
    step = rows // folds

    def joined(ref, base):
        cuts = [ref[base:base + step, 2 * lanes * g:2 * lanes * (g + 1)].astype(f32) for g in range(folds)]
        pair = jnp.concatenate(cuts, axis=0)
        return pair[:, :lanes] + pair[:, lanes:]

    def factors(ref, base):
        return ref[base:base + rows], ref[base + rows:base + 2 * rows]

    blocks = (
        (own[...], (ufac[0], ufac[1])),
        (joined(near, 0), factors(near, step)),
        (joined(far, 0), factors(far, 2 * step)),
        (joined(far_near, step), factors(far_near, 2 * step)),
    )
    total = None
    for b, (wave, (ur, ui)) in enumerate(blocks):
        misfit = wave - (dot(ur, c) + dot(ui, ci))
        if maybe_misfit:
            if b < 2:
                maybe_misfit[b][...] = misfit
            else:
                maybe_misfit[2][b - 2] = misfit
        mt = misfit.T.astype(bf16)
        mr, mi = mt[:width], mt[width:]
        turned = jnp.concatenate([mi, -mr], axis=0)
        term = dot(mt, ur) + dot(turned, ui)
        total = term if total is None else total + term
    flat = total.T.astype(bf16)
    rank = adjoint.shape[1]
    for j in range(adjoint.shape[0]):
        adjoint[j] = flat[j * rank:(j + 1) * rank]


def adjoint_sides(adjoint, *, group):
    count, rank, lanes = adjoint.shape
    rows = count // group
    a = adjoint[...].astype(f32).reshape(rows, group, rank, lanes)
    re, im = [], []
    for k in range(group // 2):
        even = a[:, 2 * k].reshape(rows * rank, lanes)
        odd = a[:, 2 * k + 1].reshape(rows * rank, lanes)
        r, i = interleave(even, odd)
        re.append(r)
        im.append(i)
    re = jnp.concatenate(re, axis=1)
    im = jnp.concatenate(im, axis=1)
    real_side = jnp.concatenate([re, -im], axis=0).astype(bf16)
    imag_side = jnp.concatenate([im, re], axis=0).astype(bf16)
    return real_side, imag_side


def shrink(sr, si):
    magnitude = jnp.sqrt(sr * sr + si * si)
    factor = jnp.maximum(magnitude - THRESHOLD, 0.0) / jnp.maximum(magnitude, THRESHOLD)
    return sr * factor, si * factor


def updated(sides, xr, xi, vcat):
    gr, gi = (dot(vcat, side, ((0,), (0,))) for side in sides)
    return shrink(xr + STEP * gr, xi + STEP * gi)


def middle_kernel(adjoint, x, vfac, x_new, out, *, group, width):
    vcat = flat_factors(vfac)
    xr, xi = updated(adjoint_sides(adjoint, group=group), x[0], x[1], vcat)
    x_new[0] = xr
    x_new[1] = xi
    send_coeffs(vcat, xr.astype(bf16), xi.astype(bf16), out, group=group, width=width)


def last_kernel(adjoint, x, vfac, x_new, *, group, width):
    sources = x.shape[1]
    piece = sources // PIECES

    def run(stage, sems):
        sides = adjoint_sides(adjoint, group=group)
        copies = []
        for k in range(PIECES):
            cut = slice(k * piece, (k + 1) * piece)
            stage[0, cut], stage[1, cut] = updated(sides, x[0, cut], x[1, cut], flat_factors(vfac, cut))
            copies.append(pltpu.make_async_copy(stage.at[:, cut], x_new.at[:, cut], sems.at[k]))
            copies[-1].start()
        for copy in copies:
            copy.wait()

    pl.run_scoped(run, pltpu.VMEM(x.shape, f32), pltpu.SemaphoreType.DMA((PIECES,)))


def residual_kernel(misfit, near, far, far_near, out, *, group, width):
    q = group_index(group)

    def place(scratch, stage, sem):
        scratch[0] = misfit[...]
        scratch[1] = near[...]
        scratch[2] = far[0]
        scratch[3] = far_near[1]
        pieces = [scratch[jnp.bitwise_xor(q, s)] for s in range(group)]
        for k in range(group // 2):
            re, im = interleave(pieces[2 * k], pieces[2 * k + 1])
            stage[0, :, 2 * width * k:2 * width * (k + 1)] = re
            stage[1, :, 2 * width * k:2 * width * (k + 1)] = im
        copy = pltpu.make_async_copy(stage, out, sem)
        copy.start()
        copy.wait()

    pl.run_scoped(
        place,
        pltpu.VMEM((group,) + misfit.shape, f32),
        pltpu.VMEM(out.shape, f32),
        pltpu.SemaphoreType.DMA(()),
    )


def call(kernel, out_shape, *args, from_hbm=False, **static):
    on_chip = pl.BlockSpec(memory_space=pltpu.VMEM)
    off_chip = pl.BlockSpec(memory_space=pltpu.HBM)
    space = pltpu.HBM if from_hbm else pltpu.VMEM
    many = isinstance(out_shape, tuple)

    def spec(out):
        return off_chip if isinstance(out, jax.ShapeDtypeStruct) else on_chip

    return pl.pallas_call(
        functools.partial(kernel, **static),
        out_shape=out_shape,
        in_specs=[off_chip if from_hbm else on_chip] * len(args),
        out_specs=tuple(map(spec, out_shape)) if many else spec(out_shape),
        compiler_params=pltpu.CompilerParams(vmem_limit_bytes=VMEM_LIMIT),
    )(*(pltpu.with_memory_space_constraint(arg, space) for arg in args))


def body(data, x_init, ufac, vfac):
    tiles = lax.axis_size("tile")
    tile_rows, rank, _ = vfac.shape[1:]
    rows = data.shape[1]
    points = data.shape[2]
    group = tiles // tile_rows
    assert group == 4
    width = points // group
    lanes = 2 * width
    static = dict(group=group, width=width)
    shape = pltpu.VMEM
    result = jax.ShapeDtypeStruct

    def exchange(value, bit):
        return lax.ppermute(value, "tile", [(s, s ^ bit) for s in range(tiles)])

    def spread(value):
        return lax.all_to_all(value, "tile", split_axis=0, concat_axis=0, tiled=True)

    wide = ufac.shape[2]
    step = rows * 2 * lanes // wide
    assert wide % (2 * lanes) == 0 and step % 16 == 0
    chunks = shape((tiles, rank, lanes), bf16)
    to_far, to_near, own, ufac, estimate, vfac, coeffs = call(
        first_kernel,
        (
            shape((2 * rows + 2 * step, wide), bf16),
            shape((2 * rows + step, wide), bf16),
            shape((rows, lanes), f32),
            shape(ufac.shape, bf16),
            shape(x_init.shape, f32),
            shape(vfac.shape, bf16),
            chunks,
        ),
        data, x_init, ufac, vfac, from_hbm=True, **static,
    )
    far = exchange(to_far, 2)
    near = exchange(to_near, 1)
    far_near = exchange(far, 1)
    for iteration in range(ITERS):
        last = iteration == ITERS - 1
        block = shape((rows, lanes), f32)
        outs = (chunks, block, block, shape((2, rows, lanes), f32)) if last else (chunks,)
        row = call(row_kernel, outs, spread(coeffs), own, ufac, near, far, far_near, width=width)
        if last:
            _, misfit, to_near, to_far = row
            misfit_far = exchange(to_far, 2)
            misfit_near = exchange(to_near, 1)
            misfit_far_near = exchange(misfit_far, 1)
        adjoint = spread(row[0])
        if last:
            estimate = call(last_kernel, result(x_init.shape, f32), adjoint, estimate, vfac, **static)
        else:
            estimate, coeffs = call(
                middle_kernel, (shape(x_init.shape, f32), chunks), adjoint, estimate, vfac, **static
            )
    residual = call(
        residual_kernel, result(data.shape, f32), misfit, misfit_near, misfit_far, misfit_far_near, **static
    )
    return (estimate, residual)


def solution(mesh):
    in_specs = (
        P("freq", "tile", None),
        P("freq", "tile", None),
        P("freq", "tile", None),
        P("freq", None, None, "tile"),
    )
    out_specs = (P("freq", "tile", None), P("freq", "tile", None))
    return jax.shard_map(body, mesh=mesh, in_specs=in_specs, out_specs=out_specs, check_vma=False)
```

profile of v0, /device:TPU:0, one launch (start us, length us, event | category | flops | bytes accessed | tf_op | source)
XLA Modules:
  0.0 64.7 jit_solution(17951358087502367579)
XLA Ops:
  0.6 1.8 %shard_map.59 = (bf16[512,256]{1,0:T(8,128)(2,1)S(1)}, bf16[384,256]{1,0:T(8,128)(2,1)S(1)}, f32[128,128]{1,0:T(8,128)S(1)}, bf16[2,128,256]{2,1,0:T(8,128)(2,1)...) custom-call(f32[2,128,256]{2,1,0:T(8,128)} %data.1, ...), custom_call_target="tpu_custom_call" | custom-call | tf_op jit(solution)/shard_map/pallas_call | solution.py:255
  2.4 3.1 %collective-permute-start.1 = (bf16[512,256]{1,0:T(8,128)(2,1)S(1)}, bf16[512,256]{1,0:T(8,128)(2,1)S(1)}, u32[]{:S(2)}, u32[]{:S(2)}) collective-permute-start(bf16[512,256]{1,0:T(8,128)(2,1)S(1)} %get-tuple-element.19), channel_id=1, source_target_pairs={{0,2},{1,3},{2,0},{3,1},{4,6},{5,7},{6,4},{7,5},{8,10},{9,11},{10,... | collective-permute-start | bytes 786440 | tf_op jit(solution)/shard_map/ppermute | solution.py:278
  5.5 6.3 %collective-permute-done.1.far = bf16[512,256]{1,0:T(8,128)(2,1)S(1)} collective-permute-done((bf16[512,256]{1,0:T(8,128)(2,1)S(1)}, bf16[512,256]{1,0:T(8,128)(2,1)S(1)}, u32[]{:S(2)}, u32[]{:S(2)}) %collective-permute-start.1) | collective-permute-done | bytes 262176 | tf_op jit(solution)/shard_map/ppermute | solution.py:278
  11.8 0.0 collective-permute-start.2
  11.8 0.5 collective-permute-start
  12.3 12.8 %all_to_all.20.coeffs = bf16[16,16,128]{2,1,0:T(8,128)(2,1)S(1)} all-to-all(bf16[16,16,128]{2,1,0:T(8,128)(2,1)S(1)} %get-tuple-element.15), channel_id=1, replica_groups=mesh['freq'=2,'tile'=16] {'tile'}, dimensions={0} | all-to-all | bytes 131072 | tf_op jit(solution)/shard_map/all_to_all | solution.py:281
  25.1 0.0 collective-permute-done.near
  25.1 0.0 collective-permute-done.2.far_near
  25.1 0.8 %shard_map.60 = bf16[16,16,128]{2,1,0:T(8,128)(2,1)S(1)} custom-call(bf16[16,16,128]{2,1,0:T(8,128)(2,1)S(1)} %all_to_all.20.coeffs, f32[128,128]{1,0:T(8,128)S(1)} %get-tuple-element.16.own, bf16[2,128,256]{2,1,0:T(8,128)(2,1)S(1)} %get-tuple-element.17.ufac, bf16[384,256]{1,0:T(8,128)(2,1)S(1)} %collective-permute-done.near, ...), custom_call_target="tpu_custom_call" | custom-call | tf_op jit(solution)/shard_map/pallas_call | solution.py:255
  25.9 9.5 %all_to_all.21.adjoint = bf16[16,16,128]{2,1,0:T(8,128)(2,1)S(1)} all-to-all(bf16[16,16,128]{2,1,0:T(8,128)(2,1)S(1)} %shard_map.60), channel_id=1, replica_groups=mesh['freq'=2,'tile'=16] {'tile'}, dimensions={0} | all-to-all | bytes 131072 | tf_op jit(solution)/shard_map/all_to_all | solution.py:281
  35.4 0.9 %shard_map.61 = (f32[2,512,256]{2,1,0:T(8,128)S(1)}, bf16[16,16,128]{2,1,0:T(8,128)(2,1)S(1)}) custom-call(bf16[16,16,128]{2,1,0:T(8,128)(2,1)S(1)} %all_to_all.21.adjoint, f32[2,512,256]{2,1,0:T(8,128)S(1)} %get-tuple-element.20.x, bf16[2,4,16,512]{3,2,1,0:T(8,128)(2,1)S(1)} %get-tuple-element.21.vfac), custom_call_target="tpu_custom_call" | custom-call | tf_op jit(solution)/shard_map/pallas_call | solution.py:255
  36.3 9.5 %all_to_all.22.coeffs = bf16[16,16,128]{2,1,0:T(8,128)(2,1)S(1)} all-to-all(bf16[16,16,128]{2,1,0:T(8,128)(2,1)S(1)} %get-tuple-element.22), channel_id=1, replica_groups=mesh['freq'=2,'tile'=16] {'tile'}, dimensions={0} | all-to-all | bytes 131072 | tf_op jit(solution)/shard_map/all_to_all | solution.py:281
  45.8 1.4 %shard_map.62 = (bf16[16,16,128]{2,1,0:T(8,128)(2,1)}, f32[128,128]{1,0:T(8,128)S(1)}, f32[128,128]{1,0:T(8,128)S(1)}, f32[2,128,128]{2,1,0:T(8,128)S(1)}) custom-call(bf16[16,16,128]{2,1,0:T(8,128)(2,1)S(1)} %all_to_all.22.coeffs, f32[128,128]{1,0:T(8,128)S(1)} %get-tuple-element.16.own, bf16[2,128,256]{2,1,0:T(8,128)(2,1)S(1)} %get-tuple-element.17.ufac, ...), custom_call_target="tpu_custom_call" | custom-call | tf_op jit(solution)/shard_map/pallas_call | solution.py:255
  47.2 0.1 collective-permute-start.4
  47.3 4.9 %collective-permute-done.4.far = f32[2,128,128]{2,1,0:T(8,128)S(1)} collective-permute-done((f32[2,128,128]{2,1,0:T(8,128)S(1)}, f32[2,128,128]{2,1,0:T(8,128)S(1)}, u32[]{:S(2)}, u32[]{:S(2)}) %collective-permute-start.4) | collective-permute-done | bytes 131104 | tf_op jit(solution)/shard_map/ppermute | solution.py:278
  52.2 0.0 collective-permute-start.5
  52.2 3.5 %all-to-all-start.3 = ((bf16[16,16,128]{2,1,0:T(8,128)(2,1)}), bf16[16,16,128]{2,1,0:T(8,128)(2,1)S(1)}, u32[]{:S(2)}, u32[]{:S(2)}) async-start(bf16[16,16,128]{2,1,0:T(8,128)(2,1)} %get-tuple-element.23), calls=%async_computation.3 | async-start | bytes 131072 | tf_op jit(solution)/shard_map/all_to_all | solution.py:281
  55.7 0.5 collective-permute-start.3
  56.2 6.4 %all-to-all-done.3.adjoint = bf16[16,16,128]{2,1,0:T(8,128)(2,1)S(1)} async-done(((bf16[16,16,128]{2,1,0:T(8,128)(2,1)}), bf16[16,16,128]{2,1,0:T(8,128)(2,1)S(1)}, u32[]{:S(2)}, u32[]{:S(2)}) %all-to-all-start.3) | async-done | bytes 65568 | tf_op jit(solution)/shard_map/all_to_all | solution.py:281
  62.6 1.3 %shard_map.63 = f32[2,512,256]{2,1,0:T(8,128)} custom-call(bf16[16,16,128]{2,1,0:T(8,128)(2,1)S(1)} %all-to-all-done.3.adjoint, f32[2,512,256]{2,1,0:T(8,128)S(1)} %get-tuple-element.24.x, bf16[2,4,16,512]{3,2,1,0:T(8,128)(2,1)S(1)} %get-tuple-element.21.vfac), custom_call_target="tpu_custom_call" | custom-call | tf_op jit(solution)/shard_map/pallas_call | solution.py:255
  63.9 0.0 collective-permute-done.3.near
  63.9 0.0 collective-permute-done.5.far_near
  63.9 0.9 %shard_map.64 = f32[2,128,256]{2,1,0:T(8,128)} custom-call(f32[128,128]{1,0:T(8,128)S(1)} %get-tuple-element.25.misfit, f32[128,128]{1,0:T(8,128)S(1)} %collective-permute-done.3.near, f32[2,128,128]{2,1,0:T(8,128)S(1)} %collective-permute-done.4.far, f32[2,128,128]{2,1,0:T(8,128)S(1)} %collective-permute-done.5.far_near), custom_call_target="tpu_custom_call" | custom-call | tf_op jit(solution)/shard_map/pallas_call | solution.py:255
Async XLA Ops:
  2.4 9.4 %collective-permute-start.1 = (bf16[512,256]{1,0:T(8,128)(2,1)S(1)}, bf16[512,256]{1,0:T(8,128)(2,1)S(1)}, u32[]{:S(2)}, u32[]{:S(2)}) collective-permute-start(bf16[512,256]{1,0:T(8,128)(2,1)S(1)} %get-tuple-element.19), channel_id=1, source_target_pairs={{0,2},{1,3},{2,0},{3,1},{4,6},{5,7},{6,4},{7,5},{8,10},{9,11},{10,... | collective-permute-start | bytes 786440 | tf_op jit(solution)/shard_map/ppermute | solution.py:278
  11.8 13.4 %collective-permute-start.2 = (bf16[512,256]{1,0:T(8,128)(2,1)S(1)}, bf16[512,256]{1,0:T(8,128)(2,1)S(1)}, u32[]{:S(2)}, u32[]{:S(2)}) collective-permute-start(bf16[512,256]{1,0:T(8,128)(2,1)S(1)} %collective-permute-done.1.far), channel_id=1, source_target_pairs={{0,1},{1,0},{2,3},{3,2},{4,5},{5,4},{6,7},{7,6},{8,9},{9,8},{10,11... | collective-permute-start | bytes 786440 | tf_op jit(solution)/shard_map/ppermute | solution.py:278
  11.8 13.4 %collective-permute-start = (bf16[384,256]{1,0:T(8,128)(2,1)S(1)}, bf16[384,256]{1,0:T(8,128)(2,1)S(1)}, u32[]{:S(2)}, u32[]{:S(2)}) collective-permute-start(bf16[384,256]{1,0:T(8,128)(2,1)S(1)} %get-tuple-element.18), channel_id=1, source_target_pairs={{0,1},{1,0},{2,3},{3,2},{4,5},{5,4},{6,7},{7,6},{8,9},{9,8},{10,11... | collective-permute-start | bytes 589832 | tf_op jit(solution)/shard_map/ppermute | solution.py:278
  47.2 5.0 %collective-permute-start.4 = (f32[2,128,128]{2,1,0:T(8,128)S(1)}, f32[2,128,128]{2,1,0:T(8,128)S(1)}, u32[]{:S(2)}, u32[]{:S(2)}) collective-permute-start(f32[2,128,128]{2,1,0:T(8,128)S(1)} %get-tuple-element.27), channel_id=1, source_target_pairs={{0,2},{1,3},{2,0},{3,1},{4,6},{5,7},{6,4},{7,5},{8,10},{9,11},{10,... | collective-permute-start | bytes 393224 | tf_op jit(solution)/shard_map/ppermute | solution.py:278
  52.2 11.7 %collective-permute-start.5 = (f32[2,128,128]{2,1,0:T(8,128)S(1)}, f32[2,128,128]{2,1,0:T(8,128)S(1)}, u32[]{:S(2)}, u32[]{:S(2)}) collective-permute-start(f32[2,128,128]{2,1,0:T(8,128)S(1)} %collective-permute-done.4.far), channel_id=1, source_target_pairs={{0,1},{1,0},{2,3},{3,2},{4,5},{5,4},{6,7},{7,6},{8,9},{9,8},{10,11... | collective-permute-start | bytes 393224 | tf_op jit(solution)/shard_map/ppermute | solution.py:278
  52.2 10.4 %all-to-all-start.3 = ((bf16[16,16,128]{2,1,0:T(8,128)(2,1)}), bf16[16,16,128]{2,1,0:T(8,128)(2,1)S(1)}, u32[]{:S(2)}, u32[]{:S(2)}) async-start(bf16[16,16,128]{2,1,0:T(8,128)(2,1)} %get-tuple-element.23), calls=%async_computation.3 | async-start | bytes 131072 | tf_op jit(solution)/shard_map/all_to_all | solution.py:281
  55.7 8.2 %collective-permute-start.3 = (f32[128,128]{1,0:T(8,128)S(1)}, f32[128,128]{1,0:T(8,128)S(1)}, u32[]{:S(2)}, u32[]{:S(2)}) collective-permute-start(f32[128,128]{1,0:T(8,128)S(1)} %get-tuple-element.26), channel_id=1, source_target_pairs={{0,1},{1,0},{2,3},{3,2},{4,5},{5,4},{6,7},{7,6},{8,9},{9,8},{10,11... | collective-permute-start | bytes 196616 | tf_op jit(solution)/shard_map/ppermute | solution.py:278
where the time goes:
time: 65 us; the launch traced here: 64.7 us
  blocking collectives  31.8 us (49%)
  waiting for transfers between devices  17.6 us (27%)
  starting transfers between devices  7.66 us (12%)
  Pallas kernels  7.04 us (11%)
  between operations  0.67 us (1%)
    all_to_all x3, blocking collectives, spread(): lax.all_to_all(value, 'tile', split_axis=0, concat_axis=0, tiled=True)  31.8 us
    ppermute x6, waiting for transfers between devices, exchange(): return lax.ppermute(value, 'tile', [(s, s ^ bit) for s in range(tiles)])  11.2 us
    pallas_call x6, Pallas kernels, call(): pl.pallas_call(functools.partial(kernel, **static), out_shape=out_shape,...  7.04 us
    all_to_all x1, waiting for transfers between devices, spread(): lax.all_to_all(value, 'tile', split_axis=0, concat_axis=0, tiled=True)  6.39 us
    ppermute x6, starting transfers between devices, exchange(): return lax.ppermute(value, 'tile', [(s, s ^ bit) for s in range(tiles)])  4.15 us
    all_to_all x1, starting transfers between devices, spread(): lax.all_to_all(value, 'tile', split_axis=0, concat_axis=0, tiled=True)  3.5 us
  transfers between devices with their start and end apart: 7, of which 3 were waited for; matrix products, arithmetic and copies ran while one was open for 0% of the time, Pallas kernels for 2%

commit v1 on v0

--- a/solution.py
+++ b/solution.py
@@ -8,7 +8,6 @@
 from jax.sharding import PartitionSpec as P
 
 
-ITERS = 2
 STEP = 0.4
 THRESHOLD = 0.4
 VMEM_LIMIT = 24 << 20
@@ -53,6 +52,10 @@
 
 def group_index(group):
     return lax.rem(lax.axis_index("tile"), group)
+
+
+def row_index(group):
+    return lax.div(lax.axis_index("tile"), group)
 
 
 def split(block):
@@ -121,12 +124,10 @@
     )
 
 
-def row_kernel(coeffs, own, ufac, near, far, far_near, adjoint, *maybe_misfit, width):
+def row_core(c, own, ufac, near, far, corner, misfits, width):
     lanes = 2 * width
     rows = own.shape[0]
-    c = coeffs[...].reshape(-1, lanes)
     ci = times_i(c.astype(f32)).astype(bf16)
-
     folds = ufac.shape[2] // (2 * lanes)
     step = rows // folds
 
@@ -142,43 +143,165 @@
         (own[...], (ufac[0], ufac[1])),
         (joined(near, 0), factors(near, step)),
         (joined(far, 0), factors(far, 2 * step)),
-        (joined(far_near, step), factors(far_near, 2 * step)),
+        (joined(corner, step), factors(corner, 2 * step)),
     )
     total = None
     for b, (wave, (ur, ui)) in enumerate(blocks):
         misfit = wave - (dot(ur, c) + dot(ui, ci))
-        if maybe_misfit:
-            if b < 2:
-                maybe_misfit[b][...] = misfit
-            else:
-                maybe_misfit[2][b - 2] = misfit
+        if misfits and b < 2:
+            misfits[b][...] = misfit
+        elif misfits:
+            misfits[2][b - 2] = misfit
         mt = misfit.T.astype(bf16)
         mr, mi = mt[:width], mt[width:]
         turned = jnp.concatenate([mi, -mr], axis=0)
         term = dot(mt, ur) + dot(turned, ui)
         total = term if total is None else total + term
-    flat = total.T.astype(bf16)
+    return total.T.astype(bf16)
+
+
+def to_chunks(flat, adjoint):
     rank = adjoint.shape[1]
     for j in range(adjoint.shape[0]):
         adjoint[j] = flat[j * rank:(j + 1) * rank]
+
+
+def row_kernel(coeffs, own, ufac, near, far, corner, adjoint, *misfits, width):
+    c = coeffs[...].reshape(-1, 2 * width)
+    to_chunks(row_core(c, own, ufac, near, far, corner, misfits, width), adjoint)
+
+
+def row_first_kernel(coeffs, own, ufac, near, far, corner, *pieces, group, width):
+    z = row_index(group)
+    rank = coeffs.shape[1]
+    c = coeffs[...].reshape(-1, 2 * width)
+    flat = row_core(c, own, ufac, near, far, corner, (), width)
+
+    def place(scratch):
+        for j in range(flat.shape[0] // rank):
+            scratch[jnp.bitwise_xor(z, j // group), j % group] = flat[j * rank:(j + 1) * rank]
+        for b, piece in enumerate(pieces):
+            piece[...] = scratch[b]
+
+    pl.run_scoped(place, pltpu.VMEM((len(pieces),) + pieces[0].shape, bf16))
+
+
+def row_last_kernel(*refs, group, width, count):
+    pieces, (own, ufac, near, far, corner, adjoint), misfits = refs[:count], refs[count:count + 6], refs[count + 6:]
+    z = row_index(group)
+
+    def run(scratch):
+        for b, piece in enumerate(pieces):
+            scratch[jnp.bitwise_xor(z, b)] = piece[...]
+        c = scratch[...].reshape(-1, 2 * width)
+        to_chunks(row_core(c, own, ufac, near, far, corner, misfits, width), adjoint)
+
+    pl.run_scoped(run, pltpu.VMEM((count,) + pieces[0].shape, bf16))
+
+
+def pack_kernel(x, vfac, to_far, to_near, own, *, group, width):
+    q = group_index(group)
+    sources = x.shape[1]
+    lanes = 2 * width
+    vcat = flat_factors(vfac)
+    tall = vcat.shape[0]
+
+    def place(scratch):
+        for s, block in enumerate(slices_of(x[0], x[1], width)):
+            scratch[jnp.bitwise_xor(q, s)] = block.astype(bf16)
+        own[...] = scratch[0]
+        to_near[:sources] = scratch[1]
+        to_far[:sources, :lanes] = scratch[2]
+        to_far[:sources, lanes:] = scratch[3]
+
+    pl.run_scoped(place, pltpu.VMEM((group, sources, lanes), bf16))
+    for ref in (to_near, to_far):
+        wide = ref.shape[1]
+        for h in range(sources // wide):
+            ref[sources + h * tall:sources + (h + 1) * tall] = flat_factors(vfac, slice(h * wide, (h + 1) * wide))
+
+
+def middle_columns_kernel(*refs, group, width, count):
+    pieces, refs = refs[:count], refs[count:]
+    (x_own, v_own, near, far, corner), refs = refs[:5], refs[5:]
+    outs, (adj_own, adj_near, adj_far) = refs[:count], refs[count:]
+    q = group_index(group)
+    z = row_index(group)
+    sources, lanes = x_own.shape
+    rank = pieces[0].shape[1]
+    side = count * rank
+    tall = 2 * side
+
+    def factors(ref):
+        wide = ref.shape[1]
+        cuts = [ref[sources + h * tall:sources + (h + 1) * tall] for h in range(sources // wide)]
+        return jnp.concatenate(cuts, axis=1)
+
+    def run(adj, coeffs):
+        for b, piece in enumerate(pieces):
+            for k in range(group):
+                adj[k, jnp.bitwise_xor(z, b)] = piece[jnp.bitwise_xor(q, k)]
+        columns = (
+            (x_own[...], flat_factors(v_own)),
+            (near[:sources], factors(near)),
+            (far[:sources, :lanes], factors(far)),
+            (corner[:sources, lanes:], factors(corner)),
+        )
+        for k, (x, vcat) in enumerate(columns):
+            a = adj[k].reshape(side, lanes)
+            if k == 0:
+                adj_own[...] = a
+            elif k == 1:
+                adj_near[...] = a
+            else:
+                adj_far[k - 2] = a
+            turned = times_i(a.astype(f32)).astype(bf16)
+            s = x.astype(f32) + STEP * dot(vcat, jnp.concatenate([a, turned], axis=0), ((0,), (0,)))
+            square = s * s
+            magnitude = jnp.sqrt(square + swap_halves(square))
+            factor = jnp.maximum(magnitude - THRESHOLD, 0.0) / jnp.maximum(magnitude, THRESHOLD)
+            t = dot(vcat, (s * factor).astype(bf16))
+            c = (t[:side] - times_i(t[side:])).astype(bf16)
+            for i in range(count):
+                coeffs[i, jnp.bitwise_xor(q, k)] = c[i * rank:(i + 1) * rank]
+        for b, out in enumerate(outs):
+            out[...] = coeffs[jnp.bitwise_xor(z, b)]
+
+    pl.run_scoped(
+        run,
+        pltpu.VMEM((group, count, rank, lanes), bf16),
+        pltpu.VMEM((count, group, rank, lanes), bf16),
+    )
+
+
+def own_column_kernel(adj_own, adj_near, adj_far, adj_corner, x, vfac, x_new, *, group, width):
+    q = group_index(group)
+
+    def run(scratch):
+        scratch[0] = adj_own[...]
+        scratch[1] = adj_near[...]
+        scratch[2] = adj_far[0]
+        scratch[3] = adj_corner[1]
+        sides = sides_of([scratch[jnp.bitwise_xor(q, s)].astype(f32) for s in range(group)])
+        x_new[0], x_new[1] = updated(sides, x[0], x[1], flat_factors(vfac))
+
+    pl.run_scoped(run, pltpu.VMEM((group,) + adj_own.shape, bf16))
+
+
+def sides_of(quarters):
+    pairs = [interleave(*quarters[k:k + 2]) for k in range(0, len(quarters), 2)]
+    re = jnp.concatenate([r for r, _ in pairs], axis=1)
+    im = jnp.concatenate([i for _, i in pairs], axis=1)
+    real_side = jnp.concatenate([re, -im], axis=0).astype(bf16)
+    imag_side = jnp.concatenate([im, re], axis=0).astype(bf16)
+    return real_side, imag_side
 
 
 def adjoint_sides(adjoint, *, group):
     count, rank, lanes = adjoint.shape
     rows = count // group
     a = adjoint[...].astype(f32).reshape(rows, group, rank, lanes)
-    re, im = [], []
-    for k in range(group // 2):
-        even = a[:, 2 * k].reshape(rows * rank, lanes)
-        odd = a[:, 2 * k + 1].reshape(rows * rank, lanes)
-        r, i = interleave(even, odd)
-        re.append(r)
-        im.append(i)
-    re = jnp.concatenate(re, axis=1)
-    im = jnp.concatenate(im, axis=1)
-    real_side = jnp.concatenate([re, -im], axis=0).astype(bf16)
-    imag_side = jnp.concatenate([im, re], axis=0).astype(bf16)
-    return real_side, imag_side
+    return sides_of([a[:, s].reshape(rows * rank, lanes) for s in range(group)])
 
 
 def shrink(sr, si):
@@ -299,28 +422,66 @@
     )
     far = exchange(to_far, 2)
     near = exchange(to_near, 1)
-    far_near = exchange(far, 1)
-    for iteration in range(ITERS):
-        last = iteration == ITERS - 1
-        block = shape((rows, lanes), f32)
-        outs = (chunks, block, block, shape((2, rows, lanes), f32)) if last else (chunks,)
-        row = call(row_kernel, outs, spread(coeffs), own, ufac, near, far, far_near, width=width)
-        if last:
-            _, misfit, to_near, to_far = row
-            misfit_far = exchange(to_far, 2)
-            misfit_near = exchange(to_near, 1)
-            misfit_far_near = exchange(misfit_far, 1)
-        adjoint = spread(row[0])
-        if last:
-            estimate = call(last_kernel, result(x_init.shape, f32), adjoint, estimate, vfac, **static)
-        else:
-            estimate, coeffs = call(
-                middle_kernel, (shape(x_init.shape, f32), chunks), adjoint, estimate, vfac, **static
-            )
+    corner = exchange(far, 1)
+    gathered = (own, ufac, near, far, corner)
+    block = shape((rows, lanes), f32)
+    row_outs = (chunks, block, block, shape((2, rows, lanes), f32))
+    received = spread(coeffs)
+    if tile_rows == 4:
+        sources = x_init.shape[1]
+        tall = 2 * tile_rows * rank
+        piece = shape((group, rank, lanes), bf16)
+        side = (tile_rows * rank, lanes)
+        counted = dict(count=tile_rows, **static)
+
+        def along_rows(pieces):
+            order = {b: exchange(pieces[b], b * group) for b in range(tile_rows - 1, 0, -1)}
+            return [pieces[0]] + [order[b] for b in range(1, tile_rows)]
+
+        x_far, x_near, x_own = call(
+            pack_kernel,
+            (
+                shape((sources + tall * sources // (2 * lanes), 2 * lanes), bf16),
+                shape((sources + tall * sources // lanes, lanes), bf16),
+                shape((sources, lanes), bf16),
+            ),
+            estimate, vfac, **static,
+        )
+        x_far = exchange(x_far, 2)
+        x_near = exchange(x_near, 1)
+        x_corner = exchange(x_far, 1)
+        pieces = call(row_first_kernel, (piece,) * tile_rows, received, *gathered, **static)
+        pieces = along_rows(pieces)
+        *pieces, adj_own, adj_near, adj_far = call(
+            middle_columns_kernel,
+            (piece,) * tile_rows + (shape(side, bf16), shape(side, bf16), shape((2,) + side, bf16)),
+            *pieces, x_own, vfac, x_near, x_far, x_corner, **counted,
+        )
+        pieces = along_rows(pieces)
+        adj_far = exchange(adj_far, 2)
+        adj_near = exchange(adj_near, 1)
+        adj_corner = exchange(adj_far, 1)
+        row = call(row_last_kernel, row_outs, *pieces, *gathered, **counted)
+        estimate = call(
+            own_column_kernel, shape(x_init.shape, f32),
+            adj_own, adj_near, adj_far, adj_corner, estimate, vfac, **static,
+        )
+    else:
+        (pieces,) = call(row_kernel, (chunks,), received, *gathered, width=width)
+        estimate, coeffs = call(
+            middle_kernel, (shape(x_init.shape, f32), chunks), spread(pieces), estimate, vfac, **static
+        )
+        row = call(row_kernel, row_outs, spread(coeffs), *gathered, width=width)
+    adjoint, misfit, to_near, to_far = row
+    misfit_far = exchange(to_far, 2)
+    misfit_near = exchange(to_near, 1)
+    misfit_corner = exchange(misfit_far, 1)
+    adjoint = spread(adjoint)
+    solved = call(last_kernel, result(x_init.shape, f32), adjoint, estimate, vfac, **static)
     residual = call(
-        residual_kernel, result(data.shape, f32), misfit, misfit_near, misfit_far, misfit_far_near, **static
-    )
-    return (estimate, residual)
+        residual_kernel, result(data.shape, f32), misfit, misfit_near, misfit_far, misfit_corner, **static
+    )
+    return (solved, residual)
 
 
 def solution(mesh):

time: 65 us -> 71.3 us (1.097)
  blocking collectives: 31.8 us -> 13 us
  waiting for transfers between devices: 17.6 us -> 30.7 us
  starting transfers between devices: 7.66 us -> 18.5 us
  Pallas kernels: 7.04 us -> 8.22 us
    all_to_all x3 -> x1, blocking collectives: 31.8 us -> 13 us  [spread(): lax.all_to_all(value, 'tile', split_axis=0, concat_axis=0, tiled=True)]
    ppermute x6 -> x18, waiting for transfers between devices: 11.2 us -> 29.8 us  [exchange(): return lax.ppermute(value, 'tile', [(s, s ^ bit) for s in range(tiles)])]
    ppermute x6 -> x18, starting transfers between devices: 4.15 us -> 15 us  [exchange(): return lax.ppermute(value, 'tile', [(s, s ^ bit) for s in range(tiles)])]
    all_to_all x1, waiting for transfers between devices: 6.39 us -> 0.89 us  [spread(): lax.all_to_all(value, 'tile', split_axis=0, concat_axis=0, tiled=True)]
    pallas_call x6 -> x8, Pallas kernels: 7.04 us -> 8.22 us  [call(): pl.pallas_call(functools.partial(kernel, **static), out_shape=out_shape,...]
  transfers between devices with their start and end apart: 7 -> 19, of which waited for: 3 -> 10; matrix products, arithmetic and copies ran while one was open for 0% -> 0% of each run, Pallas kernels for 2% -> 4%
where the time goes in v1:
time: 71.3 us; the launch traced here: 71.1 us
  waiting for transfers between devices  30.7 us (43%)
  starting transfers between devices  18.5 us (26%)
  blocking collectives  13 us (18%)
  Pallas kernels  8.22 us (12%)
    ppermute x18, waiting for transfers between devices, exchange(): return lax.ppermute(value, 'tile', [(s, s ^ bit) for s in range(tiles)])  29.8 us
    ppermute x18, starting transfers between devices, exchange(): return lax.ppermute(value, 'tile', [(s, s ^ bit) for s in range(tiles)])  15 us
    all_to_all x1, blocking collectives, spread(): lax.all_to_all(value, 'tile', split_axis=0, concat_axis=0, tiled=True)  13 us
    pallas_call x8, Pallas kernels, call(): pl.pallas_call(functools.partial(kernel, **static), out_shape=out_shape,...  8.22 us
    all_to_all x1, starting transfers between devices, spread(): lax.all_to_all(value, 'tile', split_axis=0, concat_axis=0, tiled=True)  3.5 us
  transfers between devices with their start and end apart: 19, of which 10 were waited for; matrix products, arithmetic and copies ran while one was open for 0% of the time, Pallas kernels for 4%

profile of v1, /device:TPU:0, one launch (start us, length us, event | category | flops | bytes accessed | tf_op | source)
XLA Modules:
  0.0 71.1 jit_solution(7020767792014349787)
XLA Ops:
  0.6 1.8 %shard_map.59 = (bf16[512,256]{1,0:T(8,128)(2,1)S(1)}, bf16[384,256]{1,0:T(8,128)(2,1)S(1)}, f32[128,128]{1,0:T(8,128)S(1)}, bf16[2,128,256]{2,1,0:T(8,128)(2,1)...) custom-call(f32[2,128,256]{2,1,0:T(8,128)} %data.1, ...), custom_call_target="tpu_custom_call" | custom-call | tf_op jit(solution)/shard_map/pallas_call | solution.py:378
  2.4 0.3 shard_map.61
  2.7 3.1 %collective-permute-start.7 = (bf16[768,256]{1,0:T(8,128)(2,1)S(1)}, bf16[768,256]{1,0:T(8,128)(2,1)S(1)}, u32[]{:S(2)}, u32[]{:S(2)}) collective-permute-start(bf16[768,256]{1,0:T(8,128)(2,1)S(1)} %get-tuple-element.40), channel_id=1, source_target_pairs={{0,2},{1,3},{2,0},{3,1},{4,6},{5,7},{6,4},{7,5},{8,10},{9,11},{10,... | collective-permute-start | bytes 1179656 | tf_op jit(solution)/shard_map/ppermute | solution.py:401
  5.8 0.1 collective-permute-start.1
  5.9 9.9 %collective-permute-done.7.refs_7_ = bf16[768,256]{1,0:T(8,128)(2,1)S(1)} collective-permute-done((bf16[768,256]{1,0:T(8,128)(2,1)S(1)}, bf16[768,256]{1,0:T(8,128)(2,1)S(1)}, u32[]{:S(2)}, u32[]{:S(2)}) %collective-permute-start.7) | collective-permute-done | bytes 393248 | tf_op jit(solution)/shard_map/ppermute | solution.py:401
  15.7 4.8 %collective-permute-done.1.far.refs_7_ = bf16[512,256]{1,0:T(8,128)(2,1)S(1)} collective-permute-done((bf16[512,256]{1,0:T(8,128)(2,1)S(1)}, bf16[512,256]{1,0:T(8,128)(2,1)S(1)}, u32[]{:S(2)}, u32[]{:S(2)}) %collective-permute-start.1) | collective-permute-done | bytes 262176 | tf_op jit(solution)/shard_map/ppermute | solution.py:401
  20.5 0.5 collective-permute-start.6
  21.0 13.0 %all_to_all.10.coeffs = bf16[16,16,128]{2,1,0:T(8,128)(2,1)S(1)} all-to-all(bf16[16,16,128]{2,1,0:T(8,128)(2,1)S(1)} %get-tuple-element.27), channel_id=1, replica_groups=mesh['freq'=2,'tile'=16] {'tile'}, dimensions={0} | all-to-all | bytes 131072 | tf_op jit(solution)/shard_map/all_to_all | solution.py:404
  34.0 0.8 %shard_map.60 = (bf16[4,16,128]{2,1,0:T(8,128)(2,1)S(1)}, bf16[4,16,128]{2,1,0:T(8,128)(2,1)S(1)}, bf16[4,16,128]{2,1,0:T(8,128)(2,1)S(1)}, bf16[4,16,128]{2,1,0:T(8,128)(2,1)S(1)}) custom-call(bf16[16,16,128]{2,1,0:T(8,128)(2,1)S(1)} %all_to_all.10.coeffs, f32[128,128]{1,0:T(8,128)S(1)} %get-tuple-element.28.own.refs_4_, ...), custom_call_target="tpu_custom_call" | custom-call | tf_op jit(solution)/shard_map/pallas_call | solution.py:378
  34.8 0.2 collective-permute-start.3
  35.0 1.0 %collective-permute-start.4 = (bf16[4,16,128]{2,1,0:T(8,128)(2,1)S(1)}, bf16[4,16,128]{2,1,0:T(8,128)(2,1)S(1)}, u32[]{:S(2)}, u32[]{:S(2)}) collective-permute-start(bf16[4,16,128]{2,1,0:T(8,128)(2,1)S(1)} %get-tuple-element.34), channel_id=1, source_target_pairs={{0,8},{1,9},{2,10},{3,11},{4,12},{5,13},{6,14},{7,15},{8,0},{9,1},... | collective-permute-start | bytes 49160 | tf_op jit(solution)/shard_map/ppermute | solution.py:401
  36.0 3.3 %collective-permute-start.5 = (bf16[4,16,128]{2,1,0:T(8,128)(2,1)S(1)}, bf16[4,16,128]{2,1,0:T(8,128)(2,1)S(1)}, u32[]{:S(2)}, u32[]{:S(2)}) collective-permute-start(bf16[4,16,128]{2,1,0:T(8,128)(2,1)S(1)} %get-tuple-element.35), channel_id=1, source_target_pairs={{0,12},{1,13},{2,14},{3,15},{4,8},{5,9},{6,10},{7,11},{8,4},{9,5},... | collective-permute-start | bytes 49160 | tf_op jit(solution)/shard_map/ppermute | solution.py:401
  39.3 0.4 collective-permute-done.4.refs_2_
  39.6 1.9 %collective-permute-done.5.refs_3_ = bf16[4,16,128]{2,1,0:T(8,128)(2,1)S(1)} collective-permute-done((bf16[4,16,128]{2,1,0:T(8,128)(2,1)S(1)}, bf16[4,16,128]{2,1,0:T(8,128)(2,1)S(1)}, u32[]{:S(2)}, u32[]{:S(2)}) %collective-permute-start.5) | collective-permute-done | bytes 16416 | tf_op jit(solution)/shard_map/ppermute | solution.py:401
  41.5 1.2 %shard_map.62 = (bf16[4,16,128]{2,1,0:T(8,128)(2,1)S(1)}, bf16[4,16,128]{2,1,0:T(8,128)(2,1)S(1)}, bf16[4,16,128]{2,1,0:T(8,128)(2,1)S(1)}, bf16[4,16,128]{2,1,0...) custom-call(bf16[4,16,128]{2,1,0:T(8,128)(2,1)S(1)} %get-tuple-element, ...), custom_call_target="tpu_custom_call" | custom-call | tf_op jit(solution)/shard_map/pallas_call | solution.py:378
  42.7 0.1 collective-permute-start.9
  42.8 3.8 %collective-permute-start.10 = (bf16[4,16,128]{2,1,0:T(8,128)(2,1)S(1)}, bf16[4,16,128]{2,1,0:T(8,128)(2,1)S(1)}, u32[]{:S(2)}, u32[]{:S(2)}) collective-permute-start(bf16[4,16,128]{2,1,0:T(8,128)(2,1)S(1)} %get-tuple-element.43), channel_id=1, source_target_pairs={{0,8},{1,9},{2,10},{3,11},{4,12},{5,13},{6,14},{7,15},{8,0},{9,1},... | collective-permute-start | bytes 49160 | tf_op jit(solution)/shard_map/ppermute | solution.py:401
  46.6 0.6 collective-permute-start.11
  47.1 1.2 %collective-permute-done.10.refs_2_ = bf16[4,16,128]{2,1,0:T(8,128)(2,1)S(1)} collective-permute-done((bf16[4,16,128]{2,1,0:T(8,128)(2,1)S(1)}, bf16[4,16,128]{2,1,0:T(8,128)(2,1)S(1)}, u32[]{:S(2)}, u32[]{:S(2)}) %collective-permute-start.10) | collective-permute-done | bytes 16416 | tf_op jit(solution)/shard_map/ppermute | solution.py:401
  48.3 3.8 %collective-permute-done.11.refs_3_ = bf16[4,16,128]{2,1,0:T(8,128)(2,1)S(1)} collective-permute-done((bf16[4,16,128]{2,1,0:T(8,128)(2,1)S(1)}, bf16[4,16,128]{2,1,0:T(8,128)(2,1)S(1)}, u32[]{:S(2)}, u32[]{:S(2)}) %collective-permute-start.11) | collective-permute-done | bytes 16416 | tf_op jit(solution)/shard_map/ppermute | solution.py:401
  52.1 1.4 %shard_map.63 = (bf16[16,16,128]{2,1,0:T(8,128)(2,1)}, f32[128,128]{1,0:T(8,128)S(1)}, f32[128,128]{1,0:T(8,128)S(1)}, f32[2,128,128]{2,1,0:T(8,128)S(1)}) custom-call(bf16[4,16,128]{2,1,0:T(8,128)(2,1)S(1)} %get-tuple-element.41.refs_0_, bf16[4,16,128]{2,1,0:T(8,128)(2,1)S(1)} %collective-permute-done.9.refs_1_, ...), custom_call_target="tpu_custom_call" | custom-call | tf_op jit(solution)/shard_map/pallas_call | solution.py:378
  53.6 0.1 collective-permute-start.16
  53.7 4.8 %collective-permute-done.16.far = f32[2,128,128]{2,1,0:T(8,128)S(1)} collective-permute-done((f32[2,128,128]{2,1,0:T(8,128)S(1)}, f32[2,128,128]{2,1,0:T(8,128)S(1)}, u32[]{:S(2)}, u32[]{:S(2)}) %collective-permute-start.16) | collective-permute-done | bytes 131104 | tf_op jit(solution)/shard_map/ppermute | solution.py:401
  58.5 3.5 %all-to-all-start.1 = ((bf16[16,16,128]{2,1,0:T(8,128)(2,1)}), bf16[16,16,128]{2,1,0:T(8,128)(2,1)S(1)}, u32[]{:S(2)}, u32[]{:S(2)}) async-start(bf16[16,16,128]{2,1,0:T(8,128)(2,1)} %get-tuple-element.45), calls=%async_computation.1 | async-start | bytes 131072 | tf_op jit(solution)/shard_map/all_to_all | solution.py:404
  62.0 1.8 %collective-permute-start.13 = (bf16[2,64,128]{2,1,0:T(8,128)(2,1)S(1)}, bf16[2,64,128]{2,1,0:T(8,128)(2,1)S(1)}, u32[]{:S(2)}, u32[]{:S(2)}) collective-permute-start(bf16[2,64,128]{2,1,0:T(8,128)(2,1)S(1)} %get-tuple-element.48), channel_id=1, source_target_pairs={{0,2},{1,3},{2,0},{3,1},{4,6},{5,7},{6,4},{7,5},{8,10},{9,11},{10,... | collective-permute-start | bytes 98312 | tf_op jit(solution)/shard_map/ppermute | solution.py:401
  63.9 2.2 %collective-permute-done.13.adj_far = bf16[2,64,128]{2,1,0:T(8,128)(2,1)S(1)} collective-permute-done((bf16[2,64,128]{2,1,0:T(8,128)(2,1)S(1)}, bf16[2,64,128]{2,1,0:T(8,128)(2,1)S(1)}, u32[]{:S(2)}, u32[]{:S(2)}) %collective-permute-start.13) | collective-permute-done | bytes 32800 | tf_op jit(solution)/shard_map/ppermute | solution.py:401
  66.0 0.5 collective-permute-start.12
  66.6 0.8 %collective-permute-done.12.adj_near = bf16[64,128]{1,0:T(8,128)(2,1)S(1)} collective-permute-done((bf16[64,128]{1,0:T(8,128)(2,1)S(1)}, bf16[64,128]{1,0:T(8,128)(2,1)S(1)}, u32[]{:S(2)}, u32[]{:S(2)}) %collective-permute-start.12) | collective-permute-done | bytes 16416 | tf_op jit(solution)/shard_map/ppermute | solution.py:401
  67.4 0.6 shard_map.64.x
  68.0 0.9 %all-to-all-done.1.adjoint = bf16[16,16,128]{2,1,0:T(8,128)(2,1)S(1)} async-done(((bf16[16,16,128]{2,1,0:T(8,128)(2,1)}), bf16[16,16,128]{2,1,0:T(8,128)(2,1)S(1)}, u32[]{:S(2)}, u32[]{:S(2)}) %all-to-all-start.1) | async-done | bytes 65568 | tf_op jit(solution)/shard_map/all_to_all | solution.py:404
  68.9 1.3 %shard_map.65 = f32[2,512,256]{2,1,0:T(8,128)} custom-call(bf16[16,16,128]{2,1,0:T(8,128)(2,1)S(1)} %all-to-all-done.1.adjoint, f32[2,512,256]{2,1,0:T(8,128)S(1)} %shard_map.64.x, bf16[2,4,16,512]{3,2,1,0:T(8,128)(2,1)S(1)} %get-tuple-element.37.vfac.refs_5_), custom_call_target="tpu_custom_call" | custom-call | tf_op jit(solution)/shard_map/pallas_call | solution.py:378
  70.2 0.9 %shard_map.66 = f32[2,128,256]{2,1,0:T(8,128)} custom-call(f32[128,128]{1,0:T(8,128)S(1)} %get-tuple-element.49.misfit, f32[128,128]{1,0:T(8,128)S(1)} %collective-permute-done.15.near, f32[2,128,128]{2,1,0:T(8,128)S(1)} %collective-permute-done.16.far, f32[2,128,128]{2,1,0:T(8,128)S(1)} %collective-permute-done.17.far_near), custom_call_target="tpu_custom_call" | custom-call | tf_op jit(solution)/shard_map/pallas_call | solution.py:378
  (15 shorter events, 0.0 us)
Async XLA Ops:
  2.7 13.0 %collective-permute-start.7 = (bf16[768,256]{1,0:T(8,128)(2,1)S(1)}, bf16[768,256]{1,0:T(8,128)(2,1)S(1)}, u32[]{:S(2)}, u32[]{:S(2)}) collective-permute-start(bf16[768,256]{1,0:T(8,128)(2,1)S(1)} %get-tuple-element.40), channel_id=1, source_target_pairs={{0,2},{1,3},{2,0},{3,1},{4,6},{5,7},{6,4},{7,5},{8,10},{9,11},{10,... | collective-permute-start | bytes 1179656 | tf_op jit(solution)/shard_map/ppermute | solution.py:401
  5.8 14.7 %collective-permute-start.1 = (bf16[512,256]{1,0:T(8,128)(2,1)S(1)}, bf16[512,256]{1,0:T(8,128)(2,1)S(1)}, u32[]{:S(2)}, u32[]{:S(2)}) collective-permute-start(bf16[512,256]{1,0:T(8,128)(2,1)S(1)} %get-tuple-element.31), channel_id=1, source_target_pairs={{0,2},{1,3},{2,0},{3,1},{4,6},{5,7},{6,4},{7,5},{8,10},{9,11},{10,... | collective-permute-start | bytes 786440 | tf_op jit(solution)/shard_map/ppermute | solution.py:401
  15.7 25.8 %collective-permute-start.8 = (bf16[768,256]{1,0:T(8,128)(2,1)S(1)}, bf16[768,256]{1,0:T(8,128)(2,1)S(1)}, u32[]{:S(2)}, u32[]{:S(2)}) collective-permute-start(bf16[768,256]{1,0:T(8,128)(2,1)S(1)} %collective-permute-done.7.refs_7_), channel_id=1, source_target_pairs={{0,1},{1,0},{2,3},{3,2},{4,5},{5,4},{6,7},{7,6},{8,9},{9,8},{10,11... | collective-permute-start | bytes 1179656 | tf_op jit(solution)/shard_map/ppermute | solution.py:401
  20.5 13.5 %collective-permute-start.2 = (bf16[512,256]{1,0:T(8,128)(2,1)S(1)}, bf16[512,256]{1,0:T(8,128)(2,1)S(1)}, u32[]{:S(2)}, u32[]{:S(2)}) collective-permute-start(bf16[512,256]{1,0:T(8,128)(2,1)S(1)} %collective-permute-done.1.far.refs_7_), channel_id=1, source_target_pairs={{0,1},{1,0},{2,3},{3,2},{4,5},{5,4},{6,7},{7,6},{8,9},{9,8},{10,11... | collective-permute-start | bytes 786440 | tf_op jit(solution)/shard_map/ppermute | solution.py:401
  20.5 18.7 %collective-permute-start.6 = (bf16[1024,128]{1,0:T(8,128)(2,1)S(1)}, bf16[1024,128]{1,0:T(8,128)(2,1)S(1)}, u32[]{:S(2)}, u32[]{:S(2)}) collective-permute-start(bf16[1024,128]{1,0:T(8,128)(2,1)S(1)} %get-tuple-element.39), channel_id=1, source_target_pairs={{0,1},{1,0},{2,3},{3,2},{4,5},{5,4},{6,7},{7,6},{8,9},{9,8},{10,11... | collective-permute-start | bytes 786440 | tf_op jit(solution)/shard_map/ppermute | solution.py:401
  21.0 13.0 %collective-permute-start = (bf16[384,256]{1,0:T(8,128)(2,1)S(1)}, bf16[384,256]{1,0:T(8,128)(2,1)S(1)}, u32[]{:S(2)}, u32[]{:S(2)}) collective-permute-start(bf16[384,256]{1,0:T(8,128)(2,1)S(1)} %get-tuple-element.30), channel_id=1, source_target_pairs={{0,1},{1,0},{2,3},{3,2},{4,5},{5,4},{6,7},{7,6},{8,9},{9,8},{10,11... | collective-permute-start | bytes 589832 | tf_op jit(solution)/shard_map/ppermute | solution.py:401
  34.8 4.5 %collective-permute-start.3 = (bf16[4,16,128]{2,1,0:T(8,128)(2,1)S(1)}, bf16[4,16,128]{2,1,0:T(8,128)(2,1)S(1)}, u32[]{:S(2)}, u32[]{:S(2)}) collective-permute-start(bf16[4,16,128]{2,1,0:T(8,128)(2,1)S(1)} %get-tuple-element.33), channel_id=1, source_target_pairs={{0,4},{1,5},{2,6},{3,7},{4,0},{5,1},{6,2},{7,3},{8,12},{9,13},{10,... | collective-permute-start | bytes 49160 | tf_op jit(solution)/shard_map/ppermute | solution.py:401
  35.0 4.6 %collective-permute-start.4 = (bf16[4,16,128]{2,1,0:T(8,128)(2,1)S(1)}, bf16[4,16,128]{2,1,0:T(8,128)(2,1)S(1)}, u32[]{:S(2)}, u32[]{:S(2)}) collective-permute-start(bf16[4,16,128]{2,1,0:T(8,128)(2,1)S(1)} %get-tuple-element.34), channel_id=1, source_target_pairs={{0,8},{1,9},{2,10},{3,11},{4,12},{5,13},{6,14},{7,15},{8,0},{9,1},... | collective-permute-start | bytes 49160 | tf_op jit(solution)/shard_map/ppermute | solution.py:401
  36.0 5.5 %collective-permute-start.5 = (bf16[4,16,128]{2,1,0:T(8,128)(2,1)S(1)}, bf16[4,16,128]{2,1,0:T(8,128)(2,1)S(1)}, u32[]{:S(2)}, u32[]{:S(2)}) collective-permute-start(bf16[4,16,128]{2,1,0:T(8,128)(2,1)S(1)} %get-tuple-element.35), channel_id=1, source_target_pairs={{0,12},{1,13},{2,14},{3,15},{4,8},{5,9},{6,10},{7,11},{8,4},{9,5},... | collective-permute-start | bytes 49160 | tf_op jit(solution)/shard_map/ppermute | solution.py:401
  42.7 4.5 %collective-permute-start.9 = (bf16[4,16,128]{2,1,0:T(8,128)(2,1)S(1)}, bf16[4,16,128]{2,1,0:T(8,128)(2,1)S(1)}, u32[]{:S(2)}, u32[]{:S(2)}) collective-permute-start(bf16[4,16,128]{2,1,0:T(8,128)(2,1)S(1)} %get-tuple-element.42), channel_id=1, source_target_pairs={{0,4},{1,5},{2,6},{3,7},{4,0},{5,1},{6,2},{7,3},{8,12},{9,13},{10,... | collective-permute-start | bytes 49160 | tf_op jit(solution)/shard_map/ppermute | solution.py:401
  42.8 5.5 %collective-permute-start.10 = (bf16[4,16,128]{2,1,0:T(8,128)(2,1)S(1)}, bf16[4,16,128]{2,1,0:T(8,128)(2,1)S(1)}, u32[]{:S(2)}, u32[]{:S(2)}) collective-permute-start(bf16[4,16,128]{2,1,0:T(8,128)(2,1)S(1)} %get-tuple-element.43), channel_id=1, source_target_pairs={{0,8},{1,9},{2,10},{3,11},{4,12},{5,13},{6,14},{7,15},{8,0},{9,1},... | collective-permute-start | bytes 49160 | tf_op jit(solution)/shard_map/ppermute | solution.py:401
  46.6 5.5 %collective-permute-start.11 = (bf16[4,16,128]{2,1,0:T(8,128)(2,1)S(1)}, bf16[4,16,128]{2,1,0:T(8,128)(2,1)S(1)}, u32[]{:S(2)}, u32[]{:S(2)}) collective-permute-start(bf16[4,16,128]{2,1,0:T(8,128)(2,1)S(1)} %get-tuple-element.44), channel_id=1, source_target_pairs={{0,12},{1,13},{2,14},{3,15},{4,8},{5,9},{6,10},{7,11},{8,4},{9,5},... | collective-permute-start | bytes 49160 | tf_op jit(solution)/shard_map/ppermute | solution.py:401
  53.6 5.0 %collective-permute-start.16 = (f32[2,128,128]{2,1,0:T(8,128)S(1)}, f32[2,128,128]{2,1,0:T(8,128)S(1)}, u32[]{:S(2)}, u32[]{:S(2)}) collective-permute-start(f32[2,128,128]{2,1,0:T(8,128)S(1)} %get-tuple-element.51), channel_id=1, source_target_pairs={{0,2},{1,3},{2,0},{3,1},{4,6},{5,7},{6,4},{7,5},{8,10},{9,11},{10,... | collective-permute-start | bytes 393224 | tf_op jit(solution)/shard_map/ppermute | solution.py:401
  58.5 11.7 %collective-permute-start.17 = (f32[2,128,128]{2,1,0:T(8,128)S(1)}, f32[2,128,128]{2,1,0:T(8,128)S(1)}, u32[]{:S(2)}, u32[]{:S(2)}) collective-permute-start(f32[2,128,128]{2,1,0:T(8,128)S(1)} %collective-permute-done.16.far), channel_id=1, source_target_pairs={{0,1},{1,0},{2,3},{3,2},{4,5},{5,4},{6,7},{7,6},{8,9},{9,8},{10,11... | collective-permute-start | bytes 393224 | tf_op jit(solution)/shard_map/ppermute | solution.py:401
  58.5 10.4 %all-to-all-start.1 = ((bf16[16,16,128]{2,1,0:T(8,128)(2,1)}), bf16[16,16,128]{2,1,0:T(8,128)(2,1)S(1)}, u32[]{:S(2)}, u32[]{:S(2)}) async-start(bf16[16,16,128]{2,1,0:T(8,128)(2,1)} %get-tuple-element.45), calls=%async_computation.1 | async-start | bytes 131072 | tf_op jit(solution)/shard_map/all_to_all | solution.py:404
  62.0 4.0 %collective-permute-start.13 = (bf16[2,64,128]{2,1,0:T(8,128)(2,1)S(1)}, bf16[2,64,128]{2,1,0:T(8,128)(2,1)S(1)}, u32[]{:S(2)}, u32[]{:S(2)}) collective-permute-start(bf16[2,64,128]{2,1,0:T(8,128)(2,1)S(1)} %get-tuple-element.48), channel_id=1, source_target_pairs={{0,2},{1,3},{2,0},{3,1},{4,6},{5,7},{6,4},{7,5},{8,10},{9,11},{10,... | collective-permute-start | bytes 98312 | tf_op jit(solution)/shard_map/ppermute | solution.py:401
  63.9 6.3 %collective-permute-start.15 = (f32[128,128]{1,0:T(8,128)S(1)}, f32[128,128]{1,0:T(8,128)S(1)}, u32[]{:S(2)}, u32[]{:S(2)}) collective-permute-start(f32[128,128]{1,0:T(8,128)S(1)} %get-tuple-element.50), channel_id=1, source_target_pairs={{0,1},{1,0},{2,3},{3,2},{4,5},{5,4},{6,7},{7,6},{8,9},{9,8},{10,11... | collective-permute-start | bytes 196616 | tf_op jit(solution)/shard_map/ppermute | solution.py:401
  66.0 1.4 %collective-permute-start.14 = (bf16[2,64,128]{2,1,0:T(8,128)(2,1)S(1)}, bf16[2,64,128]{2,1,0:T(8,128)(2,1)S(1)}, u32[]{:S(2)}, u32[]{:S(2)}) collective-permute-start(bf16[2,64,128]{2,1,0:T(8,128)(2,1)S(1)} %collective-permute-done.13.adj_far), channel_id=1, source_target_pairs={{0,1},{1,0},{2,3},{3,2},{4,5},{5,4},{6,7},{7,6},{8,9},{9,8},{10,11... | collective-permute-start | bytes 98312 | tf_op jit(solution)/shard_map/ppermute | solution.py:401
  66.0 1.3 %collective-permute-start.12 = (bf16[64,128]{1,0:T(8,128)(2,1)S(1)}, bf16[64,128]{1,0:T(8,128)(2,1)S(1)}, u32[]{:S(2)}, u32[]{:S(2)}) collective-permute-start(bf16[64,128]{1,0:T(8,128)(2,1)S(1)} %get-tuple-element.47), channel_id=1, source_target_pairs={{0,1},{1,0},{2,3},{3,2},{4,5},{5,4},{6,7},{7,6},{8,9},{9,8},{10,11... | collective-permute-start | bytes 49160 | tf_op jit(solution)/shard_map/ppermute | solution.py:401

commit v2 on v1

--- a/solution.py
+++ b/solution.py
@@ -12,6 +12,7 @@
 THRESHOLD = 0.4
 VMEM_LIMIT = 24 << 20
 PIECES = 4
+GATHERED = 8
 
 f32 = jnp.float32
 bf16 = jnp.bfloat16
@@ -84,8 +85,7 @@
 
 def first_kernel(data, x, ufac, vfac, to_far, to_near, own, u_own, x_own, v_own, out, *, group, width):
     rows = data.shape[1]
-    folds = ufac.shape[2] // (4 * width)
-    step = rows // folds
+    lanes = 2 * width
     q = group_index(group)
 
     def run(waves, scratch, sems):
@@ -93,57 +93,47 @@
         v_copy = pltpu.make_async_copy(vfac, v_own, sems.at[1])
         u_copy = pltpu.make_async_copy(ufac, u_own, sems.at[2])
         x_copy = pltpu.make_async_copy(x, x_own, sems.at[3])
-        for copy in (wave_copy, u_copy, v_copy, x_copy):
+        for copy in (wave_copy, x_copy, v_copy, u_copy):
             copy.start()
         wave_copy.wait()
         for s, block in enumerate(slices_of(waves[0], waves[1], width)):
             scratch[jnp.bitwise_xor(q, s)] = block
         own[...] = scratch[0]
-        for ref, base, b in ((to_near, 0, 1), (to_far, 0, 2), (to_far, step, 3)):
+        for ref, base, b in ((to_near, 0, 1), (to_far, 0, 2), (to_far, rows, 3)):
             high, low = split(scratch[b])
-            for g in range(folds):
-                cut = slice(g * step, (g + 1) * step)
-                lane = 4 * width * g
-                ref[base:base + step, lane:lane + 2 * width] = high[cut]
-                ref[base:base + step, lane + 2 * width:lane + 4 * width] = low[cut]
-        u_copy.wait()
-        for part in range(2):
-            to_near[step + rows * part:step + rows * (part + 1)] = u_own[part]
-            to_far[2 * step + rows * part:2 * step + rows * (part + 1)] = u_own[part]
+            ref[base:base + rows, :lanes] = high
+            ref[base:base + rows, lanes:] = low
         v_copy.wait()
         x_copy.wait()
         send_coeffs(
             flat_factors(v_own), x_own[0].astype(bf16), x_own[1].astype(bf16), out, group=group, width=width
         )
+        u_copy.wait()
 
     pl.run_scoped(
         run,
         pltpu.VMEM(data.shape, f32),
-        pltpu.VMEM((group, rows, 2 * width), f32),
+        pltpu.VMEM((group, rows, lanes), f32),
         pltpu.SemaphoreType.DMA((4,)),
     )
 
 
-def row_core(c, own, ufac, near, far, corner, misfits, width):
+def row_core(c, gathered, misfits, width):
+    own, *pieces = gathered
     lanes = 2 * width
     rows = own.shape[0]
     ci = times_i(c.astype(f32)).astype(bf16)
-    folds = ufac.shape[2] // (2 * lanes)
-    step = rows // folds
 
     def joined(ref, base):
-        cuts = [ref[base:base + step, 2 * lanes * g:2 * lanes * (g + 1)].astype(f32) for g in range(folds)]
-        pair = jnp.concatenate(cuts, axis=0)
+        pair = ref[base:base + rows].astype(f32)
         return pair[:, :lanes] + pair[:, lanes:]
 
-    def factors(ref, base):
-        return ref[base:base + rows], ref[base + rows:base + 2 * rows]
-
+    u_own, near, u_near, far, u_far, corner, u_corner = pieces
     blocks = (
-        (own[...], (ufac[0], ufac[1])),
-        (joined(near, 0), factors(near, step)),
-        (joined(far, 0), factors(far, 2 * step)),
-        (joined(corner, step), factors(corner, 2 * step)),
+        (own[...], u_own[...]),
+        (joined(near, 0), u_near[...]),
+        (joined(far, 0), u_far[...]),
+        (joined(corner, rows), u_corner[...]),
     )
     total = None
     for b, (wave, (ur, ui)) in enumerate(blocks):
@@ -166,16 +156,18 @@
         adjoint[j] = flat[j * rank:(j + 1) * rank]
 
 
-def row_kernel(coeffs, own, ufac, near, far, corner, adjoint, *misfits, width):
+def row_kernel(coeffs, *refs, width):
+    gathered, adjoint, misfits = refs[:GATHERED], refs[GATHERED], refs[GATHERED + 1:]
     c = coeffs[...].reshape(-1, 2 * width)
-    to_chunks(row_core(c, own, ufac, near, far, corner, misfits, width), adjoint)
-
-
-def row_first_kernel(coeffs, own, ufac, near, far, corner, *pieces, group, width):
+    to_chunks(row_core(c, gathered, misfits, width), adjoint)
+
+
+def row_first_kernel(coeffs, *refs, group, width):
+    gathered, pieces = refs[:GATHERED], refs[GATHERED:]
     z = row_index(group)
     rank = coeffs.shape[1]
     c = coeffs[...].reshape(-1, 2 * width)
-    flat = row_core(c, own, ufac, near, far, corner, (), width)
+    flat = row_core(c, gathered, (), width)
 
     def place(scratch):
         for j in range(flat.shape[0] // rank):
@@ -187,67 +179,59 @@
 
 
 def row_last_kernel(*refs, group, width, count):
-    pieces, (own, ufac, near, far, corner, adjoint), misfits = refs[:count], refs[count:count + 6], refs[count + 6:]
+    pieces, refs = refs[:count], refs[count:]
+    gathered, adjoint, misfits = refs[:GATHERED], refs[GATHERED], refs[GATHERED + 1:]
     z = row_index(group)
 
     def run(scratch):
         for b, piece in enumerate(pieces):
             scratch[jnp.bitwise_xor(z, b)] = piece[...]
         c = scratch[...].reshape(-1, 2 * width)
-        to_chunks(row_core(c, own, ufac, near, far, corner, misfits, width), adjoint)
+        to_chunks(row_core(c, gathered, misfits, width), adjoint)
 
     pl.run_scoped(run, pltpu.VMEM((count,) + pieces[0].shape, bf16))
 
 
-def pack_kernel(x, vfac, to_far, to_near, own, *, group, width):
+def pack_kernel(x, to_far, to_near, own, *, group, width):
     q = group_index(group)
-    sources = x.shape[1]
     lanes = 2 * width
-    vcat = flat_factors(vfac)
-    tall = vcat.shape[0]
 
     def place(scratch):
         for s, block in enumerate(slices_of(x[0], x[1], width)):
-            scratch[jnp.bitwise_xor(q, s)] = block.astype(bf16)
+            scratch[jnp.bitwise_xor(q, s)] = block
         own[...] = scratch[0]
-        to_near[:sources] = scratch[1]
-        to_far[:sources, :lanes] = scratch[2]
-        to_far[:sources, lanes:] = scratch[3]
-
-    pl.run_scoped(place, pltpu.VMEM((group, sources, lanes), bf16))
-    for ref in (to_near, to_far):
-        wide = ref.shape[1]
-        for h in range(sources // wide):
-            ref[sources + h * tall:sources + (h + 1) * tall] = flat_factors(vfac, slice(h * wide, (h + 1) * wide))
+        to_far[0] = scratch[2].astype(bf16)
+        to_far[1] = scratch[3].astype(bf16)
+        high, low = split(scratch[1])
+        to_near[:, :lanes] = high
+        to_near[:, lanes:] = low
+
+    pl.run_scoped(place, pltpu.VMEM((group, x.shape[1], lanes), f32))
 
 
 def middle_columns_kernel(*refs, group, width, count):
     pieces, refs = refs[:count], refs[count:]
-    (x_own, v_own, near, far, corner), refs = refs[:5], refs[5:]
+    (x_own, near, far, corner, v_own, v_near, v_far, v_corner), refs = refs[:8], refs[8:]
     outs, (adj_own, adj_near, adj_far) = refs[:count], refs[count:]
     q = group_index(group)
     z = row_index(group)
-    sources, lanes = x_own.shape
+    lanes = 2 * width
     rank = pieces[0].shape[1]
     side = count * rank
-    tall = 2 * side
-
-    def factors(ref):
-        wide = ref.shape[1]
-        cuts = [ref[sources + h * tall:sources + (h + 1) * tall] for h in range(sources // wide)]
-        return jnp.concatenate(cuts, axis=1)
 
     def run(adj, coeffs):
         for b, piece in enumerate(pieces):
             for k in range(group):
                 adj[k, jnp.bitwise_xor(z, b)] = piece[jnp.bitwise_xor(q, k)]
+        exact = near[...].astype(f32)
         columns = (
-            (x_own[...], flat_factors(v_own)),
-            (near[:sources], factors(near)),
-            (far[:sources, :lanes], factors(far)),
-            (corner[:sources, lanes:], factors(corner)),
-        )
-        for k, (x, vcat) in enumerate(columns):
+            (x_own[...], v_own),
+            (exact[:, :lanes] + exact[:, lanes:], v_near),
+            (far[0].astype(f32), v_far),
+            (corner[1].astype(f32), v_corner),
+        )
+        for k, (x, v) in enumerate(columns):
+            vcat = flat_factors(v)
             a = adj[k].reshape(side, lanes)
             if k == 0:
                 adj_own[...] = a
@@ -256,7 +240,7 @@
             else:
                 adj_far[k - 2] = a
             turned = times_i(a.astype(f32)).astype(bf16)
-            s = x.astype(f32) + STEP * dot(vcat, jnp.concatenate([a, turned], axis=0), ((0,), (0,)))
+            s = x + STEP * dot(vcat, jnp.concatenate([a, turned], axis=0), ((0,), (0,)))
             square = s * s
             magnitude = jnp.sqrt(square + swap_halves(square))
             factor = jnp.maximum(magnitude - THRESHOLD, 0.0) / jnp.maximum(magnitude, THRESHOLD)
@@ -403,15 +387,15 @@
     def spread(value):
         return lax.all_to_all(value, "tile", split_axis=0, concat_axis=0, tiled=True)
 
-    wide = ufac.shape[2]
-    step = rows * 2 * lanes // wide
-    assert wide % (2 * lanes) == 0 and step % 16 == 0
     chunks = shape((tiles, rank, lanes), bf16)
-    to_far, to_near, own, ufac, estimate, vfac, coeffs = call(
+    u_far = exchange(ufac, 2)
+    u_near = exchange(ufac, 1)
+    u_corner = exchange(u_far, 1)
+    to_far, to_near, own, u_own, estimate, v_own, coeffs = call(
         first_kernel,
         (
-            shape((2 * rows + 2 * step, wide), bf16),
-            shape((2 * rows + step, wide), bf16),
+            shape((2 * rows, 2 * lanes), bf16),
+            shape((rows, 2 * lanes), bf16),
             shape((rows, lanes), f32),
             shape(ufac.shape, bf16),
             shape(x_init.shape, f32),
@@ -423,13 +407,12 @@
     far = exchange(to_far, 2)
     near = exchange(to_near, 1)
     corner = exchange(far, 1)
-    gathered = (own, ufac, near, far, corner)
+    gathered = (own, u_own, near, u_near, far, u_far, corner, u_corner)
     block = shape((rows, lanes), f32)
     row_outs = (chunks, block, block, shape((2, rows, lanes), f32))
     received = spread(coeffs)
     if tile_rows == 4:
         sources = x_init.shape[1]
-        tall = 2 * tile_rows * rank
         piece = shape((group, rank, lanes), bf16)
         side = (tile_rows * rank, lanes)
         counted = dict(count=tile_rows, **static)
@@ -438,14 +421,17 @@
             order = {b: exchange(pieces[b], b * group) for b in range(tile_rows - 1, 0, -1)}
             return [pieces[0]] + [order[b] for b in range(1, tile_rows)]
 
+        v_far = exchange(vfac, 2)
+        v_near = exchange(vfac, 1)
+        v_corner = exchange(v_far, 1)
         x_far, x_near, x_own = call(
             pack_kernel,
             (
-                shape((sources + tall * sources // (2 * lanes), 2 * lanes), bf16),
-                shape((sources + tall * sources // lanes, lanes), bf16),
-                shape((sources, lanes), bf16),
+                shape((2, sources, lanes), bf16),
+                shape((sources, 2 * lanes), bf16),
+                shape((sources, lanes), f32),
             ),
-            estimate, vfac, **static,
+            estimate, **static,
         )
         x_far = exchange(x_far, 2)
         x_near = exchange(x_near, 1)
@@ -455,7 +441,7 @@
         *pieces, adj_own, adj_near, adj_far = call(
             middle_columns_kernel,
             (piece,) * tile_rows + (shape(side, bf16), shape(side, bf16), shape((2,) + side, bf16)),
-            *pieces, x_own, vfac, x_near, x_far, x_corner, **counted,
+            *pieces, x_own, x_near, x_far, x_corner, v_own, v_near, v_far, v_corner, **counted,
         )
         pieces = along_rows(pieces)
         adj_far = exchange(adj_far, 2)
@@ -464,12 +450,12 @@
         row = call(row_last_kernel, row_outs, *pieces, *gathered, **counted)
         estimate = call(
             own_column_kernel, shape(x_init.shape, f32),
-            adj_own, adj_near, adj_far, adj_corner, estimate, vfac, **static,
+            adj_own, adj_near, adj_far, adj_corner, estimate, v_own, **static,
         )
     else:
         (pieces,) = call(row_kernel, (chunks,), received, *gathered, width=width)
         estimate, coeffs = call(
-            middle_kernel, (shape(x_init.shape, f32), chunks), spread(pieces), estimate, vfac, **static
+            middle_kernel, (shape(x_init.shape, f32), chunks), spread(pieces), estimate, v_own, **static
         )
         row = call(row_kernel, row_outs, spread(coeffs), *gathered, width=width)
     adjoint, misfit, to_near, to_far = row
@@ -477,7 +463,7 @@
     misfit_near = exchange(to_near, 1)
     misfit_corner = exchange(misfit_far, 1)
     adjoint = spread(adjoint)
-    solved = call(last_kernel, result(x_init.shape, f32), adjoint, estimate, vfac, **static)
+    solved = call(last_kernel, result(x_init.shape, f32), adjoint, estimate, v_own, **static)
     residual = call(
         residual_kernel, result(data.shape, f32), misfit, misfit_near, misfit_far, misfit_corner, **static
     )

time: 71.3 us -> 71.3 us (level)
  starting transfers between devices: 18.5 us -> 22.5 us
  waiting for transfers between devices: 30.7 us -> 26.7 us
    ppermute x18 -> x24, waiting for transfers between devices: 29.8 us -> 25.8 us  [exchange(): return lax.ppermute(value, 'tile', [(s, s ^ bit) for s in range(tiles)])]
    ppermute x18 -> x24, starting transfers between devices: 15 us -> 19 us  [exchange(): return lax.ppermute(value, 'tile', [(s, s ^ bit) for s in range(tiles)])]
  transfers between devices with their start and end apart: 19 -> 25, of which waited for: 10 -> 11; matrix products, arithmetic and copies ran while one was open for 0% -> 0% of each run, Pallas kernels for 4% -> 4%
where the time goes in v2:
time: 71.3 us; the launch traced here: 71 us
  waiting for transfers between devices  26.7 us (37%)
  starting transfers between devices  22.5 us (32%)
  blocking collectives  12.8 us (18%)
  Pallas kernels  8.24 us (12%)
  between operations  0.72 us (1%)
    ppermute x24, waiting for transfers between devices, exchange(): return lax.ppermute(value, 'tile', [(s, s ^ bit) for s in range(tiles)])  25.8 us
    ppermute x24, starting transfers between devices, exchange(): return lax.ppermute(value, 'tile', [(s, s ^ bit) for s in range(tiles)])  19 us
    all_to_all x1, blocking collectives, spread(): lax.all_to_all(value, 'tile', split_axis=0, concat_axis=0, tiled=True)  12.8 us
    pallas_call x8, Pallas kernels, call(): pl.pallas_call(functools.partial(kernel, **static), out_shape=out_shape,...  8.24 us
    all_to_all x1, starting transfers between devices, spread(): lax.all_to_all(value, 'tile', split_axis=0, concat_axis=0, tiled=True)  3.5 us
  transfers between devices with their start and end apart: 25, of which 11 were waited for; matrix products, arithmetic and copies ran while one was open for 0% of the time, Pallas kernels for 4%

profile of v2, /device:TPU:0, one launch (start us, length us, event | category | flops | bytes accessed | tf_op | source)
XLA Modules:
  0.0 71.0 jit_solution(17641155078347010253)
XLA Ops:
  0.6 1.6 %shard_map.59 = (bf16[256,256]{1,0:T(8,128)(2,1)S(1)}, bf16[128,256]{1,0:T(8,128)(2,1)S(1)}, f32[128,128]{1,0:T(8,128)S(1)}, bf16[2,128,256]{2,1,0:T(8,128)(2,1)...) custom-call(f32[2,128,256]{2,1,0:T(8,128)} %data.1, ...), custom_call_target="tpu_custom_call" | custom-call | tf_op jit(solution)/shard_map/pallas_call | solution.py:362
  2.3 0.5 shard_map.61
  2.8 3.1 %collective-permute-start.10 = (bf16[2,512,128]{2,1,0:T(8,128)(2,1)S(1)}, bf16[2,512,128]{2,1,0:T(8,128)(2,1)S(1)}, u32[]{:S(2)}, u32[]{:S(2)}) collective-permute-start(bf16[2,512,128]{2,1,0:T(8,128)(2,1)S(1)} %get-tuple-element.39), channel_id=1, source_target_pairs={{0,2},{1,3},{2,0},{3,1},{4,6},{5,7},{6,4},{7,5},{8,10},{9,11},{10,... | collective-permute-start | bytes 786440 | tf_op jit(solution)/shard_map/ppermute | solution.py:385
  6.2 0.5 collective-permute-start
  6.7 1.7 %collective-permute-start.2 = (bf16[256,256]{1,0:T(8,128)(2,1)S(1)}, bf16[256,256]{1,0:T(8,128)(2,1)S(1)}, u32[]{:S(2)}, u32[]{:S(2)}) collective-permute-start(bf16[256,256]{1,0:T(8,128)(2,1)S(1)} %get-tuple-element.31), channel_id=1, source_target_pairs={{0,2},{1,3},{2,0},{3,1},{4,6},{5,7},{6,4},{7,5},{8,10},{9,11},{10,... | collective-permute-start | bytes 393224 | tf_op jit(solution)/shard_map/ppermute | solution.py:385
  8.4 0.9 %collective-permute-start.13 = (bf16[2,4,16,512]{3,2,1,0:T(8,128)(2,1)S(1)}, bf16[2,4,16,512]{3,2,1,0:T(8,128)(2,1)S(1)}, u32[]{:S(2)}, u32[]{:S(2)}) collective-permute-start(bf16[2,4,16,512]{3,2,1,0:T(8,128)(2,1)S(1)} %copy-done.1), channel_id=1, source_target_pairs={{0,2},{1,3},{2,0},{3,1},{4,6},{5,7},{6,4},{7,5},{8,10},{9,11},{10,... | collective-permute-start | bytes 393224 | tf_op jit(solution)/shard_map/ppermute | solution.py:385
  9.3 6.5 %collective-permute-done.3.refs_5_.refs_9_ = bf16[2,128,256]{2,1,0:T(8,128)(2,1)S(1)} collective-permute-done((bf16[2,128,256]{2,1,0:T(8,128)(2,1)S(1)}, bf16[2,128,256]{2,1,0:T(8,128)(2,1)S(1)}, u32[]{:S(2)}, u32[]{:S(2)}) %collective-permute-start.3) | collective-permute-done | bytes 131104 | tf_op jit(solution)/shard_map/ppermute | solution.py:385
  15.8 0.5 collective-permute-start.9
  16.4 2.2 %collective-permute-done.2.refs_4_.refs_8_ = bf16[256,256]{1,0:T(8,128)(2,1)S(1)} collective-permute-done((bf16[256,256]{1,0:T(8,128)(2,1)S(1)}, bf16[256,256]{1,0:T(8,128)(2,1)S(1)}, u32[]{:S(2)}, u32[]{:S(2)}) %collective-permute-start.2) | collective-permute-done | bytes 131104 | tf_op jit(solution)/shard_map/ppermute | solution.py:385
  18.6 2.0 %collective-permute-done.13.refs_10_ = bf16[2,4,16,512]{3,2,1,0:T(8,128)(2,1)S(1)} collective-permute-done((bf16[2,4,16,512]{3,2,1,0:T(8,128)(2,1)S(1)}, bf16[2,4,16,512]{3,2,1,0:T(8,128)(2,1)S(1)}, u32[]{:S(2)}, u32[]{:S(2)}) %collective-permute-start.13) | collective-permute-done | bytes 131104 | tf_op jit(solution)/shard_map/ppermute | solution.py:385
  20.6 0.5 collective-permute-start.14
  21.1 12.8 %all_to_all.10.coeffs = bf16[16,16,128]{2,1,0:T(8,128)(2,1)S(1)} all-to-all(bf16[16,16,128]{2,1,0:T(8,128)(2,1)S(1)} %get-tuple-element.27), channel_id=1, replica_groups=mesh['freq'=2,'tile'=16] {'tile'}, dimensions={0} | all-to-all | bytes 131072 | tf_op jit(solution)/shard_map/all_to_all | solution.py:388
  33.9 0.8 %shard_map.60 = (bf16[4,16,128]{2,1,0:T(8,128)(2,1)S(1)}, bf16[4,16,128]{2,1,0:T(8,128)(2,1)S(1)}, bf16[4,16,128]{2,1,0:T(8,128)(2,1)S(1)}, bf16[4,16,128]{2,1,0:T(8,128)(2,1)S(1)}) custom-call(bf16[16,16,128]{2,1,0:T(8,128)(2,1)S(1)} %all_to_all.10.coeffs, f32[128,128]{1,0:T(8,128)S(1)} %get-tuple-element.28.refs_0_.refs_4_, ...), custom_call_target="tpu_custom_call" | custom-call | tf_op jit(solution)/shard_map/pallas_call | solution.py:362
  34.9 1.0 %collective-permute-start.7 = (bf16[4,16,128]{2,1,0:T(8,128)(2,1)S(1)}, bf16[4,16,128]{2,1,0:T(8,128)(2,1)S(1)}, u32[]{:S(2)}, u32[]{:S(2)}) collective-permute-start(bf16[4,16,128]{2,1,0:T(8,128)(2,1)S(1)} %get-tuple-element.34), channel_id=1, source_target_pairs={{0,8},{1,9},{2,10},{3,11},{4,12},{5,13},{6,14},{7,15},{8,0},{9,1},... | collective-permute-start | bytes 49160 | tf_op jit(solution)/shard_map/ppermute | solution.py:385
  35.9 3.3 %collective-permute-start.8 = (bf16[4,16,128]{2,1,0:T(8,128)(2,1)S(1)}, bf16[4,16,128]{2,1,0:T(8,128)(2,1)S(1)}, u32[]{:S(2)}, u32[]{:S(2)}) collective-permute-start(bf16[4,16,128]{2,1,0:T(8,128)(2,1)S(1)} %get-tuple-element.35), channel_id=1, source_target_pairs={{0,12},{1,13},{2,14},{3,15},{4,8},{5,9},{6,10},{7,11},{8,4},{9,5},... | collective-permute-start | bytes 49160 | tf_op jit(solution)/shard_map/ppermute | solution.py:385
  39.6 1.9 %collective-permute-done.8.refs_3_ = bf16[4,16,128]{2,1,0:T(8,128)(2,1)S(1)} collective-permute-done((bf16[4,16,128]{2,1,0:T(8,128)(2,1)S(1)}, bf16[4,16,128]{2,1,0:T(8,128)(2,1)S(1)}, u32[]{:S(2)}, u32[]{:S(2)}) %collective-permute-start.8) | collective-permute-done | bytes 16416 | tf_op jit(solution)/shard_map/ppermute | solution.py:385
  41.5 1.2 %shard_map.62 = (bf16[4,16,128]{2,1,0:T(8,128)(2,1)S(1)}, bf16[4,16,128]{2,1,0:T(8,128)(2,1)S(1)}, bf16[4,16,128]{2,1,0:T(8,128)(2,1)S(1)}, bf16[4,16,128]{2,1,0...) custom-call(bf16[4,16,128]{2,1,0:T(8,128)(2,1)S(1)} %get-tuple-element, ...), custom_call_target="tpu_custom_call" | custom-call | tf_op jit(solution)/shard_map/pallas_call | solution.py:362
  42.7 3.8 %collective-permute-start.16 = (bf16[4,16,128]{2,1,0:T(8,128)(2,1)S(1)}, bf16[4,16,128]{2,1,0:T(8,128)(2,1)S(1)}, u32[]{:S(2)}, u32[]{:S(2)}) collective-permute-start(bf16[4,16,128]{2,1,0:T(8,128)(2,1)S(1)} %get-tuple-element.43), channel_id=1, source_target_pairs={{0,8},{1,9},{2,10},{3,11},{4,12},{5,13},{6,14},{7,15},{8,0},{9,1},... | collective-permute-start | bytes 49160 | tf_op jit(solution)/shard_map/ppermute | solution.py:385
  46.5 0.6 collective-permute-start.17
  47.1 1.2 %collective-permute-done.16.refs_2_ = bf16[4,16,128]{2,1,0:T(8,128)(2,1)S(1)} collective-permute-done((bf16[4,16,128]{2,1,0:T(8,128)(2,1)S(1)}, bf16[4,16,128]{2,1,0:T(8,128)(2,1)S(1)}, u32[]{:S(2)}, u32[]{:S(2)}) %collective-permute-start.16) | collective-permute-done | bytes 16416 | tf_op jit(solution)/shard_map/ppermute | solution.py:385
  48.3 3.8 %collective-permute-done.17.refs_3_ = bf16[4,16,128]{2,1,0:T(8,128)(2,1)S(1)} collective-permute-done((bf16[4,16,128]{2,1,0:T(8,128)(2,1)S(1)}, bf16[4,16,128]{2,1,0:T(8,128)(2,1)S(1)}, u32[]{:S(2)}, u32[]{:S(2)}) %collective-permute-start.17) | collective-permute-done | bytes 16416 | tf_op jit(solution)/shard_map/ppermute | solution.py:385
  52.1 1.4 %shard_map.63 = (bf16[16,16,128]{2,1,0:T(8,128)(2,1)}, f32[128,128]{1,0:T(8,128)S(1)}, f32[128,128]{1,0:T(8,128)S(1)}, f32[2,128,128]{2,1,0:T(8,128)S(1)}) custom-call(bf16[4,16,128]{2,1,0:T(8,128)(2,1)S(1)} %get-tuple-element.41.refs_0_, bf16[4,16,128]{2,1,0:T(8,128)(2,1)S(1)} %collective-permute-done.15.refs_1_, ...), custom_call_target="tpu_custom_call" | custom-call | tf_op jit(solution)/shard_map/pallas_call | solution.py:362
  53.6 4.8 %collective-permute-done.22.far = f32[2,128,128]{2,1,0:T(8,128)S(1)} collective-permute-done((f32[2,128,128]{2,1,0:T(8,128)S(1)}, f32[2,128,128]{2,1,0:T(8,128)S(1)}, u32[]{:S(2)}, u32[]{:S(2)}) %collective-permute-start.22) | collective-permute-done | bytes 131104 | tf_op jit(solution)/shard_map/ppermute | solution.py:385
  58.5 3.5 %all-to-all-start.1 = ((bf16[16,16,128]{2,1,0:T(8,128)(2,1)}), bf16[16,16,128]{2,1,0:T(8,128)(2,1)S(1)}, u32[]{:S(2)}, u32[]{:S(2)}) async-start(bf16[16,16,128]{2,1,0:T(8,128)(2,1)} %get-tuple-element.45), calls=%async_computation.1 | async-start | bytes 131072 | tf_op jit(solution)/shard_map/all_to_all | solution.py:388
  62.0 1.8 %collective-permute-start.19 = (bf16[2,64,128]{2,1,0:T(8,128)(2,1)S(1)}, bf16[2,64,128]{2,1,0:T(8,128)(2,1)S(1)}, u32[]{:S(2)}, u32[]{:S(2)}) collective-permute-start(bf16[2,64,128]{2,1,0:T(8,128)(2,1)S(1)} %get-tuple-element.48), channel_id=1, source_target_pairs={{0,2},{1,3},{2,0},{3,1},{4,6},{5,7},{6,4},{7,5},{8,10},{9,11},{10,... | collective-permute-start | bytes 98312 | tf_op jit(solution)/shard_map/ppermute | solution.py:385
  63.8 2.2 %collective-permute-done.19.adj_far = bf16[2,64,128]{2,1,0:T(8,128)(2,1)S(1)} collective-permute-done((bf16[2,64,128]{2,1,0:T(8,128)(2,1)S(1)}, bf16[2,64,128]{2,1,0:T(8,128)(2,1)S(1)}, u32[]{:S(2)}, u32[]{:S(2)}) %collective-permute-start.19) | collective-permute-done | bytes 32800 | tf_op jit(solution)/shard_map/ppermute | solution.py:385
  66.0 0.5 collective-permute-start.18
  66.5 0.8 %collective-permute-done.18.adj_near = bf16[64,128]{1,0:T(8,128)(2,1)S(1)} collective-permute-done((bf16[64,128]{1,0:T(8,128)(2,1)S(1)}, bf16[64,128]{1,0:T(8,128)(2,1)S(1)}, u32[]{:S(2)}, u32[]{:S(2)}) %collective-permute-start.18) | collective-permute-done | bytes 16416 | tf_op jit(solution)/shard_map/ppermute | solution.py:385
  67.3 0.6 shard_map.64.x
  68.0 0.9 %all-to-all-done.1.adjoint = bf16[16,16,128]{2,1,0:T(8,128)(2,1)S(1)} async-done(((bf16[16,16,128]{2,1,0:T(8,128)(2,1)}), bf16[16,16,128]{2,1,0:T(8,128)(2,1)S(1)}, u32[]{:S(2)}, u32[]{:S(2)}) %all-to-all-start.1) | async-done | bytes 65568 | tf_op jit(solution)/shard_map/all_to_all | solution.py:388
  68.8 1.3 %shard_map.65 = f32[2,512,256]{2,1,0:T(8,128)} custom-call(bf16[16,16,128]{2,1,0:T(8,128)(2,1)S(1)} %all-to-all-done.1.adjoint, f32[2,512,256]{2,1,0:T(8,128)S(1)} %shard_map.64.x, bf16[2,4,16,512]{3,2,1,0:T(8,128)(2,1)S(1)} %get-tuple-element.40.refs_8_.vfac), custom_call_target="tpu_custom_call" | custom-call | tf_op jit(solution)/shard_map/pallas_call | solution.py:362
  70.1 0.9 %shard_map.66 = f32[2,128,256]{2,1,0:T(8,128)} custom-call(f32[128,128]{1,0:T(8,128)S(1)} %get-tuple-element.49.misfit, f32[128,128]{1,0:T(8,128)S(1)} %collective-permute-done.21.near, f32[2,128,128]{2,1,0:T(8,128)S(1)} %collective-permute-done.22.far, f32[2,128,128]{2,1,0:T(8,128)S(1)} %collective-permute-done.23.far_near), custom_call_target="tpu_custom_call" | custom-call | tf_op jit(solution)/shard_map/pallas_call | solution.py:362
  (31 shorter events, 1.2 us)
Async XLA Ops:
  2.3 3.6 %copy-start = (bf16[2,128,256]{2,1,0:T(8,128)(2,1)S(1)}, bf16[2,128,256]{2,1,0:T(8,128)(2,1)}, u32[]{:S(2)}) copy-start(bf16[2,128,256]{2,1,0:T(8,128)(2,1)} %ufac.1) | copy-start | bytes 393220
  2.3 6.1 %copy-start.1 = (bf16[2,4,16,512]{3,2,1,0:T(8,128)(2,1)S(1)}, bf16[2,4,16,512]{3,2,1,0:T(8,128)(2,1)}, u32[]{:S(2)}) copy-start(bf16[2,4,16,512]{3,2,1,0:T(8,128)(2,1)} %vfac.1) | copy-start | bytes 393220
  2.8 13.5 %collective-permute-start.10 = (bf16[2,512,128]{2,1,0:T(8,128)(2,1)S(1)}, bf16[2,512,128]{2,1,0:T(8,128)(2,1)S(1)}, u32[]{:S(2)}, u32[]{:S(2)}) collective-permute-start(bf16[2,512,128]{2,1,0:T(8,128)(2,1)S(1)} %get-tuple-element.39), channel_id=1, source_target_pairs={{0,2},{1,3},{2,0},{3,1},{4,6},{5,7},{6,4},{7,5},{8,10},{9,11},{10,... | collective-permute-start | bytes 786440 | tf_op jit(solution)/shard_map/ppermute | solution.py:385
  5.8 10.0 %collective-permute-start.3 = (bf16[2,128,256]{2,1,0:T(8,128)(2,1)S(1)}, bf16[2,128,256]{2,1,0:T(8,128)(2,1)S(1)}, u32[]{:S(2)}, u32[]{:S(2)}) collective-permute-start(bf16[2,128,256]{2,1,0:T(8,128)(2,1)S(1)} %copy-done), channel_id=1, source_target_pairs={{0,2},{1,3},{2,0},{3,1},{4,6},{5,7},{6,4},{7,5},{8,10},{9,11},{10,... | collective-permute-start | bytes 393224 | tf_op jit(solution)/shard_map/ppermute | solution.py:385
  6.2 9.6 %collective-permute-start.1 = (bf16[2,128,256]{2,1,0:T(8,128)(2,1)S(1)}, bf16[2,128,256]{2,1,0:T(8,128)(2,1)S(1)}, u32[]{:S(2)}, u32[]{:S(2)}) collective-permute-start(bf16[2,128,256]{2,1,0:T(8,128)(2,1)S(1)} %copy-done), channel_id=1, source_target_pairs={{0,1},{1,0},{2,3},{3,2},{4,5},{5,4},{6,7},{7,6},{8,9},{9,8},{10,11... | collective-permute-start | bytes 393224 | tf_op jit(solution)/shard_map/ppermute | solution.py:385
  6.2 2.2 %collective-permute-start = (bf16[128,256]{1,0:T(8,128)(2,1)S(1)}, bf16[128,256]{1,0:T(8,128)(2,1)S(1)}, u32[]{:S(2)}, u32[]{:S(2)}) collective-permute-start(bf16[128,256]{1,0:T(8,128)(2,1)S(1)} %get-tuple-element.30), channel_id=1, source_target_pairs={{0,1},{1,0},{2,3},{3,2},{4,5},{5,4},{6,7},{7,6},{8,9},{9,8},{10,11... | collective-permute-start | bytes 196616 | tf_op jit(solution)/shard_map/ppermute | solution.py:385
  6.7 11.9 %collective-permute-start.2 = (bf16[256,256]{1,0:T(8,128)(2,1)S(1)}, bf16[256,256]{1,0:T(8,128)(2,1)S(1)}, u32[]{:S(2)}, u32[]{:S(2)}) collective-permute-start(bf16[256,256]{1,0:T(8,128)(2,1)S(1)} %get-tuple-element.31), channel_id=1, source_target_pairs={{0,2},{1,3},{2,0},{3,1},{4,6},{5,7},{6,4},{7,5},{8,10},{9,11},{10,... | collective-permute-start | bytes 393224 | tf_op jit(solution)/shard_map/ppermute | solution.py:385
  8.4 12.2 %collective-permute-start.13 = (bf16[2,4,16,512]{3,2,1,0:T(8,128)(2,1)S(1)}, bf16[2,4,16,512]{3,2,1,0:T(8,128)(2,1)S(1)}, u32[]{:S(2)}, u32[]{:S(2)}) collective-permute-start(bf16[2,4,16,512]{3,2,1,0:T(8,128)(2,1)S(1)} %copy-done.1), channel_id=1, source_target_pairs={{0,2},{1,3},{2,0},{3,1},{4,6},{5,7},{6,4},{7,5},{8,10},{9,11},{10,... | collective-permute-start | bytes 393224 | tf_op jit(solution)/shard_map/ppermute | solution.py:385
  15.8 4.8 %collective-permute-start.5 = (bf16[2,128,256]{2,1,0:T(8,128)(2,1)S(1)}, bf16[2,128,256]{2,1,0:T(8,128)(2,1)S(1)}, u32[]{:S(2)}, u32[]{:S(2)}) collective-permute-start(bf16[2,128,256]{2,1,0:T(8,128)(2,1)S(1)} %collective-permute-done.3.refs_5_.refs_9_), channel_id=1, source_target_pairs={{0,1},{1,0},{2,3},{3,2},{4,5},{5,4},{6,7},{7,6},{8,9},{9,8},{10,11... | collective-permute-start | bytes 393224 | tf_op jit(solution)/shard_map/ppermute | solution.py:385
  15.8 23.4 %collective-permute-start.9 = (bf16[512,256]{1,0:T(8,128)(2,1)S(1)}, bf16[512,256]{1,0:T(8,128)(2,1)S(1)}, u32[]{:S(2)}, u32[]{:S(2)}) collective-permute-start(bf16[512,256]{1,0:T(8,128)(2,1)S(1)} %get-tuple-element.38), channel_id=1, source_target_pairs={{0,1},{1,0},{2,3},{3,2},{4,5},{5,4},{6,7},{7,6},{8,9},{9,8},{10,11... | collective-permute-start | bytes 786440 | tf_op jit(solution)/shard_map/ppermute | solution.py:385
  16.3 25.2 %collective-permute-start.11 = (bf16[2,512,128]{2,1,0:T(8,128)(2,1)S(1)}, bf16[2,512,128]{2,1,0:T(8,128)(2,1)S(1)}, u32[]{:S(2)}, u32[]{:S(2)}) collective-permute-start(bf16[2,512,128]{2,1,0:T(8,128)(2,1)S(1)} %collective-permute-done.10.refs_6_), channel_id=1, source_target_pairs={{0,1},{1,0},{2,3},{3,2},{4,5},{5,4},{6,7},{7,6},{8,9},{9,8},{10,11... | collective-permute-start | bytes 786440 | tf_op jit(solution)/shard_map/ppermute | solution.py:385
  18.6 15.3 %collective-permute-start.4 = (bf16[256,256]{1,0:T(8,128)(2,1)S(1)}, bf16[256,256]{1,0:T(8,128)(2,1)S(1)}, u32[]{:S(2)}, u32[]{:S(2)}) collective-permute-start(bf16[256,256]{1,0:T(8,128)(2,1)S(1)} %collective-permute-done.2.refs_4_.refs_8_), channel_id=1, source_target_pairs={{0,1},{1,0},{2,3},{3,2},{4,5},{5,4},{6,7},{7,6},{8,9},{9,8},{10,11... | collective-permute-start | bytes 393224 | tf_op jit(solution)/shard_map/ppermute | solution.py:385
  20.6 14.4 %collective-permute-start.12 = (bf16[2,4,16,512]{3,2,1,0:T(8,128)(2,1)S(1)}, bf16[2,4,16,512]{3,2,1,0:T(8,128)(2,1)S(1)}, u32[]{:S(2)}, u32[]{:S(2)}) collective-permute-start(bf16[2,4,16,512]{3,2,1,0:T(8,128)(2,1)S(1)} %copy-done.1), channel_id=1, source_target_pairs={{0,1},{1,0},{2,3},{3,2},{4,5},{5,4},{6,7},{7,6},{8,9},{9,8},{10,11... | collective-permute-start | bytes 393224 | tf_op jit(solution)/shard_map/ppermute | solution.py:385
  20.6 15.4 %collective-permute-start.14 = (bf16[2,4,16,512]{3,2,1,0:T(8,128)(2,1)S(1)}, bf16[2,4,16,512]{3,2,1,0:T(8,128)(2,1)S(1)}, u32[]{:S(2)}, u32[]{:S(2)}) collective-permute-start(bf16[2,4,16,512]{3,2,1,0:T(8,128)(2,1)S(1)} %collective-permute-done.13.refs_10_), channel_id=1, source_target_pairs={{0,1},{1,0},{2,3},{3,2},{4,5},{5,4},{6,7},{7,6},{8,9},{9,8},{10,11... | collective-permute-start | bytes 393224 | tf_op jit(solution)/shard_map/ppermute | solution.py:385
  34.7 4.5 %collective-permute-start.6 = (bf16[4,16,128]{2,1,0:T(8,128)(2,1)S(1)}, bf16[4,16,128]{2,1,0:T(8,128)(2,1)S(1)}, u32[]{:S(2)}, u32[]{:S(2)}) collective-permute-start(bf16[4,16,128]{2,1,0:T(8,128)(2,1)S(1)} %get-tuple-element.33), channel_id=1, source_target_pairs={{0,4},{1,5},{2,6},{3,7},{4,0},{5,1},{6,2},{7,3},{8,12},{9,13},{10,... | collective-permute-start | bytes 49160 | tf_op jit(solution)/shard_map/ppermute | solution.py:385
  34.9 4.6 %collective-permute-start.7 = (bf16[4,16,128]{2,1,0:T(8,128)(2,1)S(1)}, bf16[4,16,128]{2,1,0:T(8,128)(2,1)S(1)}, u32[]{:S(2)}, u32[]{:S(2)}) collective-permute-start(bf16[4,16,128]{2,1,0:T(8,128)(2,1)S(1)} %get-tuple-element.34), channel_id=1, source_target_pairs={{0,8},{1,9},{2,10},{3,11},{4,12},{5,13},{6,14},{7,15},{8,0},{9,1},... | collective-permute-start | bytes 49160 | tf_op jit(solution)/shard_map/ppermute | solution.py:385
  35.9 5.5 %collective-permute-start.8 = (bf16[4,16,128]{2,1,0:T(8,128)(2,1)S(1)}, bf16[4,16,128]{2,1,0:T(8,128)(2,1)S(1)}, u32[]{:S(2)}, u32[]{:S(2)}) collective-permute-start(bf16[4,16,128]{2,1,0:T(8,128)(2,1)S(1)} %get-tuple-element.35), channel_id=1, source_target_pairs={{0,12},{1,13},{2,14},{3,15},{4,8},{5,9},{6,10},{7,11},{8,4},{9,5},... | collective-permute-start | bytes 49160 | tf_op jit(solution)/shard_map/ppermute | solution.py:385
  42.6 4.5 %collective-permute-start.15 = (bf16[4,16,128]{2,1,0:T(8,128)(2,1)S(1)}, bf16[4,16,128]{2,1,0:T(8,128)(2,1)S(1)}, u32[]{:S(2)}, u32[]{:S(2)}) collective-permute-start(bf16[4,16,128]{2,1,0:T(8,128)(2,1)S(1)} %get-tuple-element.42), channel_id=1, source_target_pairs={{0,4},{1,5},{2,6},{3,7},{4,0},{5,1},{6,2},{7,3},{8,12},{9,13},{10,... | collective-permute-start | bytes 49160 | tf_op jit(solution)/shard_map/ppermute | solution.py:385
  42.7 5.5 %collective-permute-start.16 = (bf16[4,16,128]{2,1,0:T(8,128)(2,1)S(1)}, bf16[4,16,128]{2,1,0:T(8,128)(2,1)S(1)}, u32[]{:S(2)}, u32[]{:S(2)}) collective-permute-start(bf16[4,16,128]{2,1,0:T(8,128)(2,1)S(1)} %get-tuple-element.43), channel_id=1, source_target_pairs={{0,8},{1,9},{2,10},{3,11},{4,12},{5,13},{6,14},{7,15},{8,0},{9,1},... | collective-permute-start | bytes 49160 | tf_op jit(solution)/shard_map/ppermute | solution.py:385
  46.5 5.5 %collective-permute-start.17 = (bf16[4,16,128]{2,1,0:T(8,128)(2,1)S(1)}, bf16[4,16,128]{2,1,0:T(8,128)(2,1)S(1)}, u32[]{:S(2)}, u32[]{:S(2)}) collective-permute-start(bf16[4,16,128]{2,1,0:T(8,128)(2,1)S(1)} %get-tuple-element.44), channel_id=1, source_target_pairs={{0,12},{1,13},{2,14},{3,15},{4,8},{5,9},{6,10},{7,11},{8,4},{9,5},... | collective-permute-start | bytes 49160 | tf_op jit(solution)/shard_map/ppermute | solution.py:385
  53.5 5.0 %collective-permute-start.22 = (f32[2,128,128]{2,1,0:T(8,128)S(1)}, f32[2,128,128]{2,1,0:T(8,128)S(1)}, u32[]{:S(2)}, u32[]{:S(2)}) collective-permute-start(f32[2,128,128]{2,1,0:T(8,128)S(1)} %get-tuple-element.51), channel_id=1, source_target_pairs={{0,2},{1,3},{2,0},{3,1},{4,6},{5,7},{6,4},{7,5},{8,10},{9,11},{10,... | collective-permute-start | bytes 393224 | tf_op jit(solution)/shard_map/ppermute | solution.py:385
  58.5 11.7 %collective-permute-start.23 = (f32[2,128,128]{2,1,0:T(8,128)S(1)}, f32[2,128,128]{2,1,0:T(8,128)S(1)}, u32[]{:S(2)}, u32[]{:S(2)}) collective-permute-start(f32[2,128,128]{2,1,0:T(8,128)S(1)} %collective-permute-done.22.far), channel_id=1, source_target_pairs={{0,1},{1,0},{2,3},{3,2},{4,5},{5,4},{6,7},{7,6},{8,9},{9,8},{10,11... | collective-permute-start | bytes 393224 | tf_op jit(solution)/shard_map/ppermute | solution.py:385
  58.5 10.4 %all-to-all-start.1 = ((bf16[16,16,128]{2,1,0:T(8,128)(2,1)}), bf16[16,16,128]{2,1,0:T(8,128)(2,1)S(1)}, u32[]{:S(2)}, u32[]{:S(2)}) async-start(bf16[16,16,128]{2,1,0:T(8,128)(2,1)} %get-tuple-element.45), calls=%async_computation.1 | async-start | bytes 131072 | tf_op jit(solution)/shard_map/all_to_all | solution.py:388
  62.0 4.0 %collective-permute-start.19 = (bf16[2,64,128]{2,1,0:T(8,128)(2,1)S(1)}, bf16[2,64,128]{2,1,0:T(8,128)(2,1)S(1)}, u32[]{:S(2)}, u32[]{:S(2)}) collective-permute-start(bf16[2,64,128]{2,1,0:T(8,128)(2,1)S(1)} %get-tuple-element.48), channel_id=1, source_target_pairs={{0,2},{1,3},{2,0},{3,1},{4,6},{5,7},{6,4},{7,5},{8,10},{9,11},{10,... | collective-permute-start | bytes 98312 | tf_op jit(solution)/shard_map/ppermute | solution.py:385
  63.8 6.3 %collective-permute-start.21 = (f32[128,128]{1,0:T(8,128)S(1)}, f32[128,128]{1,0:T(8,128)S(1)}, u32[]{:S(2)}, u32[]{:S(2)}) collective-permute-start(f32[128,128]{1,0:T(8,128)S(1)} %get-tuple-element.50), channel_id=1, source_target_pairs={{0,1},{1,0},{2,3},{3,2},{4,5},{5,4},{6,7},{7,6},{8,9},{9,8},{10,11... | collective-permute-start | bytes 196616 | tf_op jit(solution)/shard_map/ppermute | solution.py:385
  66.0 1.4 %collective-permute-start.20 = (bf16[2,64,128]{2,1,0:T(8,128)(2,1)S(1)}, bf16[2,64,128]{2,1,0:T(8,128)(2,1)S(1)}, u32[]{:S(2)}, u32[]{:S(2)}) collective-permute-start(bf16[2,64,128]{2,1,0:T(8,128)(2,1)S(1)} %collective-permute-done.19.adj_far), channel_id=1, source_target_pairs={{0,1},{1,0},{2,3},{3,2},{4,5},{5,4},{6,7},{7,6},{8,9},{9,8},{10,11... | collective-permute-start | bytes 98312 | tf_op jit(solution)/shard_map/ppermute | solution.py:385
  66.0 1.3 %collective-permute-start.18 = (bf16[64,128]{1,0:T(8,128)(2,1)S(1)}, bf16[64,128]{1,0:T(8,128)(2,1)S(1)}, u32[]{:S(2)}, u32[]{:S(2)}) collective-permute-start(bf16[64,128]{1,0:T(8,128)(2,1)S(1)} %get-tuple-element.47), channel_id=1, source_target_pairs={{0,1},{1,0},{2,3},{3,2},{4,5},{5,4},{6,7},{7,6},{8,9},{9,8},{10,11... | collective-permute-start | bytes 49160 | tf_op jit(solution)/shard_map/ppermute | solution.py:385

commit v3 on v1

--- a/solution.py
+++ b/solution.py
@@ -82,13 +82,15 @@
     return vfac[:, :, :, cut].reshape(parts * rows * rank, -1)
 
 
-def first_kernel(data, x, ufac, vfac, to_far, to_near, own, u_own, x_own, v_own, out, *, group, width):
+def first_kernel(data, x, ufac, vfac, to_far, to_near, own, u_own, x_own, v_own, out, *columns, group, width):
     rows = data.shape[1]
+    sources = x.shape[1]
+    lanes = 2 * width
     folds = ufac.shape[2] // (4 * width)
     step = rows // folds
     q = group_index(group)
 
-    def run(waves, scratch, sems):
+    def run(waves, scratch, quarters, sems):
         wave_copy = pltpu.make_async_copy(data, waves, sems.at[0])
         v_copy = pltpu.make_async_copy(vfac, v_own, sems.at[1])
         u_copy = pltpu.make_async_copy(ufac, u_own, sems.at[2])
@@ -111,7 +113,23 @@
             to_near[step + rows * part:step + rows * (part + 1)] = u_own[part]
             to_far[2 * step + rows * part:2 * step + rows * (part + 1)] = u_own[part]
         v_copy.wait()
+        if columns:
+            far_x, near_x, block_x = columns
+            tall = 2 * v_own.shape[1] * v_own.shape[2]
+            wide = far_x.shape[1]
+            for h in range(sources // wide):
+                cut = slice(h * wide, (h + 1) * wide)
+                far_x[sources + h * tall:sources + (h + 1) * tall] = flat_factors(v_own, cut)
         x_copy.wait()
+        if columns:
+            for s, block in enumerate(slices_of(x_own[0], x_own[1], width)):
+                quarters[jnp.bitwise_xor(q, s)] = block
+            block_x[...] = quarters[0]
+            high, low = split(quarters[1])
+            near_x[:, :lanes] = high
+            near_x[:, lanes:] = low
+            far_x[:sources, :lanes] = quarters[2].astype(bf16)
+            far_x[:sources, lanes:] = quarters[3].astype(bf16)
         send_coeffs(
             flat_factors(v_own), x_own[0].astype(bf16), x_own[1].astype(bf16), out, group=group, width=width
         )
@@ -120,6 +138,7 @@
         run,
         pltpu.VMEM(data.shape, f32),
         pltpu.VMEM((group, rows, 2 * width), f32),
+        pltpu.VMEM((group, sources, lanes), f32),
         pltpu.SemaphoreType.DMA((4,)),
     )
 
@@ -199,31 +218,9 @@
     pl.run_scoped(run, pltpu.VMEM((count,) + pieces[0].shape, bf16))
 
 
-def pack_kernel(x, vfac, to_far, to_near, own, *, group, width):
-    q = group_index(group)
-    sources = x.shape[1]
-    lanes = 2 * width
-    vcat = flat_factors(vfac)
-    tall = vcat.shape[0]
-
-    def place(scratch):
-        for s, block in enumerate(slices_of(x[0], x[1], width)):
-            scratch[jnp.bitwise_xor(q, s)] = block.astype(bf16)
-        own[...] = scratch[0]
-        to_near[:sources] = scratch[1]
-        to_far[:sources, :lanes] = scratch[2]
-        to_far[:sources, lanes:] = scratch[3]
-
-    pl.run_scoped(place, pltpu.VMEM((group, sources, lanes), bf16))
-    for ref in (to_near, to_far):
-        wide = ref.shape[1]
-        for h in range(sources // wide):
-            ref[sources + h * tall:sources + (h + 1) * tall] = flat_factors(vfac, slice(h * wide, (h + 1) * wide))
-
-
 def middle_columns_kernel(*refs, group, width, count):
     pieces, refs = refs[:count], refs[count:]
-    (x_own, v_own, near, far, corner), refs = refs[:5], refs[5:]
+    (x_own, v_own, near, v_near, far, corner), refs = refs[:6], refs[6:]
     outs, (adj_own, adj_near, adj_far) = refs[:count], refs[count:]
     q = group_index(group)
     z = row_index(group)
@@ -241,11 +238,12 @@
         for b, piece in enumerate(pieces):
             for k in range(group):
                 adj[k, jnp.bitwise_xor(z, b)] = piece[jnp.bitwise_xor(q, k)]
+        exact = near[...].astype(f32)
         columns = (
             (x_own[...], flat_factors(v_own)),
-            (near[:sources], factors(near)),
-            (far[:sources, :lanes], factors(far)),
-            (corner[:sources, lanes:], factors(corner)),
+            (exact[:, :lanes] + exact[:, lanes:], flat_factors(v_near)),
+            (far[:sources, :lanes].astype(f32), factors(far)),
+            (corner[:sources, lanes:].astype(f32), factors(corner)),
         )
         for k, (x, vcat) in enumerate(columns):
             a = adj[k].reshape(side, lanes)
@@ -256,7 +254,7 @@
             else:
                 adj_far[k - 2] = a
             turned = times_i(a.astype(f32)).astype(bf16)
-            s = x.astype(f32) + STEP * dot(vcat, jnp.concatenate([a, turned], axis=0), ((0,), (0,)))
+            s = x + STEP * dot(vcat, jnp.concatenate([a, turned], axis=0), ((0,), (0,)))
             square = s * s
             magnitude = jnp.sqrt(square + swap_halves(square))
             factor = jnp.maximum(magnitude - THRESHOLD, 0.0) / jnp.maximum(magnitude, THRESHOLD)
@@ -407,7 +405,15 @@
     step = rows * 2 * lanes // wide
     assert wide % (2 * lanes) == 0 and step % 16 == 0
     chunks = shape((tiles, rank, lanes), bf16)
-    to_far, to_near, own, ufac, estimate, vfac, coeffs = call(
+    sources = x_init.shape[1]
+    tall = 2 * tile_rows * rank
+    columns = (
+        shape((sources + tall * sources // (2 * lanes), 2 * lanes), bf16),
+        shape((sources, 2 * lanes), bf16),
+        shape((sources, lanes), f32),
+    )
+    by_columns = tile_rows == 4
+    to_far, to_near, own, ufac, estimate, vfac, coeffs, *columns = call(
         first_kernel,
         (
             shape((2 * rows + 2 * step, wide), bf16),
@@ -417,7 +423,7 @@
             shape(x_init.shape, f32),
             shape(vfac.shape, bf16),
             chunks,
-        ),
+        ) + (columns if by_columns else ()),
         data, x_init, ufac, vfac, from_hbm=True, **static,
     )
     far = exchange(to_far, 2)
@@ -427,9 +433,7 @@
     block = shape((rows, lanes), f32)
     row_outs = (chunks, block, block, shape((2, rows, lanes), f32))
     received = spread(coeffs)
-    if tile_rows == 4:
-        sources = x_init.shape[1]
-        tall = 2 * tile_rows * rank
+    if by_columns:
         piece = shape((group, rank, lanes), bf16)
         side = (tile_rows * rank, lanes)
         counted = dict(count=tile_rows, **static)
@@ -438,24 +442,17 @@
             order = {b: exchange(pieces[b], b * group) for b in range(tile_rows - 1, 0, -1)}
             return [pieces[0]] + [order[b] for b in range(1, tile_rows)]
 
-        x_far, x_near, x_own = call(
-            pack_kernel,
-            (
-                shape((sources + tall * sources // (2 * lanes), 2 * lanes), bf16),
-                shape((sources + tall * sources // lanes, lanes), bf16),
-                shape((sources, lanes), bf16),
-            ),
-            estimate, vfac, **static,
-        )
+        x_far, x_near, x_own = columns
         x_far = exchange(x_far, 2)
         x_near = exchange(x_near, 1)
+        v_near = exchange(vfac, 1)
         x_corner = exchange(x_far, 1)
         pieces = call(row_first_kernel, (piece,) * tile_rows, received, *gathered, **static)
         pieces = along_rows(pieces)
         *pieces, adj_own, adj_near, adj_far = call(
             middle_columns_kernel,
             (piece,) * tile_rows + (shape(side, bf16), shape(side, bf16), shape((2,) + side, bf16)),
-            *pieces, x_own, vfac, x_near, x_far, x_corner, **counted,
+            *pieces, x_own, vfac, x_near, v_near, x_far, x_corner, **counted,
         )
         pieces = along_rows(pieces)
         adj_far = exchange(adj_far, 2)

time: 71.3 us -> 71.6 us (level)
    ppermute x18 -> x19, starting transfers between devices: 15 us -> 15.5 us  [exchange(): return lax.ppermute(value, 'tile', [(s, s ^ bit) for s in range(tiles)])]
    pallas_call x8 -> x7, Pallas kernels: 8.22 us -> 8.09 us  [call(): pl.pallas_call(functools.partial(kernel, **static), out_shape=out_shape,...]
    ppermute x18 -> x19, waiting for transfers between devices: 29.8 us -> 29.8 us  [exchange(): return lax.ppermute(value, 'tile', [(s, s ^ bit) for s in range(tiles)])]
  transfers between devices with their start and end apart: 19 -> 20, of which waited for: 10 -> 10; matrix products, arithmetic and copies ran while one was open for 0% -> 0% of each run, Pallas kernels for 4% -> 4%
where the time goes in v3:
time: 71.6 us; the launch traced here: 71.3 us
  waiting for transfers between devices  30.7 us (43%)
  starting transfers between devices  19 us (27%)
  blocking collectives  12.8 us (18%)
  Pallas kernels  8.09 us (11%)
    ppermute x19, waiting for transfers between devices, exchange(): return lax.ppermute(value, 'tile', [(s, s ^ bit) for s in range(tiles)])  29.8 us
    ppermute x19, starting transfers between devices, exchange(): return lax.ppermute(value, 'tile', [(s, s ^ bit) for s in range(tiles)])  15.5 us
    all_to_all x1, blocking collectives, spread(): lax.all_to_all(value, 'tile', split_axis=0, concat_axis=0, tiled=True)  12.8 us
    pallas_call x7, Pallas kernels, call(): pl.pallas_call(functools.partial(kernel, **static), out_shape=out_shape,...  8.09 us
    all_to_all x1, starting transfers between devices, spread(): lax.all_to_all(value, 'tile', split_axis=0, concat_axis=0, tiled=True)  3.5 us
  transfers between devices with their start and end apart: 20, of which 10 were waited for; matrix products, arithmetic and copies ran while one was open for 0% of the time, Pallas kernels for 4%

profile of v3, /device:TPU:0, one launch (start us, length us, event | category | flops | bytes accessed | tf_op | source)
XLA Modules:
  0.0 71.3 jit_solution(15773568732652091946)
XLA Ops:
  0.6 1.9 %shard_map.59 = (bf16[512,256]{1,0:T(8,128)(2,1)S(1)}, bf16[384,256]{1,0:T(8,128)(2,1)S(1)}, f32[128,128]{1,0:T(8,128)S(1)}, bf16[2,128,256]{2,1,0:T(8,128)(2,1)...) custom-call(f32[2,128,256]{2,1,0:T(8,128)} %data.1, ...), custom_call_target="tpu_custom_call" | custom-call | tf_op jit(solution)/shard_map/pallas_call | solution.py:376
  2.6 3.1 %collective-permute-start.8 = (bf16[768,256]{1,0:T(8,128)(2,1)S(1)}, bf16[768,256]{1,0:T(8,128)(2,1)S(1)}, u32[]{:S(2)}, u32[]{:S(2)}) collective-permute-start(bf16[768,256]{1,0:T(8,128)(2,1)S(1)} %get-tuple-element.39), channel_id=1, source_target_pairs={{0,2},{1,3},{2,0},{3,1},{4,6},{5,7},{6,4},{7,5},{8,10},{9,11},{10,... | collective-permute-start | bytes 1179656 | tf_op jit(solution)/shard_map/ppermute | solution.py:399
  5.6 0.1 collective-permute-start.1
  5.7 9.9 %collective-permute-done.8.refs_8_ = bf16[768,256]{1,0:T(8,128)(2,1)S(1)} collective-permute-done((bf16[768,256]{1,0:T(8,128)(2,1)S(1)}, bf16[768,256]{1,0:T(8,128)(2,1)S(1)}, u32[]{:S(2)}, u32[]{:S(2)}) %collective-permute-start.8) | collective-permute-done | bytes 393248 | tf_op jit(solution)/shard_map/ppermute | solution.py:399
  15.6 4.8 %collective-permute-done.1.far.refs_7_ = bf16[512,256]{1,0:T(8,128)(2,1)S(1)} collective-permute-done((bf16[512,256]{1,0:T(8,128)(2,1)S(1)}, bf16[512,256]{1,0:T(8,128)(2,1)S(1)}, u32[]{:S(2)}, u32[]{:S(2)}) %collective-permute-start.1) | collective-permute-done | bytes 262176 | tf_op jit(solution)/shard_map/ppermute | solution.py:399
  20.4 0.5 collective-permute-start.6
  20.9 0.5 collective-permute-start.7
  21.4 12.8 %all_to_all.10.coeffs = bf16[16,16,128]{2,1,0:T(8,128)(2,1)S(1)} all-to-all(bf16[16,16,128]{2,1,0:T(8,128)(2,1)S(1)} %get-tuple-element.27), channel_id=1, replica_groups=mesh['freq'=2,'tile'=16] {'tile'}, dimensions={0} | all-to-all | bytes 131072 | tf_op jit(solution)/shard_map/all_to_all | solution.py:402
  34.2 0.8 %shard_map.60 = (bf16[4,16,128]{2,1,0:T(8,128)(2,1)S(1)}, bf16[4,16,128]{2,1,0:T(8,128)(2,1)S(1)}, bf16[4,16,128]{2,1,0:T(8,128)(2,1)S(1)}, bf16[4,16,128]{2,1,0:T(8,128)(2,1)S(1)}) custom-call(bf16[16,16,128]{2,1,0:T(8,128)(2,1)S(1)} %all_to_all.10.coeffs, f32[128,128]{1,0:T(8,128)S(1)} %get-tuple-element.28.own.refs_4_, ...), custom_call_target="tpu_custom_call" | custom-call | tf_op jit(solution)/shard_map/pallas_call | solution.py:376
  35.1 0.2 collective-permute-start.3
  35.2 1.0 %collective-permute-start.4 = (bf16[4,16,128]{2,1,0:T(8,128)(2,1)S(1)}, bf16[4,16,128]{2,1,0:T(8,128)(2,1)S(1)}, u32[]{:S(2)}, u32[]{:S(2)}) collective-permute-start(bf16[4,16,128]{2,1,0:T(8,128)(2,1)S(1)} %get-tuple-element.34), channel_id=1, source_target_pairs={{0,8},{1,9},{2,10},{3,11},{4,12},{5,13},{6,14},{7,15},{8,0},{9,1},... | collective-permute-start | bytes 49160 | tf_op jit(solution)/shard_map/ppermute | solution.py:399
  36.2 3.3 %collective-permute-start.5 = (bf16[4,16,128]{2,1,0:T(8,128)(2,1)S(1)}, bf16[4,16,128]{2,1,0:T(8,128)(2,1)S(1)}, u32[]{:S(2)}, u32[]{:S(2)}) collective-permute-start(bf16[4,16,128]{2,1,0:T(8,128)(2,1)S(1)} %get-tuple-element.35), channel_id=1, source_target_pairs={{0,12},{1,13},{2,14},{3,15},{4,8},{5,9},{6,10},{7,11},{8,4},{9,5},... | collective-permute-start | bytes 49160 | tf_op jit(solution)/shard_map/ppermute | solution.py:399
  39.5 0.4 collective-permute-done.4.refs_2_
  39.9 1.9 %collective-permute-done.5.refs_3_ = bf16[4,16,128]{2,1,0:T(8,128)(2,1)S(1)} collective-permute-done((bf16[4,16,128]{2,1,0:T(8,128)(2,1)S(1)}, bf16[4,16,128]{2,1,0:T(8,128)(2,1)S(1)}, u32[]{:S(2)}, u32[]{:S(2)}) %collective-permute-start.5) | collective-permute-done | bytes 16416 | tf_op jit(solution)/shard_map/ppermute | solution.py:399
  41.8 1.2 %shard_map.61 = (bf16[4,16,128]{2,1,0:T(8,128)(2,1)S(1)}, bf16[4,16,128]{2,1,0:T(8,128)(2,1)S(1)}, bf16[4,16,128]{2,1,0:T(8,128)(2,1)S(1)}, bf16[4,16,128]{2,1,0...) custom-call(bf16[4,16,128]{2,1,0:T(8,128)(2,1)S(1)} %get-tuple-element, ...), custom_call_target="tpu_custom_call" | custom-call | tf_op jit(solution)/shard_map/pallas_call | solution.py:376
  43.0 0.1 collective-permute-start.10
  43.0 3.8 %collective-permute-start.11 = (bf16[4,16,128]{2,1,0:T(8,128)(2,1)S(1)}, bf16[4,16,128]{2,1,0:T(8,128)(2,1)S(1)}, u32[]{:S(2)}, u32[]{:S(2)}) collective-permute-start(bf16[4,16,128]{2,1,0:T(8,128)(2,1)S(1)} %get-tuple-element.42), channel_id=1, source_target_pairs={{0,8},{1,9},{2,10},{3,11},{4,12},{5,13},{6,14},{7,15},{8,0},{9,1},... | collective-permute-start | bytes 49160 | tf_op jit(solution)/shard_map/ppermute | solution.py:399
  46.9 0.6 collective-permute-start.12
  47.4 1.2 %collective-permute-done.11.refs_2_ = bf16[4,16,128]{2,1,0:T(8,128)(2,1)S(1)} collective-permute-done((bf16[4,16,128]{2,1,0:T(8,128)(2,1)S(1)}, bf16[4,16,128]{2,1,0:T(8,128)(2,1)S(1)}, u32[]{:S(2)}, u32[]{:S(2)}) %collective-permute-start.11) | collective-permute-done | bytes 16416 | tf_op jit(solution)/shard_map/ppermute | solution.py:399
  48.6 3.8 %collective-permute-done.12.refs_3_ = bf16[4,16,128]{2,1,0:T(8,128)(2,1)S(1)} collective-permute-done((bf16[4,16,128]{2,1,0:T(8,128)(2,1)S(1)}, bf16[4,16,128]{2,1,0:T(8,128)(2,1)S(1)}, u32[]{:S(2)}, u32[]{:S(2)}) %collective-permute-start.12) | collective-permute-done | bytes 16416 | tf_op jit(solution)/shard_map/ppermute | solution.py:399
  52.4 1.4 %shard_map.62 = (bf16[16,16,128]{2,1,0:T(8,128)(2,1)}, f32[128,128]{1,0:T(8,128)S(1)}, f32[128,128]{1,0:T(8,128)S(1)}, f32[2,128,128]{2,1,0:T(8,128)S(1)}) custom-call(bf16[4,16,128]{2,1,0:T(8,128)(2,1)S(1)} %get-tuple-element.40.refs_0_, bf16[4,16,128]{2,1,0:T(8,128)(2,1)S(1)} %collective-permute-done.10.refs_1_, ...), custom_call_target="tpu_custom_call" | custom-call | tf_op jit(solution)/shard_map/pallas_call | solution.py:376
  53.8 0.1 collective-permute-start.17
  53.9 4.8 %collective-permute-done.17.far = f32[2,128,128]{2,1,0:T(8,128)S(1)} collective-permute-done((f32[2,128,128]{2,1,0:T(8,128)S(1)}, f32[2,128,128]{2,1,0:T(8,128)S(1)}, u32[]{:S(2)}, u32[]{:S(2)}) %collective-permute-start.17) | collective-permute-done | bytes 131104 | tf_op jit(solution)/shard_map/ppermute | solution.py:399
  58.8 3.5 %all-to-all-start.1 = ((bf16[16,16,128]{2,1,0:T(8,128)(2,1)}), bf16[16,16,128]{2,1,0:T(8,128)(2,1)S(1)}, u32[]{:S(2)}, u32[]{:S(2)}) async-start(bf16[16,16,128]{2,1,0:T(8,128)(2,1)} %get-tuple-element.44), calls=%async_computation.1 | async-start | bytes 131072 | tf_op jit(solution)/shard_map/all_to_all | solution.py:402
  62.3 1.8 %collective-permute-start.14 = (bf16[2,64,128]{2,1,0:T(8,128)(2,1)S(1)}, bf16[2,64,128]{2,1,0:T(8,128)(2,1)S(1)}, u32[]{:S(2)}, u32[]{:S(2)}) collective-permute-start(bf16[2,64,128]{2,1,0:T(8,128)(2,1)S(1)} %get-tuple-element.47), channel_id=1, source_target_pairs={{0,2},{1,3},{2,0},{3,1},{4,6},{5,7},{6,4},{7,5},{8,10},{9,11},{10,... | collective-permute-start | bytes 98312 | tf_op jit(solution)/shard_map/ppermute | solution.py:399
  64.1 2.2 %collective-permute-done.14.adj_far = bf16[2,64,128]{2,1,0:T(8,128)(2,1)S(1)} collective-permute-done((bf16[2,64,128]{2,1,0:T(8,128)(2,1)S(1)}, bf16[2,64,128]{2,1,0:T(8,128)(2,1)S(1)}, u32[]{:S(2)}, u32[]{:S(2)}) %collective-permute-start.14) | collective-permute-done | bytes 32800 | tf_op jit(solution)/shard_map/ppermute | solution.py:399
  66.3 0.5 collective-permute-start.13
  66.8 0.8 %collective-permute-done.13.adj_near = bf16[64,128]{1,0:T(8,128)(2,1)S(1)} collective-permute-done((bf16[64,128]{1,0:T(8,128)(2,1)S(1)}, bf16[64,128]{1,0:T(8,128)(2,1)S(1)}, u32[]{:S(2)}, u32[]{:S(2)}) %collective-permute-start.13) | collective-permute-done | bytes 16416 | tf_op jit(solution)/shard_map/ppermute | solution.py:399
  67.7 0.6 shard_map.63.x
  68.3 0.9 %all-to-all-done.1.adjoint = bf16[16,16,128]{2,1,0:T(8,128)(2,1)S(1)} async-done(((bf16[16,16,128]{2,1,0:T(8,128)(2,1)}), bf16[16,16,128]{2,1,0:T(8,128)(2,1)S(1)}, u32[]{:S(2)}, u32[]{:S(2)}) %all-to-all-start.1) | async-done | bytes 65568 | tf_op jit(solution)/shard_map/all_to_all | solution.py:402
  69.2 1.3 %shard_map.64 = f32[2,512,256]{2,1,0:T(8,128)} custom-call(bf16[16,16,128]{2,1,0:T(8,128)(2,1)S(1)} %all-to-all-done.1.adjoint, f32[2,512,256]{2,1,0:T(8,128)S(1)} %shard_map.63.x, bf16[2,4,16,512]{3,2,1,0:T(8,128)(2,1)S(1)} %get-tuple-element.37.refs_5_.vfac), custom_call_target="tpu_custom_call" | custom-call | tf_op jit(solution)/shard_map/pallas_call | solution.py:376
  70.5 0.9 %shard_map.65 = f32[2,128,256]{2,1,0:T(8,128)} custom-call(f32[128,128]{1,0:T(8,128)S(1)} %get-tuple-element.49.misfit, f32[128,128]{1,0:T(8,128)S(1)} %collective-permute-done.16.near, f32[2,128,128]{2,1,0:T(8,128)S(1)} %collective-permute-done.17.far, f32[2,128,128]{2,1,0:T(8,128)S(1)} %collective-permute-done.18.far_near), custom_call_target="tpu_custom_call" | custom-call | tf_op jit(solution)/shard_map/pallas_call | solution.py:376
  (16 shorter events, 0.0 us)
Async XLA Ops:
  2.6 13.0 %collective-permute-start.8 = (bf16[768,256]{1,0:T(8,128)(2,1)S(1)}, bf16[768,256]{1,0:T(8,128)(2,1)S(1)}, u32[]{:S(2)}, u32[]{:S(2)}) collective-permute-start(bf16[768,256]{1,0:T(8,128)(2,1)S(1)} %get-tuple-element.39), channel_id=1, source_target_pairs={{0,2},{1,3},{2,0},{3,1},{4,6},{5,7},{6,4},{7,5},{8,10},{9,11},{10,... | collective-permute-start | bytes 1179656 | tf_op jit(solution)/shard_map/ppermute | solution.py:399
  5.6 14.7 %collective-permute-start.1 = (bf16[512,256]{1,0:T(8,128)(2,1)S(1)}, bf16[512,256]{1,0:T(8,128)(2,1)S(1)}, u32[]{:S(2)}, u32[]{:S(2)}) collective-permute-start(bf16[512,256]{1,0:T(8,128)(2,1)S(1)} %get-tuple-element.31), channel_id=1, source_target_pairs={{0,2},{1,3},{2,0},{3,1},{4,6},{5,7},{6,4},{7,5},{8,10},{9,11},{10,... | collective-permute-start | bytes 786440 | tf_op jit(solution)/shard_map/ppermute | solution.py:399
  15.6 26.2 %collective-permute-start.9 = (bf16[768,256]{1,0:T(8,128)(2,1)S(1)}, bf16[768,256]{1,0:T(8,128)(2,1)S(1)}, u32[]{:S(2)}, u32[]{:S(2)}) collective-permute-start(bf16[768,256]{1,0:T(8,128)(2,1)S(1)} %collective-permute-done.8.refs_8_), channel_id=1, source_target_pairs={{0,1},{1,0},{2,3},{3,2},{4,5},{5,4},{6,7},{7,6},{8,9},{9,8},{10,11... | collective-permute-start | bytes 1179656 | tf_op jit(solution)/shard_map/ppermute | solution.py:399
  20.4 13.9 %collective-permute-start.2 = (bf16[512,256]{1,0:T(8,128)(2,1)S(1)}, bf16[512,256]{1,0:T(8,128)(2,1)S(1)}, u32[]{:S(2)}, u32[]{:S(2)}) collective-permute-start(bf16[512,256]{1,0:T(8,128)(2,1)S(1)} %collective-permute-done.1.far.refs_7_), channel_id=1, source_target_pairs={{0,1},{1,0},{2,3},{3,2},{4,5},{5,4},{6,7},{7,6},{8,9},{9,8},{10,11... | collective-permute-start | bytes 786440 | tf_op jit(solution)/shard_map/ppermute | solution.py:399
  20.4 19.1 %collective-permute-start.6 = (bf16[512,256]{1,0:T(8,128)(2,1)S(1)}, bf16[512,256]{1,0:T(8,128)(2,1)S(1)}, u32[]{:S(2)}, u32[]{:S(2)}) collective-permute-start(bf16[512,256]{1,0:T(8,128)(2,1)S(1)} %get-tuple-element.38), channel_id=1, source_target_pairs={{0,1},{1,0},{2,3},{3,2},{4,5},{5,4},{6,7},{7,6},{8,9},{9,8},{10,11... | collective-permute-start | bytes 786440 | tf_op jit(solution)/shard_map/ppermute | solution.py:399
  20.9 13.4 %collective-permute-start = (bf16[384,256]{1,0:T(8,128)(2,1)S(1)}, bf16[384,256]{1,0:T(8,128)(2,1)S(1)}, u32[]{:S(2)}, u32[]{:S(2)}) collective-permute-start(bf16[384,256]{1,0:T(8,128)(2,1)S(1)} %get-tuple-element.30), channel_id=1, source_target_pairs={{0,1},{1,0},{2,3},{3,2},{4,5},{5,4},{6,7},{7,6},{8,9},{9,8},{10,11... | collective-permute-start | bytes 589832 | tf_op jit(solution)/shard_map/ppermute | solution.py:399
  20.9 15.4 %collective-permute-start.7 = (bf16[2,4,16,512]{3,2,1,0:T(8,128)(2,1)S(1)}, bf16[2,4,16,512]{3,2,1,0:T(8,128)(2,1)S(1)}, u32[]{:S(2)}, u32[]{:S(2)}) collective-permute-start(bf16[2,4,16,512]{3,2,1,0:T(8,128)(2,1)S(1)} %get-tuple-element.37.refs_5_.vfac), channel_id=1, source_target_pairs={{0,1},{1,0},{2,3},{3,2},{4,5},{5,4},{6,7},{7,6},{8,9},{9,8},{10,11... | collective-permute-start | bytes 393224 | tf_op jit(solution)/shard_map/ppermute | solution.py:399
  35.1 4.5 %collective-permute-start.3 = (bf16[4,16,128]{2,1,0:T(8,128)(2,1)S(1)}, bf16[4,16,128]{2,1,0:T(8,128)(2,1)S(1)}, u32[]{:S(2)}, u32[]{:S(2)}) collective-permute-start(bf16[4,16,128]{2,1,0:T(8,128)(2,1)S(1)} %get-tuple-element.33), channel_id=1, source_target_pairs={{0,4},{1,5},{2,6},{3,7},{4,0},{5,1},{6,2},{7,3},{8,12},{9,13},{10,... | collective-permute-start | bytes 49160 | tf_op jit(solution)/shard_map/ppermute | solution.py:399
  35.2 4.6 %collective-permute-start.4 = (bf16[4,16,128]{2,1,0:T(8,128)(2,1)S(1)}, bf16[4,16,128]{2,1,0:T(8,128)(2,1)S(1)}, u32[]{:S(2)}, u32[]{:S(2)}) collective-permute-start(bf16[4,16,128]{2,1,0:T(8,128)(2,1)S(1)} %get-tuple-element.34), channel_id=1, source_target_pairs={{0,8},{1,9},{2,10},{3,11},{4,12},{5,13},{6,14},{7,15},{8,0},{9,1},... | collective-permute-start | bytes 49160 | tf_op jit(solution)/shard_map/ppermute | solution.py:399
  36.2 5.5 %collective-permute-start.5 = (bf16[4,16,128]{2,1,0:T(8,128)(2,1)S(1)}, bf16[4,16,128]{2,1,0:T(8,128)(2,1)S(1)}, u32[]{:S(2)}, u32[]{:S(2)}) collective-permute-start(bf16[4,16,128]{2,1,0:T(8,128)(2,1)S(1)} %get-tuple-element.35), channel_id=1, source_target_pairs={{0,12},{1,13},{2,14},{3,15},{4,8},{5,9},{6,10},{7,11},{8,4},{9,5},... | collective-permute-start | bytes 49160 | tf_op jit(solution)/shard_map/ppermute | solution.py:399
  43.0 4.5 %collective-permute-start.10 = (bf16[4,16,128]{2,1,0:T(8,128)(2,1)S(1)}, bf16[4,16,128]{2,1,0:T(8,128)(2,1)S(1)}, u32[]{:S(2)}, u32[]{:S(2)}) collective-permute-start(bf16[4,16,128]{2,1,0:T(8,128)(2,1)S(1)} %get-tuple-element.41), channel_id=1, source_target_pairs={{0,4},{1,5},{2,6},{3,7},{4,0},{5,1},{6,2},{7,3},{8,12},{9,13},{10,... | collective-permute-start | bytes 49160 | tf_op jit(solution)/shard_map/ppermute | solution.py:399
  43.0 5.5 %collective-permute-start.11 = (bf16[4,16,128]{2,1,0:T(8,128)(2,1)S(1)}, bf16[4,16,128]{2,1,0:T(8,128)(2,1)S(1)}, u32[]{:S(2)}, u32[]{:S(2)}) collective-permute-start(bf16[4,16,128]{2,1,0:T(8,128)(2,1)S(1)} %get-tuple-element.42), channel_id=1, source_target_pairs={{0,8},{1,9},{2,10},{3,11},{4,12},{5,13},{6,14},{7,15},{8,0},{9,1},... | collective-permute-start | bytes 49160 | tf_op jit(solution)/shard_map/ppermute | solution.py:399
  46.9 5.5 %collective-permute-start.12 = (bf16[4,16,128]{2,1,0:T(8,128)(2,1)S(1)}, bf16[4,16,128]{2,1,0:T(8,128)(2,1)S(1)}, u32[]{:S(2)}, u32[]{:S(2)}) collective-permute-start(bf16[4,16,128]{2,1,0:T(8,128)(2,1)S(1)} %get-tuple-element.43), channel_id=1, source_target_pairs={{0,12},{1,13},{2,14},{3,15},{4,8},{5,9},{6,10},{7,11},{8,4},{9,5},... | collective-permute-start | bytes 49160 | tf_op jit(solution)/shard_map/ppermute | solution.py:399
  53.8 5.0 %collective-permute-start.17 = (f32[2,128,128]{2,1,0:T(8,128)S(1)}, f32[2,128,128]{2,1,0:T(8,128)S(1)}, u32[]{:S(2)}, u32[]{:S(2)}) collective-permute-start(f32[2,128,128]{2,1,0:T(8,128)S(1)} %get-tuple-element.51), channel_id=1, source_target_pairs={{0,2},{1,3},{2,0},{3,1},{4,6},{5,7},{6,4},{7,5},{8,10},{9,11},{10,... | collective-permute-start | bytes 393224 | tf_op jit(solution)/shard_map/ppermute | solution.py:399
  58.8 11.7 %collective-permute-start.18 = (f32[2,128,128]{2,1,0:T(8,128)S(1)}, f32[2,128,128]{2,1,0:T(8,128)S(1)}, u32[]{:S(2)}, u32[]{:S(2)}) collective-permute-start(f32[2,128,128]{2,1,0:T(8,128)S(1)} %collective-permute-done.17.far), channel_id=1, source_target_pairs={{0,1},{1,0},{2,3},{3,2},{4,5},{5,4},{6,7},{7,6},{8,9},{9,8},{10,11... | collective-permute-start | bytes 393224 | tf_op jit(solution)/shard_map/ppermute | solution.py:399
  58.8 10.4 %all-to-all-start.1 = ((bf16[16,16,128]{2,1,0:T(8,128)(2,1)}), bf16[16,16,128]{2,1,0:T(8,128)(2,1)S(1)}, u32[]{:S(2)}, u32[]{:S(2)}) async-start(bf16[16,16,128]{2,1,0:T(8,128)(2,1)} %get-tuple-element.44), calls=%async_computation.1 | async-start | bytes 131072 | tf_op jit(solution)/shard_map/all_to_all | solution.py:402
  62.3 4.0 %collective-permute-start.14 = (bf16[2,64,128]{2,1,0:T(8,128)(2,1)S(1)}, bf16[2,64,128]{2,1,0:T(8,128)(2,1)S(1)}, u32[]{:S(2)}, u32[]{:S(2)}) collective-permute-start(bf16[2,64,128]{2,1,0:T(8,128)(2,1)S(1)} %get-tuple-element.47), channel_id=1, source_target_pairs={{0,2},{1,3},{2,0},{3,1},{4,6},{5,7},{6,4},{7,5},{8,10},{9,11},{10,... | collective-permute-start | bytes 98312 | tf_op jit(solution)/shard_map/ppermute | solution.py:399
  64.1 6.3 %collective-permute-start.16 = (f32[128,128]{1,0:T(8,128)S(1)}, f32[128,128]{1,0:T(8,128)S(1)}, u32[]{:S(2)}, u32[]{:S(2)}) collective-permute-start(f32[128,128]{1,0:T(8,128)S(1)} %get-tuple-element.50), channel_id=1, source_target_pairs={{0,1},{1,0},{2,3},{3,2},{4,5},{5,4},{6,7},{7,6},{8,9},{9,8},{10,11... | collective-permute-start | bytes 196616 | tf_op jit(solution)/shard_map/ppermute | solution.py:399
  66.3 1.4 %collective-permute-start.15 = (bf16[2,64,128]{2,1,0:T(8,128)(2,1)S(1)}, bf16[2,64,128]{2,1,0:T(8,128)(2,1)S(1)}, u32[]{:S(2)}, u32[]{:S(2)}) collective-permute-start(bf16[2,64,128]{2,1,0:T(8,128)(2,1)S(1)} %collective-permute-done.14.adj_far), channel_id=1, source_target_pairs={{0,1},{1,0},{2,3},{3,2},{4,5},{5,4},{6,7},{7,6},{8,9},{9,8},{10,11... | collective-permute-start | bytes 98312 | tf_op jit(solution)/shard_map/ppermute | solution.py:399
  66.3 1.3 %collective-permute-start.13 = (bf16[64,128]{1,0:T(8,128)(2,1)S(1)}, bf16[64,128]{1,0:T(8,128)(2,1)S(1)}, u32[]{:S(2)}, u32[]{:S(2)}) collective-permute-start(bf16[64,128]{1,0:T(8,128)(2,1)S(1)} %get-tuple-element.46), channel_id=1, source_target_pairs={{0,1},{1,0},{2,3},{3,2},{4,5},{5,4},{6,7},{7,6},{8,9},{9,8},{10,11... | collective-permute-start | bytes 49160 | tf_op jit(solution)/shard_map/ppermute | solution.py:399

commit v4 on v3

--- a/solution.py
+++ b/solution.py
@@ -82,21 +82,28 @@
     return vfac[:, :, :, cut].reshape(parts * rows * rank, -1)
 
 
-def first_kernel(data, x, ufac, vfac, to_far, to_near, own, u_own, x_own, v_own, out, *columns, group, width):
+def first_kernel(data, x, ufac, vfac, out, to_far, to_near, own, u_own, x_own, v_own, *columns, group, width):
     rows = data.shape[1]
     sources = x.shape[1]
     lanes = 2 * width
-    folds = ufac.shape[2] // (4 * width)
+    folds = ufac.shape[2] // (2 * lanes)
     step = rows // folds
     q = group_index(group)
 
-    def run(waves, scratch, quarters, sems):
-        wave_copy = pltpu.make_async_copy(data, waves, sems.at[0])
+    def run(stage, waves, scratch, quarters, sems):
+        x_copy = pltpu.make_async_copy(x, x_own, sems.at[0])
         v_copy = pltpu.make_async_copy(vfac, v_own, sems.at[1])
-        u_copy = pltpu.make_async_copy(ufac, u_own, sems.at[2])
-        x_copy = pltpu.make_async_copy(x, x_own, sems.at[3])
-        for copy in (wave_copy, u_copy, v_copy, x_copy):
+        wave_copy = pltpu.make_async_copy(data, waves, sems.at[2])
+        u_copy = pltpu.make_async_copy(ufac, u_own, sems.at[3])
+        out_copy = pltpu.make_async_copy(stage, out, sems.at[4])
+        for copy in (x_copy, v_copy, wave_copy, u_copy):
             copy.start()
+        v_copy.wait()
+        x_copy.wait()
+        send_coeffs(
+            flat_factors(v_own), x_own[0].astype(bf16), x_own[1].astype(bf16), stage, group=group, width=width
+        )
+        out_copy.start()
         wave_copy.wait()
         for s, block in enumerate(slices_of(waves[0], waves[1], width)):
             scratch[jnp.bitwise_xor(q, s)] = block
@@ -105,41 +112,38 @@
             high, low = split(scratch[b])
             for g in range(folds):
                 cut = slice(g * step, (g + 1) * step)
-                lane = 4 * width * g
-                ref[base:base + step, lane:lane + 2 * width] = high[cut]
-                ref[base:base + step, lane + 2 * width:lane + 4 * width] = low[cut]
+                lane = 2 * lanes * g
+                ref[base:base + step, lane:lane + lanes] = high[cut]
+                ref[base:base + step, lane + lanes:lane + 2 * lanes] = low[cut]
         u_copy.wait()
         for part in range(2):
             to_near[step + rows * part:step + rows * (part + 1)] = u_own[part]
             to_far[2 * step + rows * part:2 * step + rows * (part + 1)] = u_own[part]
-        v_copy.wait()
         if columns:
-            far_x, near_x, block_x = columns
+            shared_x, far_x, near_x, block_x = columns
             tall = 2 * v_own.shape[1] * v_own.shape[2]
-            wide = far_x.shape[1]
-            for h in range(sources // wide):
-                cut = slice(h * wide, (h + 1) * wide)
-                far_x[sources + h * tall:sources + (h + 1) * tall] = flat_factors(v_own, cut)
-        x_copy.wait()
-        if columns:
             for s, block in enumerate(slices_of(x_own[0], x_own[1], width)):
                 quarters[jnp.bitwise_xor(q, s)] = block
             block_x[...] = quarters[0]
             high, low = split(quarters[1])
             near_x[:, :lanes] = high
             near_x[:, lanes:] = low
-            far_x[:sources, :lanes] = quarters[2].astype(bf16)
-            far_x[:sources, lanes:] = quarters[3].astype(bf16)
-        send_coeffs(
-            flat_factors(v_own), x_own[0].astype(bf16), x_own[1].astype(bf16), out, group=group, width=width
-        )
+            far_x[...] = quarters[2].astype(bf16)
+            half = sources // 2
+            shared_x[:half, :lanes] = quarters[3, :half].astype(bf16)
+            shared_x[:half, lanes:] = quarters[3, half:].astype(bf16)
+            for h in range(sources // (2 * lanes)):
+                cut = slice(h * 2 * lanes, (h + 1) * 2 * lanes)
+                shared_x[half + h * tall:half + (h + 1) * tall] = flat_factors(v_own, cut)
+        out_copy.wait()
 
     pl.run_scoped(
         run,
+        pltpu.VMEM(out.shape, bf16),
         pltpu.VMEM(data.shape, f32),
-        pltpu.VMEM((group, rows, 2 * width), f32),
+        pltpu.VMEM((group, rows, lanes), f32),
         pltpu.VMEM((group, sources, lanes), f32),
-        pltpu.SemaphoreType.DMA((4,)),
+        pltpu.SemaphoreType.DMA((5,)),
     )
 
 
@@ -220,7 +224,7 @@
 
 def middle_columns_kernel(*refs, group, width, count):
     pieces, refs = refs[:count], refs[count:]
-    (x_own, v_own, near, v_near, far, corner), refs = refs[:6], refs[6:]
+    (x_own, v_own, near, v_near, far, shared, corner), refs = refs[:7], refs[7:]
     outs, (adj_own, adj_near, adj_far) = refs[:count], refs[count:]
     q = group_index(group)
     z = row_index(group)
@@ -229,9 +233,11 @@
     side = count * rank
     tall = 2 * side
 
+    half = sources // 2
+
     def factors(ref):
         wide = ref.shape[1]
-        cuts = [ref[sources + h * tall:sources + (h + 1) * tall] for h in range(sources // wide)]
+        cuts = [ref[half + h * tall:half + (h + 1) * tall] for h in range(sources // wide)]
         return jnp.concatenate(cuts, axis=1)
 
     def run(adj, coeffs):
@@ -242,8 +248,11 @@
         columns = (
             (x_own[...], flat_factors(v_own)),
             (exact[:, :lanes] + exact[:, lanes:], flat_factors(v_near)),
-            (far[:sources, :lanes].astype(f32), factors(far)),
-            (corner[:sources, lanes:].astype(f32), factors(corner)),
+            (far[...].astype(f32), factors(shared)),
+            (
+                jnp.concatenate([corner[:half, :lanes], corner[:half, lanes:]], axis=0).astype(f32),
+                factors(corner),
+            ),
         )
         for k, (x, vcat) in enumerate(columns):
             a = adj[k].reshape(side, lanes)
@@ -408,21 +417,22 @@
     sources = x_init.shape[1]
     tall = 2 * tile_rows * rank
     columns = (
-        shape((sources + tall * sources // (2 * lanes), 2 * lanes), bf16),
+        shape((sources // 2 + tall * sources // (2 * lanes), 2 * lanes), bf16),
+        shape((sources, lanes), bf16),
         shape((sources, 2 * lanes), bf16),
         shape((sources, lanes), f32),
     )
     by_columns = tile_rows == 4
-    to_far, to_near, own, ufac, estimate, vfac, coeffs, *columns = call(
+    coeffs, to_far, to_near, own, ufac, estimate, vfac, *columns = call(
         first_kernel,
         (
+            result(chunks.shape, bf16),
             shape((2 * rows + 2 * step, wide), bf16),
             shape((2 * rows + step, wide), bf16),
             shape((rows, lanes), f32),
             shape(ufac.shape, bf16),
             shape(x_init.shape, f32),
             shape(vfac.shape, bf16),
-            chunks,
         ) + (columns if by_columns else ()),
         data, x_init, ufac, vfac, from_hbm=True, **static,
     )
@@ -442,17 +452,18 @@
             order = {b: exchange(pieces[b], b * group) for b in range(tile_rows - 1, 0, -1)}
             return [pieces[0]] + [order[b] for b in range(1, tile_rows)]
 
-        x_far, x_near, x_own = columns
+        x_shared, x_far, x_near, x_own = columns
+        x_shared = exchange(x_shared, 2)
         x_far = exchange(x_far, 2)
         x_near = exchange(x_near, 1)
         v_near = exchange(vfac, 1)
-        x_corner = exchange(x_far, 1)
+        x_corner = exchange(x_shared, 1)
         pieces = call(row_first_kernel, (piece,) * tile_rows, received, *gathered, **static)
         pieces = along_rows(pieces)
         *pieces, adj_own, adj_near, adj_far = call(
             middle_columns_kernel,
             (piece,) * tile_rows + (shape(side, bf16), shape(side, bf16), shape((2,) + side, bf16)),
-            *pieces, x_own, vfac, x_near, v_near, x_far, x_corner, **counted,
+            *pieces, x_own, vfac, x_near, v_near, x_far, x_shared, x_corner, **counted,
         )
         pieces = along_rows(pieces)
         adj_far = exchange(adj_far, 2)

time: 71.6 us -> 68.9 us (0.962)
  waiting for transfers between devices: 30.7 us -> 27.4 us
  starting transfers between devices: 19 us -> 20.5 us
  blocking collectives: 12.8 us -> 11.7 us
    ppermute x19 -> x20, waiting for transfers between devices: 29.8 us -> 26.5 us  [exchange(): return lax.ppermute(value, 'tile', [(s, s ^ bit) for s in range(tiles)])]
    ppermute x19 -> x20, starting transfers between devices: 15.5 us -> 17 us  [exchange(): return lax.ppermute(value, 'tile', [(s, s ^ bit) for s in range(tiles)])]
    all_to_all x1, blocking collectives: 12.8 us -> 11.7 us  [spread(): lax.all_to_all(value, 'tile', split_axis=0, concat_axis=0, tiled=True)]
  transfers between devices with their start and end apart: 20 -> 21, of which waited for: 10 -> 10; matrix products, arithmetic and copies ran while one was open for 0% -> 0% of each run, Pallas kernels for 4% -> 4%
where the time goes in v4:
time: 68.9 us; the launch traced here: 68.6 us
  waiting for transfers between devices  27.4 us (40%)
  starting transfers between devices  20.5 us (30%)
  blocking collectives  11.7 us (17%)
  Pallas kernels  8.43 us (12%)
  between operations  0.7 us (1%)
    ppermute x20, waiting for transfers between devices, exchange(): return lax.ppermute(value, 'tile', [(s, s ^ bit) for s in range(tiles)])  26.5 us
    ppermute x20, starting transfers between devices, exchange(): return lax.ppermute(value, 'tile', [(s, s ^ bit) for s in range(tiles)])  17 us
    all_to_all x1, blocking collectives, spread(): lax.all_to_all(value, 'tile', split_axis=0, concat_axis=0, tiled=True)  11.7 us
    pallas_call x7, Pallas kernels, call(): pl.pallas_call(functools.partial(kernel, **static), out_shape=out_shape,...  8.43 us
    all_to_all x1, starting transfers between devices, spread(): lax.all_to_all(value, 'tile', split_axis=0, concat_axis=0, tiled=True)  3.5 us
  transfers between devices with their start and end apart: 21, of which 10 were waited for; matrix products, arithmetic and copies ran while one was open for 0% of the time, Pallas kernels for 4%

profile of v4, /device:TPU:0, one launch (start us, length us, event | category | flops | bytes accessed | tf_op | source)
XLA Modules:
  0.0 68.6 jit_solution(5328107732648722120)
XLA Ops:
  0.6 2.3 %shard_map.59 = (bf16[16,16,128]{2,1,0:T(8,128)(2,1)S(1)}, bf16[512,256]{1,0:T(8,128)(2,1)S(1)}, bf16[384,256]{1,0:T(8,128)(2,1)S(1)}, f32[128,128]{1,0:T(8,128)...) custom-call(f32[2,128,256]{2,1,0:T(8,128)} %data.1, ...), custom_call_target="tpu_custom_call" | custom-call | tf_op jit(solution)/shard_map/pallas_call | solution.py:385
  2.9 3.1 %collective-permute-start.1 = (bf16[512,256]{1,0:T(8,128)(2,1)S(1)}, bf16[512,256]{1,0:T(8,128)(2,1)S(1)}, u32[]{:S(2)}, u32[]{:S(2)}) collective-permute-start(bf16[512,256]{1,0:T(8,128)(2,1)S(1)} %get-tuple-element.32), channel_id=1, source_target_pairs={{0,2},{1,3},{2,0},{3,1},{4,6},{5,7},{6,4},{7,5},{8,10},{9,11},{10,... | collective-permute-start | bytes 786440 | tf_op jit(solution)/shard_map/ppermute | solution.py:408
  6.0 0.1 collective-permute-start.9
  6.1 7.1 %collective-permute-done.1.far.refs_7_ = bf16[512,256]{1,0:T(8,128)(2,1)S(1)} collective-permute-done((bf16[512,256]{1,0:T(8,128)(2,1)S(1)}, bf16[512,256]{1,0:T(8,128)(2,1)S(1)}, u32[]{:S(2)}, u32[]{:S(2)}) %collective-permute-start.1) | collective-permute-done | bytes 262176 | tf_op jit(solution)/shard_map/ppermute | solution.py:408
  13.1 0.5 collective-permute-start.6
  13.6 4.3 %collective-permute-done.9.refs_9_ = bf16[512,256]{1,0:T(8,128)(2,1)S(1)} collective-permute-done((bf16[512,256]{1,0:T(8,128)(2,1)S(1)}, bf16[512,256]{1,0:T(8,128)(2,1)S(1)}, u32[]{:S(2)}, u32[]{:S(2)}) %collective-permute-start.9) | collective-permute-done | bytes 262176 | tf_op jit(solution)/shard_map/ppermute | solution.py:408
  17.9 1.7 %collective-permute-start.8 = (bf16[512,128]{1,0:T(8,128)(2,1)S(1)}, bf16[512,128]{1,0:T(8,128)(2,1)S(1)}, u32[]{:S(2)}, u32[]{:S(2)}) collective-permute-start(bf16[512,128]{1,0:T(8,128)(2,1)S(1)} %get-tuple-element.40), channel_id=1, source_target_pairs={{0,2},{1,3},{2,0},{3,1},{4,6},{5,7},{6,4},{7,5},{8,10},{9,11},{10,... | collective-permute-start | bytes 393224 | tf_op jit(solution)/shard_map/ppermute | solution.py:408
  19.6 0.2 collective-permute-start.7
  19.9 11.7 %all_to_all.10.coeffs = bf16[16,16,128]{2,1,0:T(8,128)(2,1)S(1)} all-to-all(bf16[16,16,128]{2,1,0:T(8,128)(2,1)S(1)} %get-tuple-element.28), channel_id=1, replica_groups=mesh['freq'=2,'tile'=16] {'tile'}, dimensions={0} | all-to-all | bytes 131072 | tf_op jit(solution)/shard_map/all_to_all | solution.py:411
  31.5 0.8 %shard_map.60 = (bf16[4,16,128]{2,1,0:T(8,128)(2,1)S(1)}, bf16[4,16,128]{2,1,0:T(8,128)(2,1)S(1)}, bf16[4,16,128]{2,1,0:T(8,128)(2,1)S(1)}, bf16[4,16,128]{2,1,0:T(8,128)(2,1)S(1)}) custom-call(bf16[16,16,128]{2,1,0:T(8,128)(2,1)S(1)} %all_to_all.10.coeffs, f32[128,128]{1,0:T(8,128)S(1)} %get-tuple-element.29.own.refs_4_, ...), custom_call_target="tpu_custom_call" | custom-call | tf_op jit(solution)/shard_map/pallas_call | solution.py:385
  32.4 0.2 collective-permute-start.3
  32.5 1.0 %collective-permute-start.4 = (bf16[4,16,128]{2,1,0:T(8,128)(2,1)S(1)}, bf16[4,16,128]{2,1,0:T(8,128)(2,1)S(1)}, u32[]{:S(2)}, u32[]{:S(2)}) collective-permute-start(bf16[4,16,128]{2,1,0:T(8,128)(2,1)S(1)} %get-tuple-element.35), channel_id=1, source_target_pairs={{0,8},{1,9},{2,10},{3,11},{4,12},{5,13},{6,14},{7,15},{8,0},{9,1},... | collective-permute-start | bytes 49160 | tf_op jit(solution)/shard_map/ppermute | solution.py:408
  33.5 3.3 %collective-permute-start.5 = (bf16[4,16,128]{2,1,0:T(8,128)(2,1)S(1)}, bf16[4,16,128]{2,1,0:T(8,128)(2,1)S(1)}, u32[]{:S(2)}, u32[]{:S(2)}) collective-permute-start(bf16[4,16,128]{2,1,0:T(8,128)(2,1)S(1)} %get-tuple-element.36), channel_id=1, source_target_pairs={{0,12},{1,13},{2,14},{3,15},{4,8},{5,9},{6,10},{7,11},{8,4},{9,5},... | collective-permute-start | bytes 49160 | tf_op jit(solution)/shard_map/ppermute | solution.py:408
  36.8 0.4 collective-permute-done.4.refs_2_
  37.2 1.9 %collective-permute-done.5.refs_3_ = bf16[4,16,128]{2,1,0:T(8,128)(2,1)S(1)} collective-permute-done((bf16[4,16,128]{2,1,0:T(8,128)(2,1)S(1)}, bf16[4,16,128]{2,1,0:T(8,128)(2,1)S(1)}, u32[]{:S(2)}, u32[]{:S(2)}) %collective-permute-start.5) | collective-permute-done | bytes 16416 | tf_op jit(solution)/shard_map/ppermute | solution.py:408
  39.1 1.2 %shard_map.61 = (bf16[4,16,128]{2,1,0:T(8,128)(2,1)S(1)}, bf16[4,16,128]{2,1,0:T(8,128)(2,1)S(1)}, bf16[4,16,128]{2,1,0:T(8,128)(2,1)S(1)}, bf16[4,16,128]{2,1,0...) custom-call(bf16[4,16,128]{2,1,0:T(8,128)(2,1)S(1)} %get-tuple-element, ...), custom_call_target="tpu_custom_call" | custom-call | tf_op jit(solution)/shard_map/pallas_call | solution.py:385
  40.3 3.8 %collective-permute-start.12 = (bf16[4,16,128]{2,1,0:T(8,128)(2,1)S(1)}, bf16[4,16,128]{2,1,0:T(8,128)(2,1)S(1)}, u32[]{:S(2)}, u32[]{:S(2)}) collective-permute-start(bf16[4,16,128]{2,1,0:T(8,128)(2,1)S(1)} %get-tuple-element.44), channel_id=1, source_target_pairs={{0,8},{1,9},{2,10},{3,11},{4,12},{5,13},{6,14},{7,15},{8,0},{9,1},... | collective-permute-start | bytes 49160 | tf_op jit(solution)/shard_map/ppermute | solution.py:408
  44.2 0.6 collective-permute-start.13
  44.7 1.2 %collective-permute-done.12.refs_2_ = bf16[4,16,128]{2,1,0:T(8,128)(2,1)S(1)} collective-permute-done((bf16[4,16,128]{2,1,0:T(8,128)(2,1)S(1)}, bf16[4,16,128]{2,1,0:T(8,128)(2,1)S(1)}, u32[]{:S(2)}, u32[]{:S(2)}) %collective-permute-start.12) | collective-permute-done | bytes 16416 | tf_op jit(solution)/shard_map/ppermute | solution.py:408
  45.9 3.8 %collective-permute-done.13.refs_3_ = bf16[4,16,128]{2,1,0:T(8,128)(2,1)S(1)} collective-permute-done((bf16[4,16,128]{2,1,0:T(8,128)(2,1)S(1)}, bf16[4,16,128]{2,1,0:T(8,128)(2,1)S(1)}, u32[]{:S(2)}, u32[]{:S(2)}) %collective-permute-start.13) | collective-permute-done | bytes 16416 | tf_op jit(solution)/shard_map/ppermute | solution.py:408
  49.7 1.4 %shard_map.62 = (bf16[16,16,128]{2,1,0:T(8,128)(2,1)}, f32[128,128]{1,0:T(8,128)S(1)}, f32[128,128]{1,0:T(8,128)S(1)}, f32[2,128,128]{2,1,0:T(8,128)S(1)}) custom-call(bf16[4,16,128]{2,1,0:T(8,128)(2,1)S(1)} %get-tuple-element.42.refs_0_, bf16[4,16,128]{2,1,0:T(8,128)(2,1)S(1)} %collective-permute-done.11.refs_1_, ...), custom_call_target="tpu_custom_call" | custom-call | tf_op jit(solution)/shard_map/pallas_call | solution.py:385
  51.1 0.1 collective-permute-start.18
  51.2 4.8 %collective-permute-done.18.far = f32[2,128,128]{2,1,0:T(8,128)S(1)} collective-permute-done((f32[2,128,128]{2,1,0:T(8,128)S(1)}, f32[2,128,128]{2,1,0:T(8,128)S(1)}, u32[]{:S(2)}, u32[]{:S(2)}) %collective-permute-start.18) | collective-permute-done | bytes 131104 | tf_op jit(solution)/shard_map/ppermute | solution.py:408
  56.1 3.5 %all-to-all-start.1 = ((bf16[16,16,128]{2,1,0:T(8,128)(2,1)}), bf16[16,16,128]{2,1,0:T(8,128)(2,1)S(1)}, u32[]{:S(2)}, u32[]{:S(2)}) async-start(bf16[16,16,128]{2,1,0:T(8,128)(2,1)} %get-tuple-element.46), calls=%async_computation.1 | async-start | bytes 131072 | tf_op jit(solution)/shard_map/all_to_all | solution.py:411
  59.6 1.8 %collective-permute-start.15 = (bf16[2,64,128]{2,1,0:T(8,128)(2,1)S(1)}, bf16[2,64,128]{2,1,0:T(8,128)(2,1)S(1)}, u32[]{:S(2)}, u32[]{:S(2)}) collective-permute-start(bf16[2,64,128]{2,1,0:T(8,128)(2,1)S(1)} %get-tuple-element.49), channel_id=1, source_target_pairs={{0,2},{1,3},{2,0},{3,1},{4,6},{5,7},{6,4},{7,5},{8,10},{9,11},{10,... | collective-permute-start | bytes 98312 | tf_op jit(solution)/shard_map/ppermute | solution.py:408
  61.4 2.2 %collective-permute-done.15.adj_far = bf16[2,64,128]{2,1,0:T(8,128)(2,1)S(1)} collective-permute-done((bf16[2,64,128]{2,1,0:T(8,128)(2,1)S(1)}, bf16[2,64,128]{2,1,0:T(8,128)(2,1)S(1)}, u32[]{:S(2)}, u32[]{:S(2)}) %collective-permute-start.15) | collective-permute-done | bytes 32800 | tf_op jit(solution)/shard_map/ppermute | solution.py:408
  63.6 0.5 collective-permute-start.14
  64.1 0.8 %collective-permute-done.14.adj_near = bf16[64,128]{1,0:T(8,128)(2,1)S(1)} collective-permute-done((bf16[64,128]{1,0:T(8,128)(2,1)S(1)}, bf16[64,128]{1,0:T(8,128)(2,1)S(1)}, u32[]{:S(2)}, u32[]{:S(2)}) %collective-permute-start.14) | collective-permute-done | bytes 16416 | tf_op jit(solution)/shard_map/ppermute | solution.py:408
  65.0 0.6 shard_map.63.x
  65.6 0.9 %all-to-all-done.1.adjoint = bf16[16,16,128]{2,1,0:T(8,128)(2,1)S(1)} async-done(((bf16[16,16,128]{2,1,0:T(8,128)(2,1)}), bf16[16,16,128]{2,1,0:T(8,128)(2,1)S(1)}, u32[]{:S(2)}, u32[]{:S(2)}) %all-to-all-start.1) | async-done | bytes 65568 | tf_op jit(solution)/shard_map/all_to_all | solution.py:411
  66.5 1.3 %shard_map.64 = f32[2,512,256]{2,1,0:T(8,128)} custom-call(bf16[16,16,128]{2,1,0:T(8,128)(2,1)S(1)} %all-to-all-done.1.adjoint, f32[2,512,256]{2,1,0:T(8,128)S(1)} %shard_map.63.x, bf16[2,4,16,512]{3,2,1,0:T(8,128)(2,1)S(1)} %get-tuple-element.38.refs_5_.vfac), custom_call_target="tpu_custom_call" | custom-call | tf_op jit(solution)/shard_map/pallas_call | solution.py:385
  67.8 0.9 %shard_map.65 = f32[2,128,256]{2,1,0:T(8,128)} custom-call(f32[128,128]{1,0:T(8,128)S(1)} %get-tuple-element.51.misfit, f32[128,128]{1,0:T(8,128)S(1)} %collective-permute-done.17.near, f32[2,128,128]{2,1,0:T(8,128)S(1)} %collective-permute-done.18.far, f32[2,128,128]{2,1,0:T(8,128)S(1)} %collective-permute-done.19.far_near), custom_call_target="tpu_custom_call" | custom-call | tf_op jit(solution)/shard_map/pallas_call | solution.py:385
  (18 shorter events, 0.1 us)
Async XLA Ops:
  2.9 10.2 %collective-permute-start.1 = (bf16[512,256]{1,0:T(8,128)(2,1)S(1)}, bf16[512,256]{1,0:T(8,128)(2,1)S(1)}, u32[]{:S(2)}, u32[]{:S(2)}) collective-permute-start(bf16[512,256]{1,0:T(8,128)(2,1)S(1)} %get-tuple-element.32), channel_id=1, source_target_pairs={{0,2},{1,3},{2,0},{3,1},{4,6},{5,7},{6,4},{7,5},{8,10},{9,11},{10,... | collective-permute-start | bytes 786440 | tf_op jit(solution)/shard_map/ppermute | solution.py:408
  6.0 11.9 %collective-permute-start.9 = (bf16[512,256]{1,0:T(8,128)(2,1)S(1)}, bf16[512,256]{1,0:T(8,128)(2,1)S(1)}, u32[]{:S(2)}, u32[]{:S(2)}) collective-permute-start(bf16[512,256]{1,0:T(8,128)(2,1)S(1)} %get-tuple-element.41), channel_id=1, source_target_pairs={{0,2},{1,3},{2,0},{3,1},{4,6},{5,7},{6,4},{7,5},{8,10},{9,11},{10,... | collective-permute-start | bytes 786440 | tf_op jit(solution)/shard_map/ppermute | solution.py:408
  6.1 13.6 %collective-permute-start = (bf16[384,256]{1,0:T(8,128)(2,1)S(1)}, bf16[384,256]{1,0:T(8,128)(2,1)S(1)}, u32[]{:S(2)}, u32[]{:S(2)}) collective-permute-start(bf16[384,256]{1,0:T(8,128)(2,1)S(1)} %get-tuple-element.31), channel_id=1, source_target_pairs={{0,1},{1,0},{2,3},{3,2},{4,5},{5,4},{6,7},{7,6},{8,9},{9,8},{10,11... | collective-permute-start | bytes 589832 | tf_op jit(solution)/shard_map/ppermute | solution.py:408
  13.1 18.4 %collective-permute-start.2 = (bf16[512,256]{1,0:T(8,128)(2,1)S(1)}, bf16[512,256]{1,0:T(8,128)(2,1)S(1)}, u32[]{:S(2)}, u32[]{:S(2)}) collective-permute-start(bf16[512,256]{1,0:T(8,128)(2,1)S(1)} %collective-permute-done.1.far.refs_7_), channel_id=1, source_target_pairs={{0,1},{1,0},{2,3},{3,2},{4,5},{5,4},{6,7},{7,6},{8,9},{9,8},{10,11... | collective-permute-start | bytes 786440 | tf_op jit(solution)/shard_map/ppermute | solution.py:408
  13.1 23.7 %collective-permute-start.6 = (bf16[512,256]{1,0:T(8,128)(2,1)S(1)}, bf16[512,256]{1,0:T(8,128)(2,1)S(1)}, u32[]{:S(2)}, u32[]{:S(2)}) collective-permute-start(bf16[512,256]{1,0:T(8,128)(2,1)S(1)} %get-tuple-element.39), channel_id=1, source_target_pairs={{0,1},{1,0},{2,3},{3,2},{4,5},{5,4},{6,7},{7,6},{8,9},{9,8},{10,11... | collective-permute-start | bytes 786440 | tf_op jit(solution)/shard_map/ppermute | solution.py:408
  17.9 18.9 %collective-permute-start.10 = (bf16[512,256]{1,0:T(8,128)(2,1)S(1)}, bf16[512,256]{1,0:T(8,128)(2,1)S(1)}, u32[]{:S(2)}, u32[]{:S(2)}) collective-permute-start(bf16[512,256]{1,0:T(8,128)(2,1)S(1)} %collective-permute-done.9.refs_9_), channel_id=1, source_target_pairs={{0,1},{1,0},{2,3},{3,2},{4,5},{5,4},{6,7},{7,6},{8,9},{9,8},{10,11... | collective-permute-start | bytes 786440 | tf_op jit(solution)/shard_map/ppermute | solution.py:408
  17.9 14.6 %collective-permute-start.8 = (bf16[512,128]{1,0:T(8,128)(2,1)S(1)}, bf16[512,128]{1,0:T(8,128)(2,1)S(1)}, u32[]{:S(2)}, u32[]{:S(2)}) collective-permute-start(bf16[512,128]{1,0:T(8,128)(2,1)S(1)} %get-tuple-element.40), channel_id=1, source_target_pairs={{0,2},{1,3},{2,0},{3,1},{4,6},{5,7},{6,4},{7,5},{8,10},{9,11},{10,... | collective-permute-start | bytes 393224 | tf_op jit(solution)/shard_map/ppermute | solution.py:408
  19.6 13.9 %collective-permute-start.7 = (bf16[2,4,16,512]{3,2,1,0:T(8,128)(2,1)S(1)}, bf16[2,4,16,512]{3,2,1,0:T(8,128)(2,1)S(1)}, u32[]{:S(2)}, u32[]{:S(2)}) collective-permute-start(bf16[2,4,16,512]{3,2,1,0:T(8,128)(2,1)S(1)} %get-tuple-element.38.refs_5_.vfac), channel_id=1, source_target_pairs={{0,1},{1,0},{2,3},{3,2},{4,5},{5,4},{6,7},{7,6},{8,9},{9,8},{10,11... | collective-permute-start | bytes 393224 | tf_op jit(solution)/shard_map/ppermute | solution.py:408
  32.4 4.5 %collective-permute-start.3 = (bf16[4,16,128]{2,1,0:T(8,128)(2,1)S(1)}, bf16[4,16,128]{2,1,0:T(8,128)(2,1)S(1)}, u32[]{:S(2)}, u32[]{:S(2)}) collective-permute-start(bf16[4,16,128]{2,1,0:T(8,128)(2,1)S(1)} %get-tuple-element.34), channel_id=1, source_target_pairs={{0,4},{1,5},{2,6},{3,7},{4,0},{5,1},{6,2},{7,3},{8,12},{9,13},{10,... | collective-permute-start | bytes 49160 | tf_op jit(solution)/shard_map/ppermute | solution.py:408
  32.5 4.6 %collective-permute-start.4 = (bf16[4,16,128]{2,1,0:T(8,128)(2,1)S(1)}, bf16[4,16,128]{2,1,0:T(8,128)(2,1)S(1)}, u32[]{:S(2)}, u32[]{:S(2)}) collective-permute-start(bf16[4,16,128]{2,1,0:T(8,128)(2,1)S(1)} %get-tuple-element.35), channel_id=1, source_target_pairs={{0,8},{1,9},{2,10},{3,11},{4,12},{5,13},{6,14},{7,15},{8,0},{9,1},... | collective-permute-start | bytes 49160 | tf_op jit(solution)/shard_map/ppermute | solution.py:408
  33.5 5.5 %collective-permute-start.5 = (bf16[4,16,128]{2,1,0:T(8,128)(2,1)S(1)}, bf16[4,16,128]{2,1,0:T(8,128)(2,1)S(1)}, u32[]{:S(2)}, u32[]{:S(2)}) collective-permute-start(bf16[4,16,128]{2,1,0:T(8,128)(2,1)S(1)} %get-tuple-element.36), channel_id=1, source_target_pairs={{0,12},{1,13},{2,14},{3,15},{4,8},{5,9},{6,10},{7,11},{8,4},{9,5},... | collective-permute-start | bytes 49160 | tf_op jit(solution)/shard_map/ppermute | solution.py:408
  40.3 4.5 %collective-permute-start.11 = (bf16[4,16,128]{2,1,0:T(8,128)(2,1)S(1)}, bf16[4,16,128]{2,1,0:T(8,128)(2,1)S(1)}, u32[]{:S(2)}, u32[]{:S(2)}) collective-permute-start(bf16[4,16,128]{2,1,0:T(8,128)(2,1)S(1)} %get-tuple-element.43), channel_id=1, source_target_pairs={{0,4},{1,5},{2,6},{3,7},{4,0},{5,1},{6,2},{7,3},{8,12},{9,13},{10,... | collective-permute-start | bytes 49160 | tf_op jit(solution)/shard_map/ppermute | solution.py:408
  40.3 5.5 %collective-permute-start.12 = (bf16[4,16,128]{2,1,0:T(8,128)(2,1)S(1)}, bf16[4,16,128]{2,1,0:T(8,128)(2,1)S(1)}, u32[]{:S(2)}, u32[]{:S(2)}) collective-permute-start(bf16[4,16,128]{2,1,0:T(8,128)(2,1)S(1)} %get-tuple-element.44), channel_id=1, source_target_pairs={{0,8},{1,9},{2,10},{3,11},{4,12},{5,13},{6,14},{7,15},{8,0},{9,1},... | collective-permute-start | bytes 49160 | tf_op jit(solution)/shard_map/ppermute | solution.py:408
  44.2 5.5 %collective-permute-start.13 = (bf16[4,16,128]{2,1,0:T(8,128)(2,1)S(1)}, bf16[4,16,128]{2,1,0:T(8,128)(2,1)S(1)}, u32[]{:S(2)}, u32[]{:S(2)}) collective-permute-start(bf16[4,16,128]{2,1,0:T(8,128)(2,1)S(1)} %get-tuple-element.45), channel_id=1, source_target_pairs={{0,12},{1,13},{2,14},{3,15},{4,8},{5,9},{6,10},{7,11},{8,4},{9,5},... | collective-permute-start | bytes 49160 | tf_op jit(solution)/shard_map/ppermute | solution.py:408
  51.1 5.0 %collective-permute-start.18 = (f32[2,128,128]{2,1,0:T(8,128)S(1)}, f32[2,128,128]{2,1,0:T(8,128)S(1)}, u32[]{:S(2)}, u32[]{:S(2)}) collective-permute-start(f32[2,128,128]{2,1,0:T(8,128)S(1)} %get-tuple-element.53), channel_id=1, source_target_pairs={{0,2},{1,3},{2,0},{3,1},{4,6},{5,7},{6,4},{7,5},{8,10},{9,11},{10,... | collective-permute-start | bytes 393224 | tf_op jit(solution)/shard_map/ppermute | solution.py:408
  56.1 11.7 %collective-permute-start.19 = (f32[2,128,128]{2,1,0:T(8,128)S(1)}, f32[2,128,128]{2,1,0:T(8,128)S(1)}, u32[]{:S(2)}, u32[]{:S(2)}) collective-permute-start(f32[2,128,128]{2,1,0:T(8,128)S(1)} %collective-permute-done.18.far), channel_id=1, source_target_pairs={{0,1},{1,0},{2,3},{3,2},{4,5},{5,4},{6,7},{7,6},{8,9},{9,8},{10,11... | collective-permute-start | bytes 393224 | tf_op jit(solution)/shard_map/ppermute | solution.py:408
  56.1 10.4 %all-to-all-start.1 = ((bf16[16,16,128]{2,1,0:T(8,128)(2,1)}), bf16[16,16,128]{2,1,0:T(8,128)(2,1)S(1)}, u32[]{:S(2)}, u32[]{:S(2)}) async-start(bf16[16,16,128]{2,1,0:T(8,128)(2,1)} %get-tuple-element.46), calls=%async_computation.1 | async-start | bytes 131072 | tf_op jit(solution)/shard_map/all_to_all | solution.py:411
  59.6 4.0 %collective-permute-start.15 = (bf16[2,64,128]{2,1,0:T(8,128)(2,1)S(1)}, bf16[2,64,128]{2,1,0:T(8,128)(2,1)S(1)}, u32[]{:S(2)}, u32[]{:S(2)}) collective-permute-start(bf16[2,64,128]{2,1,0:T(8,128)(2,1)S(1)} %get-tuple-element.49), channel_id=1, source_target_pairs={{0,2},{1,3},{2,0},{3,1},{4,6},{5,7},{6,4},{7,5},{8,10},{9,11},{10,... | collective-permute-start | bytes 98312 | tf_op jit(solution)/shard_map/ppermute | solution.py:408
  61.4 6.3 %collective-permute-start.17 = (f32[128,128]{1,0:T(8,128)S(1)}, f32[128,128]{1,0:T(8,128)S(1)}, u32[]{:S(2)}, u32[]{:S(2)}) collective-permute-start(f32[128,128]{1,0:T(8,128)S(1)} %get-tuple-element.52), channel_id=1, source_target_pairs={{0,1},{1,0},{2,3},{3,2},{4,5},{5,4},{6,7},{7,6},{8,9},{9,8},{10,11... | collective-permute-start | bytes 196616 | tf_op jit(solution)/shard_map/ppermute | solution.py:408
  63.6 1.4 %collective-permute-start.16 = (bf16[2,64,128]{2,1,0:T(8,128)(2,1)S(1)}, bf16[2,64,128]{2,1,0:T(8,128)(2,1)S(1)}, u32[]{:S(2)}, u32[]{:S(2)}) collective-permute-start(bf16[2,64,128]{2,1,0:T(8,128)(2,1)S(1)} %collective-permute-done.15.adj_far), channel_id=1, source_target_pairs={{0,1},{1,0},{2,3},{3,2},{4,5},{5,4},{6,7},{7,6},{8,9},{9,8},{10,11... | collective-permute-start | bytes 98312 | tf_op jit(solution)/shard_map/ppermute | solution.py:408
  63.6 1.3 %collective-permute-start.14 = (bf16[64,128]{1,0:T(8,128)(2,1)S(1)}, bf16[64,128]{1,0:T(8,128)(2,1)S(1)}, u32[]{:S(2)}, u32[]{:S(2)}) collective-permute-start(bf16[64,128]{1,0:T(8,128)(2,1)S(1)} %get-tuple-element.48), channel_id=1, source_target_pairs={{0,1},{1,0},{2,3},{3,2},{4,5},{5,4},{6,7},{7,6},{8,9},{9,8},{10,11... | collective-permute-start | bytes 49160 | tf_op jit(solution)/shard_map/ppermute | solution.py:408

commit v5 on v4

--- a/solution.py
+++ b/solution.py
@@ -82,6 +82,19 @@
     return vfac[:, :, :, cut].reshape(parts * rows * rank, -1)
 
 
+def half_blocks(x, which, parity, lanes):
+    cut = pl.ds(pl.multiple_of(which * lanes, lanes), lanes)
+    even, odd = interleave(x[0, :, cut], x[1, :, cut])
+    first = jnp.broadcast_to(parity, even.shape) == 0
+    return jnp.where(first, even, odd), jnp.where(first, odd, even)
+
+
+def blocks_kernel(x_own, x_near, own, near, *, group, width):
+    q = group_index(group)
+    for x, out in ((x_own, own), (x_near, near)):
+        out[...], _ = half_blocks(x, lax.div(q, 2), lax.rem(q, 2), 2 * width)
+
+
 def first_kernel(data, x, ufac, vfac, out, to_far, to_near, own, u_own, x_own, v_own, *columns, group, width):
     rows = data.shape[1]
     sources = x.shape[1]
@@ -90,7 +103,7 @@
     step = rows // folds
     q = group_index(group)
 
-    def run(stage, waves, scratch, quarters, sems):
+    def run(stage, waves, scratch, sems):
         x_copy = pltpu.make_async_copy(x, x_own, sems.at[0])
         v_copy = pltpu.make_async_copy(vfac, v_own, sems.at[1])
         wave_copy = pltpu.make_async_copy(data, waves, sems.at[2])
@@ -120,18 +133,13 @@
             to_near[step + rows * part:step + rows * (part + 1)] = u_own[part]
             to_far[2 * step + rows * part:2 * step + rows * (part + 1)] = u_own[part]
         if columns:
-            shared_x, far_x, near_x, block_x = columns
+            shared_x, far_x = columns
             tall = 2 * v_own.shape[1] * v_own.shape[2]
-            for s, block in enumerate(slices_of(x_own[0], x_own[1], width)):
-                quarters[jnp.bitwise_xor(q, s)] = block
-            block_x[...] = quarters[0]
-            high, low = split(quarters[1])
-            near_x[:, :lanes] = high
-            near_x[:, lanes:] = low
-            far_x[...] = quarters[2].astype(bf16)
+            same, other = half_blocks(x_own, 1 - lax.div(q, 2), lax.rem(q, 2), lanes)
+            far_x[...] = same.astype(bf16)
             half = sources // 2
-            shared_x[:half, :lanes] = quarters[3, :half].astype(bf16)
-            shared_x[:half, lanes:] = quarters[3, half:].astype(bf16)
+            shared_x[:half, :lanes] = other[:half].astype(bf16)
+            shared_x[:half, lanes:] = other[half:].astype(bf16)
             for h in range(sources // (2 * lanes)):
                 cut = slice(h * 2 * lanes, (h + 1) * 2 * lanes)
                 shared_x[half + h * tall:half + (h + 1) * tall] = flat_factors(v_own, cut)
@@ -142,7 +150,6 @@
         pltpu.VMEM(out.shape, bf16),
         pltpu.VMEM(data.shape, f32),
         pltpu.VMEM((group, rows, lanes), f32),
-        pltpu.VMEM((group, sources, lanes), f32),
         pltpu.SemaphoreType.DMA((5,)),
     )
 
@@ -244,10 +251,9 @@
         for b, piece in enumerate(pieces):
             for k in range(group):
                 adj[k, jnp.bitwise_xor(z, b)] = piece[jnp.bitwise_xor(q, k)]
-        exact = near[...].astype(f32)
         columns = (
             (x_own[...], flat_factors(v_own)),
-            (exact[:, :lanes] + exact[:, lanes:], flat_factors(v_near)),
+            (near[...], flat_factors(v_near)),
             (far[...].astype(f32), factors(shared)),
             (
                 jnp.concatenate([corner[:half, :lanes], corner[:half, lanes:]], axis=0).astype(f32),
@@ -419,8 +425,6 @@
     columns = (
         shape((sources // 2 + tall * sources // (2 * lanes), 2 * lanes), bf16),
         shape((sources, lanes), bf16),
-        shape((sources, 2 * lanes), bf16),
-        shape((sources, lanes), f32),
     )
     by_columns = tile_rows == 4
     coeffs, to_far, to_near, own, ufac, estimate, vfac, *columns = call(
@@ -452,10 +456,11 @@
             order = {b: exchange(pieces[b], b * group) for b in range(tile_rows - 1, 0, -1)}
             return [pieces[0]] + [order[b] for b in range(1, tile_rows)]
 
-        x_shared, x_far, x_near, x_own = columns
+        x_shared, x_far = columns
         x_shared = exchange(x_shared, 2)
         x_far = exchange(x_far, 2)
-        x_near = exchange(x_near, 1)
+        x_near = exchange(x_init, 1)
+        x_own, x_near = call(blocks_kernel, (shape((sources, lanes), f32),) * 2, estimate, x_near, **static)
         v_near = exchange(vfac, 1)
         x_corner = exchange(x_shared, 1)
         pieces = call(row_first_kernel, (piece,) * tile_rows, received, *gathered, **static)
@@ -486,9 +491,7 @@
     misfit_corner = exchange(misfit_far, 1)
     adjoint = spread(adjoint)
     solved = call(last_kernel, result(x_init.shape, f32), adjoint, estimate, vfac, **static)
-    residual = call(
-        residual_kernel, result(data.shape, f32), misfit, misfit_near, misfit_far, misfit_corner, **static
-    )
+    residual = call(residual_kernel, result(data.shape, f32), misfit, misfit_near, misfit_far, misfit_corner, **static)
     return (solved, residual)
 
 

time: 68.9 us -> 71.3 us (1.035)
  blocking collectives: 11.7 us -> 0 us
  waiting for transfers between devices: 27.4 us -> 34.4 us
  starting transfers between devices: 20.5 us -> 25.4 us
  Pallas kernels: 8.43 us -> 10.4 us
    all_to_all x1 -> x0, blocking collectives: 11.7 us -> none  [spread(): lax.all_to_all(value, 'tile', split_axis=0, concat_axis=0, tiled=True)]
    all_to_all x1 -> x2, waiting for transfers between devices: 0.89 us -> 7.3 us  [spread(): lax.all_to_all(value, 'tile', split_axis=0, concat_axis=0, tiled=True)]
    all_to_all x1 -> x2, starting transfers between devices: 3.5 us -> 8.49 us  [spread(): lax.all_to_all(value, 'tile', split_axis=0, concat_axis=0, tiled=True)]
    pallas_call x7 -> x8, Pallas kernels: 8.43 us -> 10.4 us  [call(): pl.pallas_call(functools.partial(kernel, **static), out_shape=out_shape,...]
  transfers between devices with their start and end apart: 21 -> 22, of which waited for: 10 -> 10; matrix products, arithmetic and copies ran while one was open for 0% -> 0% of each run, Pallas kernels for 4% -> 8%
where the time goes in v5:
time: 71.3 us; the launch traced here: 71 us
  waiting for transfers between devices  34.4 us (48%)
  starting transfers between devices  25.4 us (36%)
  Pallas kernels  10.4 us (15%)
  between operations  0.74 us (1%)
    ppermute x20, waiting for transfers between devices, exchange(): return lax.ppermute(value, 'tile', [(s, s ^ bit) for s in range(tiles)])  27.1 us
    ppermute x20, starting transfers between devices, exchange(): return lax.ppermute(value, 'tile', [(s, s ^ bit) for s in range(tiles)])  16.9 us
    pallas_call x8, Pallas kernels, call(): pl.pallas_call(functools.partial(kernel, **static), out_shape=out_shape,...  10.4 us
    all_to_all x2, starting transfers between devices, spread(): lax.all_to_all(value, 'tile', split_axis=0, concat_axis=0, tiled=True)  8.49 us
    all_to_all x2, waiting for transfers between devices, spread(): lax.all_to_all(value, 'tile', split_axis=0, concat_axis=0, tiled=True)  7.3 us
  transfers between devices with their start and end apart: 22, of which 10 were waited for; matrix products, arithmetic and copies ran while one was open for 0% of the time, Pallas kernels for 8%

profile of v5, /device:TPU:0, one launch (start us, length us, event | category | flops | bytes accessed | tf_op | source)
XLA Modules:
  0.0 71.0 jit_solution(2933119325417253405)
XLA Ops:
  0.6 0.6 collective-permute-start.6
  1.2 2.9 %shard_map.59 = (bf16[16,16,128]{2,1,0:T(8,128)(2,1)}, bf16[512,256]{1,0:T(8,128)(2,1)S(1)}, bf16[384,256]{1,0:T(8,128)(2,1)}, f32[128,128]{1,0:T(8,128)S(1)}, b...) custom-call(f32[2,128,256]{2,1,0:T(8,128)} %data.1, ...), custom_call_target="tpu_custom_call" | custom-call | tf_op jit(solution)/shard_map/pallas_call | solution.py:391
  4.1 2.5 %collective-permute-start.1 = (bf16[512,256]{1,0:T(8,128)(2,1)S(1)}, bf16[512,256]{1,0:T(8,128)(2,1)S(1)}, u32[]{:S(2)}, u32[]{:S(2)}) collective-permute-start(bf16[512,256]{1,0:T(8,128)(2,1)S(1)} %get-tuple-element.32), channel_id=1, source_target_pairs={{0,2},{1,3},{2,0},{3,1},{4,6},{5,7},{6,4},{7,5},{8,10},{9,11},{10,... | collective-permute-start | bytes 786440 | tf_op jit(solution)/shard_map/ppermute | solution.py:414
  6.6 0.2 collective-permute-start
  6.8 6.9 %collective-permute-done.1.far.refs_7_ = bf16[512,256]{1,0:T(8,128)(2,1)S(1)} collective-permute-done((bf16[512,256]{1,0:T(8,128)(2,1)S(1)}, bf16[512,256]{1,0:T(8,128)(2,1)S(1)}, u32[]{:S(2)}, u32[]{:S(2)}) %collective-permute-start.1) | collective-permute-done | bytes 262176 | tf_op jit(solution)/shard_map/ppermute | solution.py:414
  13.8 5.4 %collective-permute-done.9.refs_9_ = bf16[512,256]{1,0:T(8,128)(2,1)S(1)} collective-permute-done((bf16[512,256]{1,0:T(8,128)(2,1)S(1)}, bf16[512,256]{1,0:T(8,128)(2,1)S(1)}, u32[]{:S(2)}, u32[]{:S(2)}) %collective-permute-start.9) | collective-permute-done | bytes 262176 | tf_op jit(solution)/shard_map/ppermute | solution.py:414
  19.2 1.7 %collective-permute-start.8 = (bf16[512,128]{1,0:T(8,128)(2,1)}, bf16[512,128]{1,0:T(8,128)(2,1)}, u32[]{:S(2)}, u32[]{:S(2)}) collective-permute-start(bf16[512,128]{1,0:T(8,128)(2,1)} %get-tuple-element.41), channel_id=1, source_target_pairs={{0,2},{1,3},{2,0},{3,1},{4,6},{5,7},{6,4},{7,5},{8,10},{9,11},{10,... | collective-permute-start | bytes 393224 | tf_op jit(solution)/shard_map/ppermute | solution.py:414
  20.9 5.0 %all-to-all-start = ((bf16[16,16,128]{2,1,0:T(8,128)(2,1)}), bf16[16,16,128]{2,1,0:T(8,128)(2,1)S(1)}, u32[]{:S(2)}, u32[]{:S(2)}) async-start(bf16[16,16,128]{2,1,0:T(8,128)(2,1)} %get-tuple-element.28), calls=%async_computation | async-start | bytes 131072 | tf_op jit(solution)/shard_map/all_to_all | solution.py:417
  25.9 0.5 collective-permute-start.7
  26.4 6.4 %all-to-all-done.coeffs = bf16[16,16,128]{2,1,0:T(8,128)(2,1)S(1)} async-done(((bf16[16,16,128]{2,1,0:T(8,128)(2,1)}), bf16[16,16,128]{2,1,0:T(8,128)(2,1)S(1)}, u32[]{:S(2)}, u32[]{:S(2)}) %all-to-all-start) | async-done | bytes 65568 | tf_op jit(solution)/shard_map/all_to_all | solution.py:417
  32.8 0.8 %shard_map.60 = (bf16[4,16,128]{2,1,0:T(8,128)(2,1)S(1)}, bf16[4,16,128]{2,1,0:T(8,128)(2,1)S(1)}, bf16[4,16,128]{2,1,0:T(8,128)(2,1)S(1)}, bf16[4,16,128]{2,1,0:T(8,128)(2,1)S(1)}) custom-call(bf16[16,16,128]{2,1,0:T(8,128)(2,1)S(1)} %all-to-all-done.coeffs, f32[128,128]{1,0:T(8,128)S(1)} %get-tuple-element.29.own.refs_4_, ...), custom_call_target="tpu_custom_call" | custom-call | tf_op jit(solution)/shard_map/pallas_call | solution.py:391
  33.6 0.2 collective-permute-start.3
  33.8 1.0 %collective-permute-start.4 = (bf16[4,16,128]{2,1,0:T(8,128)(2,1)S(1)}, bf16[4,16,128]{2,1,0:T(8,128)(2,1)S(1)}, u32[]{:S(2)}, u32[]{:S(2)}) collective-permute-start(bf16[4,16,128]{2,1,0:T(8,128)(2,1)S(1)} %get-tuple-element.35), channel_id=1, source_target_pairs={{0,8},{1,9},{2,10},{3,11},{4,12},{5,13},{6,14},{7,15},{8,0},{9,1},... | collective-permute-start | bytes 49160 | tf_op jit(solution)/shard_map/ppermute | solution.py:414
  34.8 3.3 %collective-permute-start.5 = (bf16[4,16,128]{2,1,0:T(8,128)(2,1)S(1)}, bf16[4,16,128]{2,1,0:T(8,128)(2,1)S(1)}, u32[]{:S(2)}, u32[]{:S(2)}) collective-permute-start(bf16[4,16,128]{2,1,0:T(8,128)(2,1)S(1)} %get-tuple-element.36), channel_id=1, source_target_pairs={{0,12},{1,13},{2,14},{3,15},{4,8},{5,9},{6,10},{7,11},{8,4},{9,5},... | collective-permute-start | bytes 49160 | tf_op jit(solution)/shard_map/ppermute | solution.py:414
  38.1 0.3 shard_map.61
  38.5 1.9 %collective-permute-done.5.refs_3_ = bf16[4,16,128]{2,1,0:T(8,128)(2,1)S(1)} collective-permute-done((bf16[4,16,128]{2,1,0:T(8,128)(2,1)S(1)}, bf16[4,16,128]{2,1,0:T(8,128)(2,1)S(1)}, u32[]{:S(2)}, u32[]{:S(2)}) %collective-permute-start.5) | collective-permute-done | bytes 16416 | tf_op jit(solution)/shard_map/ppermute | solution.py:414
  40.4 2.2 %shard_map.62 = (bf16[4,16,128]{2,1,0:T(8,128)(2,1)S(1)}, bf16[4,16,128]{2,1,0:T(8,128)(2,1)S(1)}, bf16[4,16,128]{2,1,0:T(8,128)(2,1)S(1)}, bf16[4,16,128]{2,1,0...) custom-call(bf16[4,16,128]{2,1,0:T(8,128)(2,1)S(1)} %get-tuple-element, ...), custom_call_target="tpu_custom_call" | custom-call | tf_op jit(solution)/shard_map/pallas_call | solution.py:391
  42.7 3.8 %collective-permute-start.12 = (bf16[4,16,128]{2,1,0:T(8,128)(2,1)S(1)}, bf16[4,16,128]{2,1,0:T(8,128)(2,1)S(1)}, u32[]{:S(2)}, u32[]{:S(2)}) collective-permute-start(bf16[4,16,128]{2,1,0:T(8,128)(2,1)S(1)} %get-tuple-element.45), channel_id=1, source_target_pairs={{0,8},{1,9},{2,10},{3,11},{4,12},{5,13},{6,14},{7,15},{8,0},{9,1},... | collective-permute-start | bytes 49160 | tf_op jit(solution)/shard_map/ppermute | solution.py:414
  46.5 0.6 collective-permute-start.13
  47.1 1.2 %collective-permute-done.12.refs_2_ = bf16[4,16,128]{2,1,0:T(8,128)(2,1)S(1)} collective-permute-done((bf16[4,16,128]{2,1,0:T(8,128)(2,1)S(1)}, bf16[4,16,128]{2,1,0:T(8,128)(2,1)S(1)}, u32[]{:S(2)}, u32[]{:S(2)}) %collective-permute-start.12) | collective-permute-done | bytes 16416 | tf_op jit(solution)/shard_map/ppermute | solution.py:414
  48.2 3.8 %collective-permute-done.13.refs_3_ = bf16[4,16,128]{2,1,0:T(8,128)(2,1)S(1)} collective-permute-done((bf16[4,16,128]{2,1,0:T(8,128)(2,1)S(1)}, bf16[4,16,128]{2,1,0:T(8,128)(2,1)S(1)}, u32[]{:S(2)}, u32[]{:S(2)}) %collective-permute-start.13) | collective-permute-done | bytes 16416 | tf_op jit(solution)/shard_map/ppermute | solution.py:414
  52.0 1.4 %shard_map.63 = (bf16[16,16,128]{2,1,0:T(8,128)(2,1)}, f32[128,128]{1,0:T(8,128)S(1)}, f32[128,128]{1,0:T(8,128)S(1)}, f32[2,128,128]{2,1,0:T(8,128)S(1)}) custom-call(bf16[4,16,128]{2,1,0:T(8,128)(2,1)S(1)} %get-tuple-element.43.refs_0_, bf16[4,16,128]{2,1,0:T(8,128)(2,1)S(1)} %collective-permute-done.11.refs_1_, ...), custom_call_target="tpu_custom_call" | custom-call | tf_op jit(solution)/shard_map/pallas_call | solution.py:391
  53.6 4.8 %collective-permute-done.18.far = f32[2,128,128]{2,1,0:T(8,128)S(1)} collective-permute-done((f32[2,128,128]{2,1,0:T(8,128)S(1)}, f32[2,128,128]{2,1,0:T(8,128)S(1)}, u32[]{:S(2)}, u32[]{:S(2)}) %collective-permute-start.18) | collective-permute-done | bytes 131104 | tf_op jit(solution)/shard_map/ppermute | solution.py:414
  58.4 3.5 %all-to-all-start.1 = ((bf16[16,16,128]{2,1,0:T(8,128)(2,1)}), bf16[16,16,128]{2,1,0:T(8,128)(2,1)S(1)}, u32[]{:S(2)}, u32[]{:S(2)}) async-start(bf16[16,16,128]{2,1,0:T(8,128)(2,1)} %get-tuple-element.47), calls=%async_computation.1 | async-start | bytes 131072 | tf_op jit(solution)/shard_map/all_to_all | solution.py:417
  61.9 1.8 %collective-permute-start.15 = (bf16[2,64,128]{2,1,0:T(8,128)(2,1)S(1)}, bf16[2,64,128]{2,1,0:T(8,128)(2,1)S(1)}, u32[]{:S(2)}, u32[]{:S(2)}) collective-permute-start(bf16[2,64,128]{2,1,0:T(8,128)(2,1)S(1)} %get-tuple-element.50), channel_id=1, source_target_pairs={{0,2},{1,3},{2,0},{3,1},{4,6},{5,7},{6,4},{7,5},{8,10},{9,11},{10,... | collective-permute-start | bytes 98312 | tf_op jit(solution)/shard_map/ppermute | solution.py:414
  63.8 2.2 %collective-permute-done.15.adj_far = bf16[2,64,128]{2,1,0:T(8,128)(2,1)S(1)} collective-permute-done((bf16[2,64,128]{2,1,0:T(8,128)(2,1)S(1)}, bf16[2,64,128]{2,1,0:T(8,128)(2,1)S(1)}, u32[]{:S(2)}, u32[]{:S(2)}) %collective-permute-start.15) | collective-permute-done | bytes 32800 | tf_op jit(solution)/shard_map/ppermute | solution.py:414
  66.0 0.5 collective-permute-start.14
  66.5 0.8 %collective-permute-done.14.adj_near = bf16[64,128]{1,0:T(8,128)(2,1)S(1)} collective-permute-done((bf16[64,128]{1,0:T(8,128)(2,1)S(1)}, bf16[64,128]{1,0:T(8,128)(2,1)S(1)}, u32[]{:S(2)}, u32[]{:S(2)}) %collective-permute-start.14) | collective-permute-done | bytes 16416 | tf_op jit(solution)/shard_map/ppermute | solution.py:414
  67.3 0.6 shard_map.64.x
  67.9 0.9 %all-to-all-done.1.adjoint = bf16[16,16,128]{2,1,0:T(8,128)(2,1)S(1)} async-done(((bf16[16,16,128]{2,1,0:T(8,128)(2,1)}), bf16[16,16,128]{2,1,0:T(8,128)(2,1)S(1)}, u32[]{:S(2)}, u32[]{:S(2)}) %all-to-all-start.1) | async-done | bytes 65568 | tf_op jit(solution)/shard_map/all_to_all | solution.py:417
  68.8 1.3 %shard_map.65 = f32[2,512,256]{2,1,0:T(8,128)} custom-call(bf16[16,16,128]{2,1,0:T(8,128)(2,1)S(1)} %all-to-all-done.1.adjoint, f32[2,512,256]{2,1,0:T(8,128)S(1)} %shard_map.64.x, bf16[2,4,16,512]{3,2,1,0:T(8,128)(2,1)S(1)} %get-tuple-element.39.refs_5_.vfac), custom_call_target="tpu_custom_call" | custom-call | tf_op jit(solution)/shard_map/pallas_call | solution.py:391
  70.1 0.9 %shard_map.66 = f32[2,128,256]{2,1,0:T(8,128)} custom-call(f32[128,128]{1,0:T(8,128)S(1)} %get-tuple-element.51.misfit, f32[128,128]{1,0:T(8,128)S(1)} %collective-permute-done.17.near, f32[2,128,128]{2,1,0:T(8,128)S(1)} %collective-permute-done.18.far, f32[2,128,128]{2,1,0:T(8,128)S(1)} %collective-permute-done.19.far_near), custom_call_target="tpu_custom_call" | custom-call | tf_op jit(solution)/shard_map/pallas_call | solution.py:391
  (20 shorter events, 0.3 us)
Async XLA Ops:
  0.6 34.2 %collective-permute-start.6 = (f32[2,512,256]{2,1,0:T(8,128)}, f32[2,512,256]{2,1,0:T(8,128)S(1)}, u32[]{:S(2)}, u32[]{:S(2)}) collective-permute-start(f32[2,512,256]{2,1,0:T(8,128)} %x.1), channel_id=1, source_target_pairs={{0,1},{1,0},{2,3},{3,2},{4,5},{5,4},{6,7},{7,6},{8,9},{9,8},{10,11... | collective-permute-start | bytes 3145736 | tf_op jit(solution)/shard_map/ppermute | solution.py:414
  4.1 9.7 %collective-permute-start.1 = (bf16[512,256]{1,0:T(8,128)(2,1)S(1)}, bf16[512,256]{1,0:T(8,128)(2,1)S(1)}, u32[]{:S(2)}, u32[]{:S(2)}) collective-permute-start(bf16[512,256]{1,0:T(8,128)(2,1)S(1)} %get-tuple-element.32), channel_id=1, source_target_pairs={{0,2},{1,3},{2,0},{3,1},{4,6},{5,7},{6,4},{7,5},{8,10},{9,11},{10,... | collective-permute-start | bytes 786440 | tf_op jit(solution)/shard_map/ppermute | solution.py:414
  6.6 12.6 %collective-permute-start.9 = (bf16[512,256]{1,0:T(8,128)(2,1)S(1)}, bf16[512,256]{1,0:T(8,128)(2,1)S(1)}, u32[]{:S(2)}, u32[]{:S(2)}) collective-permute-start(bf16[512,256]{1,0:T(8,128)(2,1)S(1)} %get-tuple-element.42), channel_id=1, source_target_pairs={{0,2},{1,3},{2,0},{3,1},{4,6},{5,7},{6,4},{7,5},{8,10},{9,11},{10,... | collective-permute-start | bytes 786440 | tf_op jit(solution)/shard_map/ppermute | solution.py:414
  6.6 19.3 %collective-permute-start = (bf16[384,256]{1,0:T(8,128)(2,1)}, bf16[384,256]{1,0:T(8,128)(2,1)S(1)}, u32[]{:S(2)}, u32[]{:S(2)}) collective-permute-start(bf16[384,256]{1,0:T(8,128)(2,1)} %get-tuple-element.31), channel_id=1, source_target_pairs={{0,1},{1,0},{2,3},{3,2},{4,5},{5,4},{6,7},{7,6},{8,9},{9,8},{10,11... | collective-permute-start | bytes 589832 | tf_op jit(solution)/shard_map/ppermute | solution.py:414
  13.8 19.1 %collective-permute-start.2 = (bf16[512,256]{1,0:T(8,128)(2,1)S(1)}, bf16[512,256]{1,0:T(8,128)(2,1)S(1)}, u32[]{:S(2)}, u32[]{:S(2)}) collective-permute-start(bf16[512,256]{1,0:T(8,128)(2,1)S(1)} %collective-permute-done.1.far.refs_7_), channel_id=1, source_target_pairs={{0,1},{1,0},{2,3},{3,2},{4,5},{5,4},{6,7},{7,6},{8,9},{9,8},{10,11... | collective-permute-start | bytes 786440 | tf_op jit(solution)/shard_map/ppermute | solution.py:414
  19.2 19.3 %collective-permute-start.10 = (bf16[512,256]{1,0:T(8,128)(2,1)S(1)}, bf16[512,256]{1,0:T(8,128)(2,1)}, u32[]{:S(2)}, u32[]{:S(2)}) collective-permute-start(bf16[512,256]{1,0:T(8,128)(2,1)S(1)} %collective-permute-done.9.refs_9_), channel_id=1, source_target_pairs={{0,1},{1,0},{2,3},{3,2},{4,5},{5,4},{6,7},{7,6},{8,9},{9,8},{10,11... | collective-permute-start | bytes 786440 | tf_op jit(solution)/shard_map/ppermute | solution.py:414
  19.2 14.6 %collective-permute-start.8 = (bf16[512,128]{1,0:T(8,128)(2,1)}, bf16[512,128]{1,0:T(8,128)(2,1)}, u32[]{:S(2)}, u32[]{:S(2)}) collective-permute-start(bf16[512,128]{1,0:T(8,128)(2,1)} %get-tuple-element.41), channel_id=1, source_target_pairs={{0,2},{1,3},{2,0},{3,1},{4,6},{5,7},{6,4},{7,5},{8,10},{9,11},{10,... | collective-permute-start | bytes 393224 | tf_op jit(solution)/shard_map/ppermute | solution.py:414
  20.9 11.9 %all-to-all-start = ((bf16[16,16,128]{2,1,0:T(8,128)(2,1)}), bf16[16,16,128]{2,1,0:T(8,128)(2,1)S(1)}, u32[]{:S(2)}, u32[]{:S(2)}) async-start(bf16[16,16,128]{2,1,0:T(8,128)(2,1)} %get-tuple-element.28), calls=%async_computation | async-start | bytes 131072 | tf_op jit(solution)/shard_map/all_to_all | solution.py:417
  25.9 12.5 %collective-permute-start.7 = (bf16[2,4,16,512]{3,2,1,0:T(8,128)(2,1)S(1)}, bf16[2,4,16,512]{3,2,1,0:T(8,128)(2,1)}, u32[]{:S(2)}, u32[]{:S(2)}) collective-permute-start(bf16[2,4,16,512]{3,2,1,0:T(8,128)(2,1)S(1)} %get-tuple-element.39.refs_5_.vfac), channel_id=1, source_target_pairs={{0,1},{1,0},{2,3},{3,2},{4,5},{5,4},{6,7},{7,6},{8,9},{9,8},{10,11... | collective-permute-start | bytes 393224 | tf_op jit(solution)/shard_map/ppermute | solution.py:414
  33.6 4.8 %collective-permute-start.3 = (bf16[4,16,128]{2,1,0:T(8,128)(2,1)S(1)}, bf16[4,16,128]{2,1,0:T(8,128)(2,1)S(1)}, u32[]{:S(2)}, u32[]{:S(2)}) collective-permute-start(bf16[4,16,128]{2,1,0:T(8,128)(2,1)S(1)} %get-tuple-element.34), channel_id=1, source_target_pairs={{0,4},{1,5},{2,6},{3,7},{4,0},{5,1},{6,2},{7,3},{8,12},{9,13},{10,... | collective-permute-start | bytes 49160 | tf_op jit(solution)/shard_map/ppermute | solution.py:414
  33.8 4.6 %collective-permute-start.4 = (bf16[4,16,128]{2,1,0:T(8,128)(2,1)S(1)}, bf16[4,16,128]{2,1,0:T(8,128)(2,1)S(1)}, u32[]{:S(2)}, u32[]{:S(2)}) collective-permute-start(bf16[4,16,128]{2,1,0:T(8,128)(2,1)S(1)} %get-tuple-element.35), channel_id=1, source_target_pairs={{0,8},{1,9},{2,10},{3,11},{4,12},{5,13},{6,14},{7,15},{8,0},{9,1},... | collective-permute-start | bytes 49160 | tf_op jit(solution)/shard_map/ppermute | solution.py:414
  34.8 5.5 %collective-permute-start.5 = (bf16[4,16,128]{2,1,0:T(8,128)(2,1)S(1)}, bf16[4,16,128]{2,1,0:T(8,128)(2,1)S(1)}, u32[]{:S(2)}, u32[]{:S(2)}) collective-permute-start(bf16[4,16,128]{2,1,0:T(8,128)(2,1)S(1)} %get-tuple-element.36), channel_id=1, source_target_pairs={{0,12},{1,13},{2,14},{3,15},{4,8},{5,9},{6,10},{7,11},{8,4},{9,5},... | collective-permute-start | bytes 49160 | tf_op jit(solution)/shard_map/ppermute | solution.py:414
  42.6 4.5 %collective-permute-start.11 = (bf16[4,16,128]{2,1,0:T(8,128)(2,1)S(1)}, bf16[4,16,128]{2,1,0:T(8,128)(2,1)S(1)}, u32[]{:S(2)}, u32[]{:S(2)}) collective-permute-start(bf16[4,16,128]{2,1,0:T(8,128)(2,1)S(1)} %get-tuple-element.44), channel_id=1, source_target_pairs={{0,4},{1,5},{2,6},{3,7},{4,0},{5,1},{6,2},{7,3},{8,12},{9,13},{10,... | collective-permute-start | bytes 49160 | tf_op jit(solution)/shard_map/ppermute | solution.py:414
  42.7 5.5 %collective-permute-start.12 = (bf16[4,16,128]{2,1,0:T(8,128)(2,1)S(1)}, bf16[4,16,128]{2,1,0:T(8,128)(2,1)S(1)}, u32[]{:S(2)}, u32[]{:S(2)}) collective-permute-start(bf16[4,16,128]{2,1,0:T(8,128)(2,1)S(1)} %get-tuple-element.45), channel_id=1, source_target_pairs={{0,8},{1,9},{2,10},{3,11},{4,12},{5,13},{6,14},{7,15},{8,0},{9,1},... | collective-permute-start | bytes 49160 | tf_op jit(solution)/shard_map/ppermute | solution.py:414
  46.5 5.5 %collective-permute-start.13 = (bf16[4,16,128]{2,1,0:T(8,128)(2,1)S(1)}, bf16[4,16,128]{2,1,0:T(8,128)(2,1)S(1)}, u32[]{:S(2)}, u32[]{:S(2)}) collective-permute-start(bf16[4,16,128]{2,1,0:T(8,128)(2,1)S(1)} %get-tuple-element.46), channel_id=1, source_target_pairs={{0,12},{1,13},{2,14},{3,15},{4,8},{5,9},{6,10},{7,11},{8,4},{9,5},... | collective-permute-start | bytes 49160 | tf_op jit(solution)/shard_map/ppermute | solution.py:414
  53.5 5.0 %collective-permute-start.18 = (f32[2,128,128]{2,1,0:T(8,128)S(1)}, f32[2,128,128]{2,1,0:T(8,128)S(1)}, u32[]{:S(2)}, u32[]{:S(2)}) collective-permute-start(f32[2,128,128]{2,1,0:T(8,128)S(1)} %get-tuple-element.53), channel_id=1, source_target_pairs={{0,2},{1,3},{2,0},{3,1},{4,6},{5,7},{6,4},{7,5},{8,10},{9,11},{10,... | collective-permute-start | bytes 393224 | tf_op jit(solution)/shard_map/ppermute | solution.py:414
  58.4 11.7 %collective-permute-start.19 = (f32[2,128,128]{2,1,0:T(8,128)S(1)}, f32[2,128,128]{2,1,0:T(8,128)S(1)}, u32[]{:S(2)}, u32[]{:S(2)}) collective-permute-start(f32[2,128,128]{2,1,0:T(8,128)S(1)} %collective-permute-done.18.far), channel_id=1, source_target_pairs={{0,1},{1,0},{2,3},{3,2},{4,5},{5,4},{6,7},{7,6},{8,9},{9,8},{10,11... | collective-permute-start | bytes 393224 | tf_op jit(solution)/shard_map/ppermute | solution.py:414
  58.4 10.4 %all-to-all-start.1 = ((bf16[16,16,128]{2,1,0:T(8,128)(2,1)}), bf16[16,16,128]{2,1,0:T(8,128)(2,1)S(1)}, u32[]{:S(2)}, u32[]{:S(2)}) async-start(bf16[16,16,128]{2,1,0:T(8,128)(2,1)} %get-tuple-element.47), calls=%async_computation.1 | async-start | bytes 131072 | tf_op jit(solution)/shard_map/all_to_all | solution.py:417
  61.9 4.0 %collective-permute-start.15 = (bf16[2,64,128]{2,1,0:T(8,128)(2,1)S(1)}, bf16[2,64,128]{2,1,0:T(8,128)(2,1)S(1)}, u32[]{:S(2)}, u32[]{:S(2)}) collective-permute-start(bf16[2,64,128]{2,1,0:T(8,128)(2,1)S(1)} %get-tuple-element.50), channel_id=1, source_target_pairs={{0,2},{1,3},{2,0},{3,1},{4,6},{5,7},{6,4},{7,5},{8,10},{9,11},{10,... | collective-permute-start | bytes 98312 | tf_op jit(solution)/shard_map/ppermute | solution.py:414
  63.8 6.3 %collective-permute-start.17 = (f32[128,128]{1,0:T(8,128)S(1)}, f32[128,128]{1,0:T(8,128)S(1)}, u32[]{:S(2)}, u32[]{:S(2)}) collective-permute-start(f32[128,128]{1,0:T(8,128)S(1)} %get-tuple-element.52), channel_id=1, source_target_pairs={{0,1},{1,0},{2,3},{3,2},{4,5},{5,4},{6,7},{7,6},{8,9},{9,8},{10,11... | collective-permute-start | bytes 196616 | tf_op jit(solution)/shard_map/ppermute | solution.py:414
  66.0 1.4 %collective-permute-start.16 = (bf16[2,64,128]{2,1,0:T(8,128)(2,1)S(1)}, bf16[2,64,128]{2,1,0:T(8,128)(2,1)S(1)}, u32[]{:S(2)}, u32[]{:S(2)}) collective-permute-start(bf16[2,64,128]{2,1,0:T(8,128)(2,1)S(1)} %collective-permute-done.15.adj_far), channel_id=1, source_target_pairs={{0,1},{1,0},{2,3},{3,2},{4,5},{5,4},{6,7},{7,6},{8,9},{9,8},{10,11... | collective-permute-start | bytes 98312 | tf_op jit(solution)/shard_map/ppermute | solution.py:414
  66.0 1.3 %collective-permute-start.14 = (bf16[64,128]{1,0:T(8,128)(2,1)S(1)}, bf16[64,128]{1,0:T(8,128)(2,1)S(1)}, u32[]{:S(2)}, u32[]{:S(2)}) collective-permute-start(bf16[64,128]{1,0:T(8,128)(2,1)S(1)} %get-tuple-element.49), channel_id=1, source_target_pairs={{0,1},{1,0},{2,3},{3,2},{4,5},{5,4},{6,7},{7,6},{8,9},{9,8},{10,11... | collective-permute-start | bytes 49160 | tf_op jit(solution)/shard_map/ppermute | solution.py:414

commit v6 on v4

--- a/solution.py
+++ b/solution.py
@@ -373,7 +373,7 @@
     )
 
 
-def call(kernel, out_shape, *args, from_hbm=False, **static):
+def call(kernel, out_shape, *args, from_hbm=False, aliases=None, **static):
     on_chip = pl.BlockSpec(memory_space=pltpu.VMEM)
     off_chip = pl.BlockSpec(memory_space=pltpu.HBM)
     space = pltpu.HBM if from_hbm else pltpu.VMEM
@@ -387,6 +387,7 @@
         out_shape=out_shape,
         in_specs=[off_chip if from_hbm else on_chip] * len(args),
         out_specs=tuple(map(spec, out_shape)) if many else spec(out_shape),
+        input_output_aliases=aliases or {},
         compiler_params=pltpu.CompilerParams(vmem_limit_bytes=VMEM_LIMIT),
     )(*(pltpu.with_memory_space_constraint(arg, space) for arg in args))
 
@@ -472,7 +473,7 @@
         row = call(row_last_kernel, row_outs, *pieces, *gathered, **counted)
         estimate = call(
             own_column_kernel, shape(x_init.shape, f32),
-            adj_own, adj_near, adj_far, adj_corner, estimate, vfac, **static,
+            adj_own, adj_near, adj_far, adj_corner, estimate, vfac, aliases={4: 0}, **static,
         )
     else:
         (pieces,) = call(row_kernel, (chunks,), received, *gathered, width=width)

time: 68.9 us -> 68.9 us (level)
  no operation moved by 1% of the time
where the time goes in v6:
time: 68.9 us; the launch traced here: 68.6 us
  waiting for transfers between devices  27.2 us (39%)
  starting transfers between devices  20.5 us (30%)
  blocking collectives  11.7 us (17%)
  Pallas kernels  8.57 us (12%)
  between operations  0.7 us (1%)
    ppermute x20, waiting for transfers between devices, exchange(): return lax.ppermute(value, 'tile', [(s, s ^ bit) for s in range(tiles)])  26.5 us
    ppermute x20, starting transfers between devices, exchange(): return lax.ppermute(value, 'tile', [(s, s ^ bit) for s in range(tiles)])  17 us
    all_to_all x1, blocking collectives, spread(): lax.all_to_all(value, 'tile', split_axis=0, concat_axis=0, tiled=True)  11.7 us
    pallas_call x7, Pallas kernels, call(): pl.pallas_call(functools.partial(kernel, **static), out_shape=out_shape,...  8.57 us
    all_to_all x1, starting transfers between devices, spread(): lax.all_to_all(value, 'tile', split_axis=0, concat_axis=0, tiled=True)  3.5 us
  transfers between devices with their start and end apart: 21, of which 10 were waited for; matrix products, arithmetic and copies ran while one was open for 0% of the time, Pallas kernels for 4%

profile of v6, /device:TPU:0, one launch (start us, length us, event | category | flops | bytes accessed | tf_op | source)
XLA Modules:
  0.0 68.6 jit_solution(14683967793832061377)
XLA Ops:
  0.6 2.3 %shard_map.59 = (bf16[16,16,128]{2,1,0:T(8,128)(2,1)S(1)}, bf16[512,256]{1,0:T(8,128)(2,1)S(1)}, bf16[384,256]{1,0:T(8,128)(2,1)S(1)}, f32[128,128]{1,0:T(8,128)...) custom-call(f32[2,128,256]{2,1,0:T(8,128)} %data.1, ...), custom_call_target="tpu_custom_call" | custom-call | tf_op jit(solution)/shard_map/pallas_call | solution.py:385
  2.9 3.1 %collective-permute-start.1 = (bf16[512,256]{1,0:T(8,128)(2,1)S(1)}, bf16[512,256]{1,0:T(8,128)(2,1)S(1)}, u32[]{:S(2)}, u32[]{:S(2)}) collective-permute-start(bf16[512,256]{1,0:T(8,128)(2,1)S(1)} %get-tuple-element.32), channel_id=1, source_target_pairs={{0,2},{1,3},{2,0},{3,1},{4,6},{5,7},{6,4},{7,5},{8,10},{9,11},{10,... | collective-permute-start | bytes 786440 | tf_op jit(solution)/shard_map/ppermute | solution.py:409
  6.0 0.1 collective-permute-start.9
  6.1 7.1 %collective-permute-done.1.far.refs_7_ = bf16[512,256]{1,0:T(8,128)(2,1)S(1)} collective-permute-done((bf16[512,256]{1,0:T(8,128)(2,1)S(1)}, bf16[512,256]{1,0:T(8,128)(2,1)S(1)}, u32[]{:S(2)}, u32[]{:S(2)}) %collective-permute-start.1) | collective-permute-done | bytes 262176 | tf_op jit(solution)/shard_map/ppermute | solution.py:409
  13.1 0.5 collective-permute-start.6
  13.6 4.3 %collective-permute-done.9.refs_9_ = bf16[512,256]{1,0:T(8,128)(2,1)S(1)} collective-permute-done((bf16[512,256]{1,0:T(8,128)(2,1)S(1)}, bf16[512,256]{1,0:T(8,128)(2,1)S(1)}, u32[]{:S(2)}, u32[]{:S(2)}) %collective-permute-start.9) | collective-permute-done | bytes 262176 | tf_op jit(solution)/shard_map/ppermute | solution.py:409
  17.9 1.7 %collective-permute-start.8 = (bf16[512,128]{1,0:T(8,128)(2,1)S(1)}, bf16[512,128]{1,0:T(8,128)(2,1)S(1)}, u32[]{:S(2)}, u32[]{:S(2)}) collective-permute-start(bf16[512,128]{1,0:T(8,128)(2,1)S(1)} %get-tuple-element.40), channel_id=1, source_target_pairs={{0,2},{1,3},{2,0},{3,1},{4,6},{5,7},{6,4},{7,5},{8,10},{9,11},{10,... | collective-permute-start | bytes 393224 | tf_op jit(solution)/shard_map/ppermute | solution.py:409
  19.6 0.2 collective-permute-start.7
  19.9 11.7 %all_to_all.10.coeffs = bf16[16,16,128]{2,1,0:T(8,128)(2,1)S(1)} all-to-all(bf16[16,16,128]{2,1,0:T(8,128)(2,1)S(1)} %get-tuple-element.28), channel_id=1, replica_groups=mesh['freq'=2,'tile'=16] {'tile'}, dimensions={0} | all-to-all | bytes 131072 | tf_op jit(solution)/shard_map/all_to_all | solution.py:412
  31.5 0.8 %shard_map.60 = (bf16[4,16,128]{2,1,0:T(8,128)(2,1)S(1)}, bf16[4,16,128]{2,1,0:T(8,128)(2,1)S(1)}, bf16[4,16,128]{2,1,0:T(8,128)(2,1)S(1)}, bf16[4,16,128]{2,1,0:T(8,128)(2,1)S(1)}) custom-call(bf16[16,16,128]{2,1,0:T(8,128)(2,1)S(1)} %all_to_all.10.coeffs, f32[128,128]{1,0:T(8,128)S(1)} %get-tuple-element.29.own.refs_4_, ...), custom_call_target="tpu_custom_call" | custom-call | tf_op jit(solution)/shard_map/pallas_call | solution.py:385
  32.4 0.2 collective-permute-start.3
  32.5 1.0 %collective-permute-start.4 = (bf16[4,16,128]{2,1,0:T(8,128)(2,1)S(1)}, bf16[4,16,128]{2,1,0:T(8,128)(2,1)S(1)}, u32[]{:S(2)}, u32[]{:S(2)}) collective-permute-start(bf16[4,16,128]{2,1,0:T(8,128)(2,1)S(1)} %get-tuple-element.35), channel_id=1, source_target_pairs={{0,8},{1,9},{2,10},{3,11},{4,12},{5,13},{6,14},{7,15},{8,0},{9,1},... | collective-permute-start | bytes 49160 | tf_op jit(solution)/shard_map/ppermute | solution.py:409
  33.5 3.3 %collective-permute-start.5 = (bf16[4,16,128]{2,1,0:T(8,128)(2,1)S(1)}, bf16[4,16,128]{2,1,0:T(8,128)(2,1)S(1)}, u32[]{:S(2)}, u32[]{:S(2)}) collective-permute-start(bf16[4,16,128]{2,1,0:T(8,128)(2,1)S(1)} %get-tuple-element.36), channel_id=1, source_target_pairs={{0,12},{1,13},{2,14},{3,15},{4,8},{5,9},{6,10},{7,11},{8,4},{9,5},... | collective-permute-start | bytes 49160 | tf_op jit(solution)/shard_map/ppermute | solution.py:409
  36.8 0.4 collective-permute-done.4.refs_2_
  37.2 1.9 %collective-permute-done.5.refs_3_ = bf16[4,16,128]{2,1,0:T(8,128)(2,1)S(1)} collective-permute-done((bf16[4,16,128]{2,1,0:T(8,128)(2,1)S(1)}, bf16[4,16,128]{2,1,0:T(8,128)(2,1)S(1)}, u32[]{:S(2)}, u32[]{:S(2)}) %collective-permute-start.5) | collective-permute-done | bytes 16416 | tf_op jit(solution)/shard_map/ppermute | solution.py:409
  39.1 1.2 %shard_map.61 = (bf16[4,16,128]{2,1,0:T(8,128)(2,1)S(1)}, bf16[4,16,128]{2,1,0:T(8,128)(2,1)S(1)}, bf16[4,16,128]{2,1,0:T(8,128)(2,1)S(1)}, bf16[4,16,128]{2,1,0...) custom-call(bf16[4,16,128]{2,1,0:T(8,128)(2,1)S(1)} %get-tuple-element, ...), custom_call_target="tpu_custom_call" | custom-call | tf_op jit(solution)/shard_map/pallas_call | solution.py:385
  40.3 3.8 %collective-permute-start.12 = (bf16[4,16,128]{2,1,0:T(8,128)(2,1)S(1)}, bf16[4,16,128]{2,1,0:T(8,128)(2,1)S(1)}, u32[]{:S(2)}, u32[]{:S(2)}) collective-permute-start(bf16[4,16,128]{2,1,0:T(8,128)(2,1)S(1)} %get-tuple-element.44), channel_id=1, source_target_pairs={{0,8},{1,9},{2,10},{3,11},{4,12},{5,13},{6,14},{7,15},{8,0},{9,1},... | collective-permute-start | bytes 49160 | tf_op jit(solution)/shard_map/ppermute | solution.py:409
  44.2 0.6 collective-permute-start.13
  44.7 1.2 %collective-permute-done.12.refs_2_ = bf16[4,16,128]{2,1,0:T(8,128)(2,1)S(1)} collective-permute-done((bf16[4,16,128]{2,1,0:T(8,128)(2,1)S(1)}, bf16[4,16,128]{2,1,0:T(8,128)(2,1)S(1)}, u32[]{:S(2)}, u32[]{:S(2)}) %collective-permute-start.12) | collective-permute-done | bytes 16416 | tf_op jit(solution)/shard_map/ppermute | solution.py:409
  45.9 3.8 %collective-permute-done.13.refs_3_ = bf16[4,16,128]{2,1,0:T(8,128)(2,1)S(1)} collective-permute-done((bf16[4,16,128]{2,1,0:T(8,128)(2,1)S(1)}, bf16[4,16,128]{2,1,0:T(8,128)(2,1)S(1)}, u32[]{:S(2)}, u32[]{:S(2)}) %collective-permute-start.13) | collective-permute-done | bytes 16416 | tf_op jit(solution)/shard_map/ppermute | solution.py:409
  49.7 1.4 %shard_map.62 = (bf16[16,16,128]{2,1,0:T(8,128)(2,1)}, f32[128,128]{1,0:T(8,128)S(1)}, f32[128,128]{1,0:T(8,128)S(1)}, f32[2,128,128]{2,1,0:T(8,128)S(1)}) custom-call(bf16[4,16,128]{2,1,0:T(8,128)(2,1)S(1)} %get-tuple-element.42.refs_0_, bf16[4,16,128]{2,1,0:T(8,128)(2,1)S(1)} %collective-permute-done.11.refs_1_, ...), custom_call_target="tpu_custom_call" | custom-call | tf_op jit(solution)/shard_map/pallas_call | solution.py:385
  51.1 0.1 collective-permute-start.18
  51.2 4.8 %collective-permute-done.18.far = f32[2,128,128]{2,1,0:T(8,128)S(1)} collective-permute-done((f32[2,128,128]{2,1,0:T(8,128)S(1)}, f32[2,128,128]{2,1,0:T(8,128)S(1)}, u32[]{:S(2)}, u32[]{:S(2)}) %collective-permute-start.18) | collective-permute-done | bytes 131104 | tf_op jit(solution)/shard_map/ppermute | solution.py:409
  56.1 3.5 %all-to-all-start.1 = ((bf16[16,16,128]{2,1,0:T(8,128)(2,1)}), bf16[16,16,128]{2,1,0:T(8,128)(2,1)S(1)}, u32[]{:S(2)}, u32[]{:S(2)}) async-start(bf16[16,16,128]{2,1,0:T(8,128)(2,1)} %get-tuple-element.46), calls=%async_computation.1 | async-start | bytes 131072 | tf_op jit(solution)/shard_map/all_to_all | solution.py:412
  59.6 1.8 %collective-permute-start.15 = (bf16[2,64,128]{2,1,0:T(8,128)(2,1)S(1)}, bf16[2,64,128]{2,1,0:T(8,128)(2,1)S(1)}, u32[]{:S(2)}, u32[]{:S(2)}) collective-permute-start(bf16[2,64,128]{2,1,0:T(8,128)(2,1)S(1)} %get-tuple-element.49), channel_id=1, source_target_pairs={{0,2},{1,3},{2,0},{3,1},{4,6},{5,7},{6,4},{7,5},{8,10},{9,11},{10,... | collective-permute-start | bytes 98312 | tf_op jit(solution)/shard_map/ppermute | solution.py:409
  61.4 2.2 %collective-permute-done.15.adj_far = bf16[2,64,128]{2,1,0:T(8,128)(2,1)S(1)} collective-permute-done((bf16[2,64,128]{2,1,0:T(8,128)(2,1)S(1)}, bf16[2,64,128]{2,1,0:T(8,128)(2,1)S(1)}, u32[]{:S(2)}, u32[]{:S(2)}) %collective-permute-start.15) | collective-permute-done | bytes 32800 | tf_op jit(solution)/shard_map/ppermute | solution.py:409
  63.6 0.5 collective-permute-start.14
  64.1 0.8 %collective-permute-done.14.adj_near = bf16[64,128]{1,0:T(8,128)(2,1)S(1)} collective-permute-done((bf16[64,128]{1,0:T(8,128)(2,1)S(1)}, bf16[64,128]{1,0:T(8,128)(2,1)S(1)}, u32[]{:S(2)}, u32[]{:S(2)}) %collective-permute-start.14) | collective-permute-done | bytes 16416 | tf_op jit(solution)/shard_map/ppermute | solution.py:409
  65.0 0.8 %shard_map.63.x = f32[2,512,256]{2,1,0:T(8,128)S(1)} custom-call(bf16[64,128]{1,0:T(8,128)(2,1)S(1)} %get-tuple-element.47.adj_own, bf16[64,128]{1,0:T(8,128)(2,1)S(1)} %collective-permute-done.14.adj_near, bf16[2,64,128]{2,1,0:T(8,128)(2,1)S(1)} %collective-permute-done.15.adj_far, ...), custom_call_target="tpu_custom_call", output_to_operand_aliasing={{}: (4, {})} | custom-call | tf_op jit(solution)/shard_map/pallas_call | solution.py:385
  65.7 0.7 %all-to-all-done.1.adjoint = bf16[16,16,128]{2,1,0:T(8,128)(2,1)S(1)} async-done(((bf16[16,16,128]{2,1,0:T(8,128)(2,1)}), bf16[16,16,128]{2,1,0:T(8,128)(2,1)S(1)}, u32[]{:S(2)}, u32[]{:S(2)}) %all-to-all-start.1) | async-done | bytes 65568 | tf_op jit(solution)/shard_map/all_to_all | solution.py:412
  66.5 1.3 %shard_map.64 = f32[2,512,256]{2,1,0:T(8,128)} custom-call(bf16[16,16,128]{2,1,0:T(8,128)(2,1)S(1)} %all-to-all-done.1.adjoint, f32[2,512,256]{2,1,0:T(8,128)S(1)} %shard_map.63.x, bf16[2,4,16,512]{3,2,1,0:T(8,128)(2,1)S(1)} %get-tuple-element.38.refs_5_.vfac), custom_call_target="tpu_custom_call" | custom-call | tf_op jit(solution)/shard_map/pallas_call | solution.py:385
  67.8 0.9 %shard_map.65 = f32[2,128,256]{2,1,0:T(8,128)} custom-call(f32[128,128]{1,0:T(8,128)S(1)} %get-tuple-element.51.misfit, f32[128,128]{1,0:T(8,128)S(1)} %collective-permute-done.17.near, f32[2,128,128]{2,1,0:T(8,128)S(1)} %collective-permute-done.18.far, f32[2,128,128]{2,1,0:T(8,128)S(1)} %collective-permute-done.19.far_near), custom_call_target="tpu_custom_call" | custom-call | tf_op jit(solution)/shard_map/pallas_call | solution.py:385
  (18 shorter events, 0.1 us)
Async XLA Ops:
  2.9 10.2 %collective-permute-start.1 = (bf16[512,256]{1,0:T(8,128)(2,1)S(1)}, bf16[512,256]{1,0:T(8,128)(2,1)S(1)}, u32[]{:S(2)}, u32[]{:S(2)}) collective-permute-start(bf16[512,256]{1,0:T(8,128)(2,1)S(1)} %get-tuple-element.32), channel_id=1, source_target_pairs={{0,2},{1,3},{2,0},{3,1},{4,6},{5,7},{6,4},{7,5},{8,10},{9,11},{10,... | collective-permute-start | bytes 786440 | tf_op jit(solution)/shard_map/ppermute | solution.py:409
  6.0 11.9 %collective-permute-start.9 = (bf16[512,256]{1,0:T(8,128)(2,1)S(1)}, bf16[512,256]{1,0:T(8,128)(2,1)S(1)}, u32[]{:S(2)}, u32[]{:S(2)}) collective-permute-start(bf16[512,256]{1,0:T(8,128)(2,1)S(1)} %get-tuple-element.41), channel_id=1, source_target_pairs={{0,2},{1,3},{2,0},{3,1},{4,6},{5,7},{6,4},{7,5},{8,10},{9,11},{10,... | collective-permute-start | bytes 786440 | tf_op jit(solution)/shard_map/ppermute | solution.py:409
  6.1 13.6 %collective-permute-start = (bf16[384,256]{1,0:T(8,128)(2,1)S(1)}, bf16[384,256]{1,0:T(8,128)(2,1)S(1)}, u32[]{:S(2)}, u32[]{:S(2)}) collective-permute-start(bf16[384,256]{1,0:T(8,128)(2,1)S(1)} %get-tuple-element.31), channel_id=1, source_target_pairs={{0,1},{1,0},{2,3},{3,2},{4,5},{5,4},{6,7},{7,6},{8,9},{9,8},{10,11... | collective-permute-start | bytes 589832 | tf_op jit(solution)/shard_map/ppermute | solution.py:409
  13.1 18.4 %collective-permute-start.2 = (bf16[512,256]{1,0:T(8,128)(2,1)S(1)}, bf16[512,256]{1,0:T(8,128)(2,1)S(1)}, u32[]{:S(2)}, u32[]{:S(2)}) collective-permute-start(bf16[512,256]{1,0:T(8,128)(2,1)S(1)} %collective-permute-done.1.far.refs_7_), channel_id=1, source_target_pairs={{0,1},{1,0},{2,3},{3,2},{4,5},{5,4},{6,7},{7,6},{8,9},{9,8},{10,11... | collective-permute-start | bytes 786440 | tf_op jit(solution)/shard_map/ppermute | solution.py:409
  13.1 23.7 %collective-permute-start.6 = (bf16[512,256]{1,0:T(8,128)(2,1)S(1)}, bf16[512,256]{1,0:T(8,128)(2,1)S(1)}, u32[]{:S(2)}, u32[]{:S(2)}) collective-permute-start(bf16[512,256]{1,0:T(8,128)(2,1)S(1)} %get-tuple-element.39), channel_id=1, source_target_pairs={{0,1},{1,0},{2,3},{3,2},{4,5},{5,4},{6,7},{7,6},{8,9},{9,8},{10,11... | collective-permute-start | bytes 786440 | tf_op jit(solution)/shard_map/ppermute | solution.py:409
  17.9 18.9 %collective-permute-start.10 = (bf16[512,256]{1,0:T(8,128)(2,1)S(1)}, bf16[512,256]{1,0:T(8,128)(2,1)S(1)}, u32[]{:S(2)}, u32[]{:S(2)}) collective-permute-start(bf16[512,256]{1,0:T(8,128)(2,1)S(1)} %collective-permute-done.9.refs_9_), channel_id=1, source_target_pairs={{0,1},{1,0},{2,3},{3,2},{4,5},{5,4},{6,7},{7,6},{8,9},{9,8},{10,11... | collective-permute-start | bytes 786440 | tf_op jit(solution)/shard_map/ppermute | solution.py:409
  17.9 14.6 %collective-permute-start.8 = (bf16[512,128]{1,0:T(8,128)(2,1)S(1)}, bf16[512,128]{1,0:T(8,128)(2,1)S(1)}, u32[]{:S(2)}, u32[]{:S(2)}) collective-permute-start(bf16[512,128]{1,0:T(8,128)(2,1)S(1)} %get-tuple-element.40), channel_id=1, source_target_pairs={{0,2},{1,3},{2,0},{3,1},{4,6},{5,7},{6,4},{7,5},{8,10},{9,11},{10,... | collective-permute-start | bytes 393224 | tf_op jit(solution)/shard_map/ppermute | solution.py:409
  19.6 13.9 %collective-permute-start.7 = (bf16[2,4,16,512]{3,2,1,0:T(8,128)(2,1)S(1)}, bf16[2,4,16,512]{3,2,1,0:T(8,128)(2,1)S(1)}, u32[]{:S(2)}, u32[]{:S(2)}) collective-permute-start(bf16[2,4,16,512]{3,2,1,0:T(8,128)(2,1)S(1)} %get-tuple-element.38.refs_5_.vfac), channel_id=1, source_target_pairs={{0,1},{1,0},{2,3},{3,2},{4,5},{5,4},{6,7},{7,6},{8,9},{9,8},{10,11... | collective-permute-start | bytes 393224 | tf_op jit(solution)/shard_map/ppermute | solution.py:409
  32.4 4.5 %collective-permute-start.3 = (bf16[4,16,128]{2,1,0:T(8,128)(2,1)S(1)}, bf16[4,16,128]{2,1,0:T(8,128)(2,1)S(1)}, u32[]{:S(2)}, u32[]{:S(2)}) collective-permute-start(bf16[4,16,128]{2,1,0:T(8,128)(2,1)S(1)} %get-tuple-element.34), channel_id=1, source_target_pairs={{0,4},{1,5},{2,6},{3,7},{4,0},{5,1},{6,2},{7,3},{8,12},{9,13},{10,... | collective-permute-start | bytes 49160 | tf_op jit(solution)/shard_map/ppermute | solution.py:409
  32.5 4.6 %collective-permute-start.4 = (bf16[4,16,128]{2,1,0:T(8,128)(2,1)S(1)}, bf16[4,16,128]{2,1,0:T(8,128)(2,1)S(1)}, u32[]{:S(2)}, u32[]{:S(2)}) collective-permute-start(bf16[4,16,128]{2,1,0:T(8,128)(2,1)S(1)} %get-tuple-element.35), channel_id=1, source_target_pairs={{0,8},{1,9},{2,10},{3,11},{4,12},{5,13},{6,14},{7,15},{8,0},{9,1},... | collective-permute-start | bytes 49160 | tf_op jit(solution)/shard_map/ppermute | solution.py:409
  33.5 5.5 %collective-permute-start.5 = (bf16[4,16,128]{2,1,0:T(8,128)(2,1)S(1)}, bf16[4,16,128]{2,1,0:T(8,128)(2,1)S(1)}, u32[]{:S(2)}, u32[]{:S(2)}) collective-permute-start(bf16[4,16,128]{2,1,0:T(8,128)(2,1)S(1)} %get-tuple-element.36), channel_id=1, source_target_pairs={{0,12},{1,13},{2,14},{3,15},{4,8},{5,9},{6,10},{7,11},{8,4},{9,5},... | collective-permute-start | bytes 49160 | tf_op jit(solution)/shard_map/ppermute | solution.py:409
  40.3 4.5 %collective-permute-start.11 = (bf16[4,16,128]{2,1,0:T(8,128)(2,1)S(1)}, bf16[4,16,128]{2,1,0:T(8,128)(2,1)S(1)}, u32[]{:S(2)}, u32[]{:S(2)}) collective-permute-start(bf16[4,16,128]{2,1,0:T(8,128)(2,1)S(1)} %get-tuple-element.43), channel_id=1, source_target_pairs={{0,4},{1,5},{2,6},{3,7},{4,0},{5,1},{6,2},{7,3},{8,12},{9,13},{10,... | collective-permute-start | bytes 49160 | tf_op jit(solution)/shard_map/ppermute | solution.py:409
  40.3 5.5 %collective-permute-start.12 = (bf16[4,16,128]{2,1,0:T(8,128)(2,1)S(1)}, bf16[4,16,128]{2,1,0:T(8,128)(2,1)S(1)}, u32[]{:S(2)}, u32[]{:S(2)}) collective-permute-start(bf16[4,16,128]{2,1,0:T(8,128)(2,1)S(1)} %get-tuple-element.44), channel_id=1, source_target_pairs={{0,8},{1,9},{2,10},{3,11},{4,12},{5,13},{6,14},{7,15},{8,0},{9,1},... | collective-permute-start | bytes 49160 | tf_op jit(solution)/shard_map/ppermute | solution.py:409
  44.2 5.5 %collective-permute-start.13 = (bf16[4,16,128]{2,1,0:T(8,128)(2,1)S(1)}, bf16[4,16,128]{2,1,0:T(8,128)(2,1)S(1)}, u32[]{:S(2)}, u32[]{:S(2)}) collective-permute-start(bf16[4,16,128]{2,1,0:T(8,128)(2,1)S(1)} %get-tuple-element.45), channel_id=1, source_target_pairs={{0,12},{1,13},{2,14},{3,15},{4,8},{5,9},{6,10},{7,11},{8,4},{9,5},... | collective-permute-start | bytes 49160 | tf_op jit(solution)/shard_map/ppermute | solution.py:409
  51.1 5.0 %collective-permute-start.18 = (f32[2,128,128]{2,1,0:T(8,128)S(1)}, f32[2,128,128]{2,1,0:T(8,128)S(1)}, u32[]{:S(2)}, u32[]{:S(2)}) collective-permute-start(f32[2,128,128]{2,1,0:T(8,128)S(1)} %get-tuple-element.53), channel_id=1, source_target_pairs={{0,2},{1,3},{2,0},{3,1},{4,6},{5,7},{6,4},{7,5},{8,10},{9,11},{10,... | collective-permute-start | bytes 393224 | tf_op jit(solution)/shard_map/ppermute | solution.py:409
  56.1 11.7 %collective-permute-start.19 = (f32[2,128,128]{2,1,0:T(8,128)S(1)}, f32[2,128,128]{2,1,0:T(8,128)S(1)}, u32[]{:S(2)}, u32[]{:S(2)}) collective-permute-start(f32[2,128,128]{2,1,0:T(8,128)S(1)} %collective-permute-done.18.far), channel_id=1, source_target_pairs={{0,1},{1,0},{2,3},{3,2},{4,5},{5,4},{6,7},{7,6},{8,9},{9,8},{10,11... | collective-permute-start | bytes 393224 | tf_op jit(solution)/shard_map/ppermute | solution.py:409
  56.1 10.4 %all-to-all-start.1 = ((bf16[16,16,128]{2,1,0:T(8,128)(2,1)}), bf16[16,16,128]{2,1,0:T(8,128)(2,1)S(1)}, u32[]{:S(2)}, u32[]{:S(2)}) async-start(bf16[16,16,128]{2,1,0:T(8,128)(2,1)} %get-tuple-element.46), calls=%async_computation.1 | async-start | bytes 131072 | tf_op jit(solution)/shard_map/all_to_all | solution.py:412
  59.6 4.0 %collective-permute-start.15 = (bf16[2,64,128]{2,1,0:T(8,128)(2,1)S(1)}, bf16[2,64,128]{2,1,0:T(8,128)(2,1)S(1)}, u32[]{:S(2)}, u32[]{:S(2)}) collective-permute-start(bf16[2,64,128]{2,1,0:T(8,128)(2,1)S(1)} %get-tuple-element.49), channel_id=1, source_target_pairs={{0,2},{1,3},{2,0},{3,1},{4,6},{5,7},{6,4},{7,5},{8,10},{9,11},{10,... | collective-permute-start | bytes 98312 | tf_op jit(solution)/shard_map/ppermute | solution.py:409
  61.4 6.3 %collective-permute-start.17 = (f32[128,128]{1,0:T(8,128)S(1)}, f32[128,128]{1,0:T(8,128)S(1)}, u32[]{:S(2)}, u32[]{:S(2)}) collective-permute-start(f32[128,128]{1,0:T(8,128)S(1)} %get-tuple-element.52), channel_id=1, source_target_pairs={{0,1},{1,0},{2,3},{3,2},{4,5},{5,4},{6,7},{7,6},{8,9},{9,8},{10,11... | collective-permute-start | bytes 196616 | tf_op jit(solution)/shard_map/ppermute | solution.py:409
  63.6 1.4 %collective-permute-start.16 = (bf16[2,64,128]{2,1,0:T(8,128)(2,1)S(1)}, bf16[2,64,128]{2,1,0:T(8,128)(2,1)S(1)}, u32[]{:S(2)}, u32[]{:S(2)}) collective-permute-start(bf16[2,64,128]{2,1,0:T(8,128)(2,1)S(1)} %collective-permute-done.15.adj_far), channel_id=1, source_target_pairs={{0,1},{1,0},{2,3},{3,2},{4,5},{5,4},{6,7},{7,6},{8,9},{9,8},{10,11... | collective-permute-start | bytes 98312 | tf_op jit(solution)/shard_map/ppermute | solution.py:409
  63.6 1.3 %collective-permute-start.14 = (bf16[64,128]{1,0:T(8,128)(2,1)S(1)}, bf16[64,128]{1,0:T(8,128)(2,1)S(1)}, u32[]{:S(2)}, u32[]{:S(2)}) collective-permute-start(bf16[64,128]{1,0:T(8,128)(2,1)S(1)} %get-tuple-element.48), channel_id=1, source_target_pairs={{0,1},{1,0},{2,3},{3,2},{4,5},{5,4},{6,7},{7,6},{8,9},{9,8},{10,11... | collective-permute-start | bytes 49160 | tf_op jit(solution)/shard_map/ppermute | solution.py:409

commit v7 on v6

--- a/solution.py
+++ b/solution.py
@@ -82,7 +82,7 @@
     return vfac[:, :, :, cut].reshape(parts * rows * rank, -1)
 
 
-def first_kernel(data, x, ufac, vfac, out, to_far, to_near, own, u_own, x_own, v_own, *columns, group, width):
+def first_kernel(data, x, ufac, vfac, out, waves, to_far, to_near, own, u_own, x_own, v_own, *columns, group, width):
     rows = data.shape[1]
     sources = x.shape[1]
     lanes = 2 * width
@@ -90,7 +90,7 @@
     step = rows // folds
     q = group_index(group)
 
-    def run(stage, waves, scratch, quarters, sems):
+    def run(stage, scratch, quarters, sems):
         x_copy = pltpu.make_async_copy(x, x_own, sems.at[0])
         v_copy = pltpu.make_async_copy(vfac, v_own, sems.at[1])
         wave_copy = pltpu.make_async_copy(data, waves, sems.at[2])
@@ -140,14 +140,13 @@
     pl.run_scoped(
         run,
         pltpu.VMEM(out.shape, bf16),
-        pltpu.VMEM(data.shape, f32),
         pltpu.VMEM((group, rows, lanes), f32),
         pltpu.VMEM((group, sources, lanes), f32),
         pltpu.SemaphoreType.DMA((5,)),
     )
 
 
-def row_core(c, own, ufac, near, far, corner, misfits, width):
+def row_core(c, own, ufac, near, far, corner, width):
     lanes = 2 * width
     rows = own.shape[0]
     ci = times_i(c.astype(f32)).astype(bf16)
@@ -169,12 +168,8 @@
         (joined(corner, step), factors(corner, 2 * step)),
     )
     total = None
-    for b, (wave, (ur, ui)) in enumerate(blocks):
+    for wave, (ur, ui) in blocks:
         misfit = wave - (dot(ur, c) + dot(ui, ci))
-        if misfits and b < 2:
-            misfits[b][...] = misfit
-        elif misfits:
-            misfits[2][b - 2] = misfit
         mt = misfit.T.astype(bf16)
         mr, mi = mt[:width], mt[width:]
         turned = jnp.concatenate([mi, -mr], axis=0)
@@ -189,16 +184,16 @@
         adjoint[j] = flat[j * rank:(j + 1) * rank]
 
 
-def row_kernel(coeffs, own, ufac, near, far, corner, adjoint, *misfits, width):
+def row_kernel(coeffs, own, ufac, near, far, corner, adjoint, *, width):
     c = coeffs[...].reshape(-1, 2 * width)
-    to_chunks(row_core(c, own, ufac, near, far, corner, misfits, width), adjoint)
+    to_chunks(row_core(c, own, ufac, near, far, corner, width), adjoint)
 
 
 def row_first_kernel(coeffs, own, ufac, near, far, corner, *pieces, group, width):
     z = row_index(group)
     rank = coeffs.shape[1]
     c = coeffs[...].reshape(-1, 2 * width)
-    flat = row_core(c, own, ufac, near, far, corner, (), width)
+    flat = row_core(c, own, ufac, near, far, corner, width)
 
     def place(scratch):
         for j in range(flat.shape[0] // rank):
@@ -210,14 +205,15 @@
 
 
 def row_last_kernel(*refs, group, width, count):
-    pieces, (own, ufac, near, far, corner, adjoint), misfits = refs[:count], refs[count:count + 6], refs[count + 6:]
+    pieces, (own, ufac, near, far, corner, adjoint, coeffs) = refs[:count], refs[count:]
     z = row_index(group)
 
     def run(scratch):
         for b, piece in enumerate(pieces):
             scratch[jnp.bitwise_xor(z, b)] = piece[...]
         c = scratch[...].reshape(-1, 2 * width)
-        to_chunks(row_core(c, own, ufac, near, far, corner, misfits, width), adjoint)
+        coeffs[...] = c
+        to_chunks(row_core(c, own, ufac, near, far, corner, width), adjoint)
 
     pl.run_scoped(run, pltpu.VMEM((count,) + pieces[0].shape, bf16))
 
@@ -348,26 +344,27 @@
     pl.run_scoped(run, pltpu.VMEM(x.shape, f32), pltpu.SemaphoreType.DMA((PIECES,)))
 
 
-def residual_kernel(misfit, near, far, far_near, out, *, group, width):
+def residual_kernel(own, near, far, corner, ufac, data, out, *, group, width):
     q = group_index(group)
+    lanes = 2 * width
+    ur, ui = ufac[0], ufac[1]
 
     def place(scratch, stage, sem):
-        scratch[0] = misfit[...]
-        scratch[1] = near[...]
-        scratch[2] = far[0]
-        scratch[3] = far_near[1]
-        pieces = [scratch[jnp.bitwise_xor(q, s)] for s in range(group)]
+        for b, ref in enumerate((own, near, far, corner)):
+            c = ref[...]
+            scratch[b] = dot(ur, c) + dot(ui, times_i(c.astype(f32)).astype(bf16))
         for k in range(group // 2):
-            re, im = interleave(pieces[2 * k], pieces[2 * k + 1])
-            stage[0, :, 2 * width * k:2 * width * (k + 1)] = re
-            stage[1, :, 2 * width * k:2 * width * (k + 1)] = im
+            cut = slice(lanes * k, lanes * (k + 1))
+            pair = (scratch[jnp.bitwise_xor(q, s)] for s in (2 * k, 2 * k + 1))
+            for part, predicted in enumerate(interleave(*pair)):
+                stage[part, :, cut] = data[part, :, cut] - predicted
         copy = pltpu.make_async_copy(stage, out, sem)
         copy.start()
         copy.wait()
 
     pl.run_scoped(
         place,
-        pltpu.VMEM((group,) + misfit.shape, f32),
+        pltpu.VMEM((group, data.shape[1], lanes), f32),
         pltpu.VMEM(out.shape, f32),
         pltpu.SemaphoreType.DMA(()),
     )
@@ -424,10 +421,11 @@
         shape((sources, lanes), f32),
     )
     by_columns = tile_rows == 4
-    coeffs, to_far, to_near, own, ufac, estimate, vfac, *columns = call(
+    coeffs, data, to_far, to_near, own, ufac, estimate, vfac, *columns = call(
         first_kernel,
         (
             result(chunks.shape, bf16),
+            shape(data.shape, f32),
             shape((2 * rows + 2 * step, wide), bf16),
             shape((2 * rows + step, wide), bf16),
             shape((rows, lanes), f32),
@@ -441,8 +439,7 @@
     near = exchange(to_near, 1)
     corner = exchange(far, 1)
     gathered = (own, ufac, near, far, corner)
-    block = shape((rows, lanes), f32)
-    row_outs = (chunks, block, block, shape((2, rows, lanes), f32))
+    flat = (tiles * rank, lanes)
     received = spread(coeffs)
     if by_columns:
         piece = shape((group, rank, lanes), bf16)
@@ -470,25 +467,27 @@
         adj_far = exchange(adj_far, 2)
         adj_near = exchange(adj_near, 1)
         adj_corner = exchange(adj_far, 1)
-        row = call(row_last_kernel, row_outs, *pieces, *gathered, **counted)
+        adjoint, coeffs = call(row_last_kernel, (chunks, shape(flat, bf16)), *pieces, *gathered, **counted)
         estimate = call(
             own_column_kernel, shape(x_init.shape, f32),
             adj_own, adj_near, adj_far, adj_corner, estimate, vfac, aliases={4: 0}, **static,
         )
     else:
-        (pieces,) = call(row_kernel, (chunks,), received, *gathered, width=width)
+        pieces = call(row_kernel, chunks, received, *gathered, width=width)
         estimate, coeffs = call(
             middle_kernel, (shape(x_init.shape, f32), chunks), spread(pieces), estimate, vfac, **static
         )
-        row = call(row_kernel, row_outs, spread(coeffs), *gathered, width=width)
-    adjoint, misfit, to_near, to_far = row
-    misfit_far = exchange(to_far, 2)
-    misfit_near = exchange(to_near, 1)
-    misfit_corner = exchange(misfit_far, 1)
+        received = spread(coeffs)
+        adjoint = call(row_kernel, chunks, received, *gathered, width=width)
+        coeffs = received.reshape(flat)
+    coeffs_far = exchange(coeffs, 2)
+    coeffs_near = exchange(coeffs, 1)
+    coeffs_corner = exchange(coeffs_far, 1)
     adjoint = spread(adjoint)
     solved = call(last_kernel, result(x_init.shape, f32), adjoint, estimate, vfac, **static)
     residual = call(
-        residual_kernel, result(data.shape, f32), misfit, misfit_near, misfit_far, misfit_corner, **static
+        residual_kernel, result(data.shape, f32),
+        coeffs, coeffs_near, coeffs_far, coeffs_corner, ufac, data, **static,
     )
     return (solved, residual)
 

time: 68.9 us -> 64.4 us (0.935)
  waiting for transfers between devices: 27.2 us -> 21.8 us
    ppermute x20, waiting for transfers between devices: 26.5 us -> 21.1 us  [exchange(): return lax.ppermute(value, 'tile', [(s, s ^ bit) for s in range(tiles)])]
  transfers between devices with their start and end apart: 21 -> 21, of which waited for: 10 -> 9; matrix products, arithmetic and copies ran while one was open for 0% -> 0% of each run, Pallas kernels for 4% -> 4%
where the time goes in v7:
time: 64.4 us; the launch traced here: 64.1 us
  waiting for transfers between devices  21.8 us (34%)
  starting transfers between devices  21 us (33%)
  blocking collectives  11.7 us (18%)
  Pallas kernels  8.93 us (14%)
  between operations  0.7 us (1%)
    ppermute x20, waiting for transfers between devices, exchange(): return lax.ppermute(value, 'tile', [(s, s ^ bit) for s in range(tiles)])  21.1 us
    ppermute x20, starting transfers between devices, exchange(): return lax.ppermute(value, 'tile', [(s, s ^ bit) for s in range(tiles)])  17.5 us
    all_to_all x1, blocking collectives, spread(): lax.all_to_all(value, 'tile', split_axis=0, concat_axis=0, tiled=True)  11.7 us
    pallas_call x7, Pallas kernels, call(): pl.pallas_call(functools.partial(kernel, **static), out_shape=out_shape,...  8.93 us
    all_to_all x1, starting transfers between devices, spread(): lax.all_to_all(value, 'tile', split_axis=0, concat_axis=0, tiled=True)  3.5 us
  transfers between devices with their start and end apart: 21, of which 9 were waited for; matrix products, arithmetic and copies ran while one was open for 0% of the time, Pallas kernels for 4%

profile of v7, /device:TPU:0, one launch (start us, length us, event | category | flops | bytes accessed | tf_op | source)
XLA Modules:
  0.0 64.1 jit_solution(1053661369983126032)
XLA Ops:
  0.6 2.3 %shard_map.59 = (bf16[16,16,128]{2,1,0:T(8,128)(2,1)S(1)}, f32[2,128,256]{2,1,0:T(8,128)S(1)}, bf16[512,256]{1,0:T(8,128)(2,1)S(1)}, bf16[384,256]{1,0:T(8,128)(...) custom-call(f32[2,128,256]{2,1,0:T(8,128)} %data.1, ...), custom_call_target="tpu_custom_call" | custom-call | tf_op jit(solution)/shard_map/pallas_call | solution.py:382
  2.9 3.1 %collective-permute-start.1 = (bf16[512,256]{1,0:T(8,128)(2,1)S(1)}, bf16[512,256]{1,0:T(8,128)(2,1)S(1)}, u32[]{:S(2)}, u32[]{:S(2)}) collective-permute-start(bf16[512,256]{1,0:T(8,128)(2,1)S(1)} %get-tuple-element.31), channel_id=1, source_target_pairs={{0,2},{1,3},{2,0},{3,1},{4,6},{5,7},{6,4},{7,5},{8,10},{9,11},{10,... | collective-permute-start | bytes 786440 | tf_op jit(solution)/shard_map/ppermute | solution.py:406
  6.0 0.1 collective-permute-start.9
  6.1 7.1 %collective-permute-done.1.far.refs_7_ = bf16[512,256]{1,0:T(8,128)(2,1)S(1)} collective-permute-done((bf16[512,256]{1,0:T(8,128)(2,1)S(1)}, bf16[512,256]{1,0:T(8,128)(2,1)S(1)}, u32[]{:S(2)}, u32[]{:S(2)}) %collective-permute-start.1) | collective-permute-done | bytes 262176 | tf_op jit(solution)/shard_map/ppermute | solution.py:406
  13.1 0.5 collective-permute-start.6
  13.6 4.3 %collective-permute-done.9.refs_9_ = bf16[512,256]{1,0:T(8,128)(2,1)S(1)} collective-permute-done((bf16[512,256]{1,0:T(8,128)(2,1)S(1)}, bf16[512,256]{1,0:T(8,128)(2,1)S(1)}, u32[]{:S(2)}, u32[]{:S(2)}) %collective-permute-start.9) | collective-permute-done | bytes 262176 | tf_op jit(solution)/shard_map/ppermute | solution.py:406
  17.9 1.7 %collective-permute-start.8 = (bf16[512,128]{1,0:T(8,128)(2,1)S(1)}, bf16[512,128]{1,0:T(8,128)(2,1)S(1)}, u32[]{:S(2)}, u32[]{:S(2)}) collective-permute-start(bf16[512,128]{1,0:T(8,128)(2,1)S(1)} %get-tuple-element.39), channel_id=1, source_target_pairs={{0,2},{1,3},{2,0},{3,1},{4,6},{5,7},{6,4},{7,5},{8,10},{9,11},{10,... | collective-permute-start | bytes 393224 | tf_op jit(solution)/shard_map/ppermute | solution.py:406
  19.6 0.2 collective-permute-start.7
  19.9 11.7 %all_to_all.10.coeffs = bf16[16,16,128]{2,1,0:T(8,128)(2,1)S(1)} all-to-all(bf16[16,16,128]{2,1,0:T(8,128)(2,1)S(1)} %get-tuple-element.27), channel_id=1, replica_groups=mesh['freq'=2,'tile'=16] {'tile'}, dimensions={0} | all-to-all | bytes 131072 | tf_op jit(solution)/shard_map/all_to_all | solution.py:409
  31.5 0.8 %shard_map.60 = (bf16[4,16,128]{2,1,0:T(8,128)(2,1)S(1)}, bf16[4,16,128]{2,1,0:T(8,128)(2,1)S(1)}, bf16[4,16,128]{2,1,0:T(8,128)(2,1)S(1)}, bf16[4,16,128]{2,1,0:T(8,128)(2,1)S(1)}) custom-call(bf16[16,16,128]{2,1,0:T(8,128)(2,1)S(1)} %all_to_all.10.coeffs, f32[128,128]{1,0:T(8,128)S(1)} %get-tuple-element.28.own.refs_4_, ...), custom_call_target="tpu_custom_call" | custom-call | tf_op jit(solution)/shard_map/pallas_call | solution.py:382
  32.4 0.2 collective-permute-start.3
  32.5 1.0 %collective-permute-start.4 = (bf16[4,16,128]{2,1,0:T(8,128)(2,1)S(1)}, bf16[4,16,128]{2,1,0:T(8,128)(2,1)S(1)}, u32[]{:S(2)}, u32[]{:S(2)}) collective-permute-start(bf16[4,16,128]{2,1,0:T(8,128)(2,1)S(1)} %get-tuple-element.34), channel_id=1, source_target_pairs={{0,8},{1,9},{2,10},{3,11},{4,12},{5,13},{6,14},{7,15},{8,0},{9,1},... | collective-permute-start | bytes 49160 | tf_op jit(solution)/shard_map/ppermute | solution.py:406
  33.5 3.3 %collective-permute-start.5 = (bf16[4,16,128]{2,1,0:T(8,128)(2,1)S(1)}, bf16[4,16,128]{2,1,0:T(8,128)(2,1)S(1)}, u32[]{:S(2)}, u32[]{:S(2)}) collective-permute-start(bf16[4,16,128]{2,1,0:T(8,128)(2,1)S(1)} %get-tuple-element.35), channel_id=1, source_target_pairs={{0,12},{1,13},{2,14},{3,15},{4,8},{5,9},{6,10},{7,11},{8,4},{9,5},... | collective-permute-start | bytes 49160 | tf_op jit(solution)/shard_map/ppermute | solution.py:406
  36.8 0.4 collective-permute-done.4.refs_2_
  37.2 1.9 %collective-permute-done.5.refs_3_ = bf16[4,16,128]{2,1,0:T(8,128)(2,1)S(1)} collective-permute-done((bf16[4,16,128]{2,1,0:T(8,128)(2,1)S(1)}, bf16[4,16,128]{2,1,0:T(8,128)(2,1)S(1)}, u32[]{:S(2)}, u32[]{:S(2)}) %collective-permute-start.5) | collective-permute-done | bytes 16416 | tf_op jit(solution)/shard_map/ppermute | solution.py:406
  39.1 1.2 %shard_map.61 = (bf16[4,16,128]{2,1,0:T(8,128)(2,1)S(1)}, bf16[4,16,128]{2,1,0:T(8,128)(2,1)S(1)}, bf16[4,16,128]{2,1,0:T(8,128)(2,1)S(1)}, bf16[4,16,128]{2,1,0...) custom-call(bf16[4,16,128]{2,1,0:T(8,128)(2,1)S(1)} %get-tuple-element, ...), custom_call_target="tpu_custom_call" | custom-call | tf_op jit(solution)/shard_map/pallas_call | solution.py:382
  40.3 3.8 %collective-permute-start.12 = (bf16[4,16,128]{2,1,0:T(8,128)(2,1)S(1)}, bf16[4,16,128]{2,1,0:T(8,128)(2,1)S(1)}, u32[]{:S(2)}, u32[]{:S(2)}) collective-permute-start(bf16[4,16,128]{2,1,0:T(8,128)(2,1)S(1)} %get-tuple-element.43), channel_id=1, source_target_pairs={{0,8},{1,9},{2,10},{3,11},{4,12},{5,13},{6,14},{7,15},{8,0},{9,1},... | collective-permute-start | bytes 49160 | tf_op jit(solution)/shard_map/ppermute | solution.py:406
  44.2 0.6 collective-permute-start.13
  44.7 1.2 %collective-permute-done.12.refs_2_ = bf16[4,16,128]{2,1,0:T(8,128)(2,1)S(1)} collective-permute-done((bf16[4,16,128]{2,1,0:T(8,128)(2,1)S(1)}, bf16[4,16,128]{2,1,0:T(8,128)(2,1)S(1)}, u32[]{:S(2)}, u32[]{:S(2)}) %collective-permute-start.12) | collective-permute-done | bytes 16416 | tf_op jit(solution)/shard_map/ppermute | solution.py:406
  45.9 3.8 %collective-permute-done.13.refs_3_ = bf16[4,16,128]{2,1,0:T(8,128)(2,1)S(1)} collective-permute-done((bf16[4,16,128]{2,1,0:T(8,128)(2,1)S(1)}, bf16[4,16,128]{2,1,0:T(8,128)(2,1)S(1)}, u32[]{:S(2)}, u32[]{:S(2)}) %collective-permute-start.13) | collective-permute-done | bytes 16416 | tf_op jit(solution)/shard_map/ppermute | solution.py:406
  49.7 1.4 %shard_map.62 = (bf16[16,16,128]{2,1,0:T(8,128)(2,1)}, bf16[256,128]{1,0:T(8,128)(2,1)S(1)}) custom-call(bf16[4,16,128]{2,1,0:T(8,128)(2,1)S(1)} %get-tuple-element.41.refs_0_, bf16[4,16,128]{2,1,0:T(8,128)(2,1)S(1)} %collective-permute-done.11.refs_1_, bf16[4,16,128]{2,1,0:T(8,128)(2,1)S(1)} %collective-permute-done.12.refs_2_, ...), custom_call_target="tpu_custom_call" | custom-call | tf_op jit(solution)/shard_map/pallas_call | solution.py:382
  51.1 0.1 collective-permute-start.18
  51.2 3.5 %all-to-all-start.1 = ((bf16[16,16,128]{2,1,0:T(8,128)(2,1)}), bf16[16,16,128]{2,1,0:T(8,128)(2,1)S(1)}, u32[]{:S(2)}, u32[]{:S(2)}) async-start(bf16[16,16,128]{2,1,0:T(8,128)(2,1)} %get-tuple-element.45), calls=%async_computation.1 | async-start | bytes 131072 | tf_op jit(solution)/shard_map/all_to_all | solution.py:409
  54.8 1.9 %collective-permute-start.15 = (bf16[2,64,128]{2,1,0:T(8,128)(2,1)S(1)}, bf16[2,64,128]{2,1,0:T(8,128)(2,1)S(1)}, u32[]{:S(2)}, u32[]{:S(2)}) collective-permute-start(bf16[2,64,128]{2,1,0:T(8,128)(2,1)S(1)} %get-tuple-element.48), channel_id=1, source_target_pairs={{0,2},{1,3},{2,0},{3,1},{4,6},{5,7},{6,4},{7,5},{8,10},{9,11},{10,... | collective-permute-start | bytes 98312 | tf_op jit(solution)/shard_map/ppermute | solution.py:406
  56.6 0.5 collective-permute-start.19
  57.1 1.6 %collective-permute-done.15.adj_far = bf16[2,64,128]{2,1,0:T(8,128)(2,1)S(1)} collective-permute-done((bf16[2,64,128]{2,1,0:T(8,128)(2,1)S(1)}, bf16[2,64,128]{2,1,0:T(8,128)(2,1)S(1)}, u32[]{:S(2)}, u32[]{:S(2)}) %collective-permute-start.15) | collective-permute-done | bytes 32800 | tf_op jit(solution)/shard_map/ppermute | solution.py:406
  58.8 0.5 collective-permute-start.14
  59.3 0.8 %collective-permute-done.14.adj_near = bf16[64,128]{1,0:T(8,128)(2,1)S(1)} collective-permute-done((bf16[64,128]{1,0:T(8,128)(2,1)S(1)}, bf16[64,128]{1,0:T(8,128)(2,1)S(1)}, u32[]{:S(2)}, u32[]{:S(2)}) %collective-permute-start.14) | collective-permute-done | bytes 16416 | tf_op jit(solution)/shard_map/ppermute | solution.py:406
  60.1 0.8 %shard_map.63.x = f32[2,512,256]{2,1,0:T(8,128)S(1)} custom-call(bf16[64,128]{1,0:T(8,128)(2,1)S(1)} %get-tuple-element.46.adj_own, bf16[64,128]{1,0:T(8,128)(2,1)S(1)} %collective-permute-done.14.adj_near, bf16[2,64,128]{2,1,0:T(8,128)(2,1)S(1)} %collective-permute-done.15.adj_far, ...), custom_call_target="tpu_custom_call", output_to_operand_aliasing={{}: (4, {})} | custom-call | tf_op jit(solution)/shard_map/pallas_call | solution.py:382
  60.9 0.7 %all-to-all-done.1.adjoint = bf16[16,16,128]{2,1,0:T(8,128)(2,1)S(1)} async-done(((bf16[16,16,128]{2,1,0:T(8,128)(2,1)}), bf16[16,16,128]{2,1,0:T(8,128)(2,1)S(1)}, u32[]{:S(2)}, u32[]{:S(2)}) %all-to-all-start.1) | async-done | bytes 65568 | tf_op jit(solution)/shard_map/all_to_all | solution.py:409
  61.6 1.3 %shard_map.64 = f32[2,512,256]{2,1,0:T(8,128)} custom-call(bf16[16,16,128]{2,1,0:T(8,128)(2,1)S(1)} %all-to-all-done.1.adjoint, f32[2,512,256]{2,1,0:T(8,128)S(1)} %shard_map.63.x, bf16[2,4,16,512]{3,2,1,0:T(8,128)(2,1)S(1)} %get-tuple-element.37.refs_5_.vfac), custom_call_target="tpu_custom_call" | custom-call | tf_op jit(solution)/shard_map/pallas_call | solution.py:382
  62.9 1.2 %shard_map.65 = f32[2,128,256]{2,1,0:T(8,128)} custom-call(bf16[256,128]{1,0:T(8,128)(2,1)S(1)} %get-tuple-element.50.own, bf16[256,128]{1,0:T(8,128)(2,1)S(1)} %collective-permute-done.17.near, bf16[256,128]{1,0:T(8,128)(2,1)S(1)} %collective-permute-done.18.far, bf16[256,128]{1,0:T(8,128)(2,1)S(1)} %collective-permute-done.19.corner, ...), custom_call_target="tpu_custom_call" | custom-call | tf_op jit(solution)/shard_map/pallas_call | solution.py:382
  (18 shorter events, 0.1 us)
Async XLA Ops:
  2.9 10.2 %collective-permute-start.1 = (bf16[512,256]{1,0:T(8,128)(2,1)S(1)}, bf16[512,256]{1,0:T(8,128)(2,1)S(1)}, u32[]{:S(2)}, u32[]{:S(2)}) collective-permute-start(bf16[512,256]{1,0:T(8,128)(2,1)S(1)} %get-tuple-element.31), channel_id=1, source_target_pairs={{0,2},{1,3},{2,0},{3,1},{4,6},{5,7},{6,4},{7,5},{8,10},{9,11},{10,... | collective-permute-start | bytes 786440 | tf_op jit(solution)/shard_map/ppermute | solution.py:406
  6.0 11.9 %collective-permute-start.9 = (bf16[512,256]{1,0:T(8,128)(2,1)S(1)}, bf16[512,256]{1,0:T(8,128)(2,1)S(1)}, u32[]{:S(2)}, u32[]{:S(2)}) collective-permute-start(bf16[512,256]{1,0:T(8,128)(2,1)S(1)} %get-tuple-element.40), channel_id=1, source_target_pairs={{0,2},{1,3},{2,0},{3,1},{4,6},{5,7},{6,4},{7,5},{8,10},{9,11},{10,... | collective-permute-start | bytes 786440 | tf_op jit(solution)/shard_map/ppermute | solution.py:406
  6.1 13.6 %collective-permute-start = (bf16[384,256]{1,0:T(8,128)(2,1)S(1)}, bf16[384,256]{1,0:T(8,128)(2,1)S(1)}, u32[]{:S(2)}, u32[]{:S(2)}) collective-permute-start(bf16[384,256]{1,0:T(8,128)(2,1)S(1)} %get-tuple-element.30), channel_id=1, source_target_pairs={{0,1},{1,0},{2,3},{3,2},{4,5},{5,4},{6,7},{7,6},{8,9},{9,8},{10,11... | collective-permute-start | bytes 589832 | tf_op jit(solution)/shard_map/ppermute | solution.py:406
  13.1 18.4 %collective-permute-start.2 = (bf16[512,256]{1,0:T(8,128)(2,1)S(1)}, bf16[512,256]{1,0:T(8,128)(2,1)S(1)}, u32[]{:S(2)}, u32[]{:S(2)}) collective-permute-start(bf16[512,256]{1,0:T(8,128)(2,1)S(1)} %collective-permute-done.1.far.refs_7_), channel_id=1, source_target_pairs={{0,1},{1,0},{2,3},{3,2},{4,5},{5,4},{6,7},{7,6},{8,9},{9,8},{10,11... | collective-permute-start | bytes 786440 | tf_op jit(solution)/shard_map/ppermute | solution.py:406
  13.1 23.7 %collective-permute-start.6 = (bf16[512,256]{1,0:T(8,128)(2,1)S(1)}, bf16[512,256]{1,0:T(8,128)(2,1)S(1)}, u32[]{:S(2)}, u32[]{:S(2)}) collective-permute-start(bf16[512,256]{1,0:T(8,128)(2,1)S(1)} %get-tuple-element.38), channel_id=1, source_target_pairs={{0,1},{1,0},{2,3},{3,2},{4,5},{5,4},{6,7},{7,6},{8,9},{9,8},{10,11... | collective-permute-start | bytes 786440 | tf_op jit(solution)/shard_map/ppermute | solution.py:406
  17.9 18.9 %collective-permute-start.10 = (bf16[512,256]{1,0:T(8,128)(2,1)S(1)}, bf16[512,256]{1,0:T(8,128)(2,1)S(1)}, u32[]{:S(2)}, u32[]{:S(2)}) collective-permute-start(bf16[512,256]{1,0:T(8,128)(2,1)S(1)} %collective-permute-done.9.refs_9_), channel_id=1, source_target_pairs={{0,1},{1,0},{2,3},{3,2},{4,5},{5,4},{6,7},{7,6},{8,9},{9,8},{10,11... | collective-permute-start | bytes 786440 | tf_op jit(solution)/shard_map/ppermute | solution.py:406
  17.9 14.6 %collective-permute-start.8 = (bf16[512,128]{1,0:T(8,128)(2,1)S(1)}, bf16[512,128]{1,0:T(8,128)(2,1)S(1)}, u32[]{:S(2)}, u32[]{:S(2)}) collective-permute-start(bf16[512,128]{1,0:T(8,128)(2,1)S(1)} %get-tuple-element.39), channel_id=1, source_target_pairs={{0,2},{1,3},{2,0},{3,1},{4,6},{5,7},{6,4},{7,5},{8,10},{9,11},{10,... | collective-permute-start | bytes 393224 | tf_op jit(solution)/shard_map/ppermute | solution.py:406
  19.6 13.9 %collective-permute-start.7 = (bf16[2,4,16,512]{3,2,1,0:T(8,128)(2,1)S(1)}, bf16[2,4,16,512]{3,2,1,0:T(8,128)(2,1)S(1)}, u32[]{:S(2)}, u32[]{:S(2)}) collective-permute-start(bf16[2,4,16,512]{3,2,1,0:T(8,128)(2,1)S(1)} %get-tuple-element.37.refs_5_.vfac), channel_id=1, source_target_pairs={{0,1},{1,0},{2,3},{3,2},{4,5},{5,4},{6,7},{7,6},{8,9},{9,8},{10,11... | collective-permute-start | bytes 393224 | tf_op jit(solution)/shard_map/ppermute | solution.py:406
  32.4 4.5 %collective-permute-start.3 = (bf16[4,16,128]{2,1,0:T(8,128)(2,1)S(1)}, bf16[4,16,128]{2,1,0:T(8,128)(2,1)S(1)}, u32[]{:S(2)}, u32[]{:S(2)}) collective-permute-start(bf16[4,16,128]{2,1,0:T(8,128)(2,1)S(1)} %get-tuple-element.33), channel_id=1, source_target_pairs={{0,4},{1,5},{2,6},{3,7},{4,0},{5,1},{6,2},{7,3},{8,12},{9,13},{10,... | collective-permute-start | bytes 49160 | tf_op jit(solution)/shard_map/ppermute | solution.py:406
  32.5 4.6 %collective-permute-start.4 = (bf16[4,16,128]{2,1,0:T(8,128)(2,1)S(1)}, bf16[4,16,128]{2,1,0:T(8,128)(2,1)S(1)}, u32[]{:S(2)}, u32[]{:S(2)}) collective-permute-start(bf16[4,16,128]{2,1,0:T(8,128)(2,1)S(1)} %get-tuple-element.34), channel_id=1, source_target_pairs={{0,8},{1,9},{2,10},{3,11},{4,12},{5,13},{6,14},{7,15},{8,0},{9,1},... | collective-permute-start | bytes 49160 | tf_op jit(solution)/shard_map/ppermute | solution.py:406
  33.5 5.5 %collective-permute-start.5 = (bf16[4,16,128]{2,1,0:T(8,128)(2,1)S(1)}, bf16[4,16,128]{2,1,0:T(8,128)(2,1)S(1)}, u32[]{:S(2)}, u32[]{:S(2)}) collective-permute-start(bf16[4,16,128]{2,1,0:T(8,128)(2,1)S(1)} %get-tuple-element.35), channel_id=1, source_target_pairs={{0,12},{1,13},{2,14},{3,15},{4,8},{5,9},{6,10},{7,11},{8,4},{9,5},... | collective-permute-start | bytes 49160 | tf_op jit(solution)/shard_map/ppermute | solution.py:406
  40.3 4.5 %collective-permute-start.11 = (bf16[4,16,128]{2,1,0:T(8,128)(2,1)S(1)}, bf16[4,16,128]{2,1,0:T(8,128)(2,1)S(1)}, u32[]{:S(2)}, u32[]{:S(2)}) collective-permute-start(bf16[4,16,128]{2,1,0:T(8,128)(2,1)S(1)} %get-tuple-element.42), channel_id=1, source_target_pairs={{0,4},{1,5},{2,6},{3,7},{4,0},{5,1},{6,2},{7,3},{8,12},{9,13},{10,... | collective-permute-start | bytes 49160 | tf_op jit(solution)/shard_map/ppermute | solution.py:406
  40.3 5.5 %collective-permute-start.12 = (bf16[4,16,128]{2,1,0:T(8,128)(2,1)S(1)}, bf16[4,16,128]{2,1,0:T(8,128)(2,1)S(1)}, u32[]{:S(2)}, u32[]{:S(2)}) collective-permute-start(bf16[4,16,128]{2,1,0:T(8,128)(2,1)S(1)} %get-tuple-element.43), channel_id=1, source_target_pairs={{0,8},{1,9},{2,10},{3,11},{4,12},{5,13},{6,14},{7,15},{8,0},{9,1},... | collective-permute-start | bytes 49160 | tf_op jit(solution)/shard_map/ppermute | solution.py:406
  44.2 5.5 %collective-permute-start.13 = (bf16[4,16,128]{2,1,0:T(8,128)(2,1)S(1)}, bf16[4,16,128]{2,1,0:T(8,128)(2,1)S(1)}, u32[]{:S(2)}, u32[]{:S(2)}) collective-permute-start(bf16[4,16,128]{2,1,0:T(8,128)(2,1)S(1)} %get-tuple-element.44), channel_id=1, source_target_pairs={{0,12},{1,13},{2,14},{3,15},{4,8},{5,9},{6,10},{7,11},{8,4},{9,5},... | collective-permute-start | bytes 49160 | tf_op jit(solution)/shard_map/ppermute | solution.py:406
  51.1 5.5 %collective-permute-start.18 = (bf16[256,128]{1,0:T(8,128)(2,1)S(1)}, bf16[256,128]{1,0:T(8,128)(2,1)S(1)}, u32[]{:S(2)}, u32[]{:S(2)}) collective-permute-start(bf16[256,128]{1,0:T(8,128)(2,1)S(1)} %get-tuple-element.50.own), channel_id=1, source_target_pairs={{0,2},{1,3},{2,0},{3,1},{4,6},{5,7},{6,4},{7,5},{8,10},{9,11},{10,... | collective-permute-start | bytes 196616 | tf_op jit(solution)/shard_map/ppermute | solution.py:406
  51.2 10.4 %all-to-all-start.1 = ((bf16[16,16,128]{2,1,0:T(8,128)(2,1)}), bf16[16,16,128]{2,1,0:T(8,128)(2,1)S(1)}, u32[]{:S(2)}, u32[]{:S(2)}) async-start(bf16[16,16,128]{2,1,0:T(8,128)(2,1)} %get-tuple-element.45), calls=%async_computation.1 | async-start | bytes 131072 | tf_op jit(solution)/shard_map/all_to_all | solution.py:409
  54.8 4.0 %collective-permute-start.15 = (bf16[2,64,128]{2,1,0:T(8,128)(2,1)S(1)}, bf16[2,64,128]{2,1,0:T(8,128)(2,1)S(1)}, u32[]{:S(2)}, u32[]{:S(2)}) collective-permute-start(bf16[2,64,128]{2,1,0:T(8,128)(2,1)S(1)} %get-tuple-element.48), channel_id=1, source_target_pairs={{0,2},{1,3},{2,0},{3,1},{4,6},{5,7},{6,4},{7,5},{8,10},{9,11},{10,... | collective-permute-start | bytes 98312 | tf_op jit(solution)/shard_map/ppermute | solution.py:406
  56.6 6.3 %collective-permute-start.17 = (bf16[256,128]{1,0:T(8,128)(2,1)S(1)}, bf16[256,128]{1,0:T(8,128)(2,1)S(1)}, u32[]{:S(2)}, u32[]{:S(2)}) collective-permute-start(bf16[256,128]{1,0:T(8,128)(2,1)S(1)} %get-tuple-element.50.own), channel_id=1, source_target_pairs={{0,1},{1,0},{2,3},{3,2},{4,5},{5,4},{6,7},{7,6},{8,9},{9,8},{10,11... | collective-permute-start | bytes 196616 | tf_op jit(solution)/shard_map/ppermute | solution.py:406
  56.6 6.3 %collective-permute-start.19 = (bf16[256,128]{1,0:T(8,128)(2,1)S(1)}, bf16[256,128]{1,0:T(8,128)(2,1)S(1)}, u32[]{:S(2)}, u32[]{:S(2)}) collective-permute-start(bf16[256,128]{1,0:T(8,128)(2,1)S(1)} %collective-permute-done.18.far), channel_id=1, source_target_pairs={{0,1},{1,0},{2,3},{3,2},{4,5},{5,4},{6,7},{7,6},{8,9},{9,8},{10,11... | collective-permute-start | bytes 196616 | tf_op jit(solution)/shard_map/ppermute | solution.py:406
  58.8 1.4 %collective-permute-start.16 = (bf16[2,64,128]{2,1,0:T(8,128)(2,1)S(1)}, bf16[2,64,128]{2,1,0:T(8,128)(2,1)S(1)}, u32[]{:S(2)}, u32[]{:S(2)}) collective-permute-start(bf16[2,64,128]{2,1,0:T(8,128)(2,1)S(1)} %collective-permute-done.15.adj_far), channel_id=1, source_target_pairs={{0,1},{1,0},{2,3},{3,2},{4,5},{5,4},{6,7},{7,6},{8,9},{9,8},{10,11... | collective-permute-start | bytes 98312 | tf_op jit(solution)/shard_map/ppermute | solution.py:406
  58.8 1.3 %collective-permute-start.14 = (bf16[64,128]{1,0:T(8,128)(2,1)S(1)}, bf16[64,128]{1,0:T(8,128)(2,1)S(1)}, u32[]{:S(2)}, u32[]{:S(2)}) collective-permute-start(bf16[64,128]{1,0:T(8,128)(2,1)S(1)} %get-tuple-element.47), channel_id=1, source_target_pairs={{0,1},{1,0},{2,3},{3,2},{4,5},{5,4},{6,7},{7,6},{8,9},{9,8},{10,11... | collective-permute-start | bytes 49160 | tf_op jit(solution)/shard_map/ppermute | solution.py:406

commit v8 on v7

--- a/solution.py
+++ b/solution.py
@@ -82,7 +82,7 @@
     return vfac[:, :, :, cut].reshape(parts * rows * rank, -1)
 
 
-def first_kernel(data, x, ufac, vfac, out, waves, to_far, to_near, own, u_own, x_own, v_own, *columns, group, width):
+def first_kernel(data, x, ufac, vfac, out, kept, to_far, to_near, own, u_own, x_own, v_own, *columns, group, width):
     rows = data.shape[1]
     sources = x.shape[1]
     lanes = 2 * width
@@ -90,7 +90,7 @@
     step = rows // folds
     q = group_index(group)
 
-    def run(stage, scratch, quarters, sems):
+    def run(stage, waves, scratch, quarters, sems):
         x_copy = pltpu.make_async_copy(x, x_own, sems.at[0])
         v_copy = pltpu.make_async_copy(vfac, v_own, sems.at[1])
         wave_copy = pltpu.make_async_copy(data, waves, sems.at[2])
@@ -108,6 +108,7 @@
         for s, block in enumerate(slices_of(waves[0], waves[1], width)):
             scratch[jnp.bitwise_xor(q, s)] = block
         own[...] = scratch[0]
+        kept[...] = waves[...]
         for ref, base, b in ((to_near, 0, 1), (to_far, 0, 2), (to_far, step, 3)):
             high, low = split(scratch[b])
             for g in range(folds):
@@ -140,6 +141,7 @@
     pl.run_scoped(
         run,
         pltpu.VMEM(out.shape, bf16),
+        pltpu.VMEM(data.shape, f32),
         pltpu.VMEM((group, rows, lanes), f32),
         pltpu.VMEM((group, sources, lanes), f32),
         pltpu.SemaphoreType.DMA((5,)),
@@ -326,13 +328,14 @@
     send_coeffs(vcat, xr.astype(bf16), xi.astype(bf16), out, group=group, width=width)
 
 
-def last_kernel(adjoint, x, vfac, x_new, *, group, width):
+def last_kernel(adjoint, x, vfac, misfit, x_new, residual, *, group, width):
     sources = x.shape[1]
     piece = sources // PIECES
 
     def run(stage, sems):
+        copies = [pltpu.make_async_copy(misfit, residual, sems.at[PIECES])]
+        copies[0].start()
         sides = adjoint_sides(adjoint, group=group)
-        copies = []
         for k in range(PIECES):
             cut = slice(k * piece, (k + 1) * piece)
             stage[0, cut], stage[1, cut] = updated(sides, x[0, cut], x[1, cut], flat_factors(vfac, cut))
@@ -341,7 +344,7 @@
         for copy in copies:
             copy.wait()
 
-    pl.run_scoped(run, pltpu.VMEM(x.shape, f32), pltpu.SemaphoreType.DMA((PIECES,)))
+    pl.run_scoped(run, pltpu.VMEM(x.shape, f32), pltpu.SemaphoreType.DMA((PIECES + 1,)))
 
 
 def residual_kernel(own, near, far, corner, ufac, data, out, *, group, width):
@@ -349,7 +352,7 @@
     lanes = 2 * width
     ur, ui = ufac[0], ufac[1]
 
-    def place(scratch, stage, sem):
+    def place(scratch):
         for b, ref in enumerate((own, near, far, corner)):
             c = ref[...]
             scratch[b] = dot(ur, c) + dot(ui, times_i(c.astype(f32)).astype(bf16))
@@ -357,17 +360,9 @@
             cut = slice(lanes * k, lanes * (k + 1))
             pair = (scratch[jnp.bitwise_xor(q, s)] for s in (2 * k, 2 * k + 1))
             for part, predicted in enumerate(interleave(*pair)):
-                stage[part, :, cut] = data[part, :, cut] - predicted
-        copy = pltpu.make_async_copy(stage, out, sem)
-        copy.start()
-        copy.wait()
-
-    pl.run_scoped(
-        place,
-        pltpu.VMEM((group, data.shape[1], lanes), f32),
-        pltpu.VMEM(out.shape, f32),
-        pltpu.SemaphoreType.DMA(()),
-    )
+                out[part, :, cut] = data[part, :, cut] - predicted
+
+    pl.run_scoped(place, pltpu.VMEM((group, data.shape[1], lanes), f32))
 
 
 def call(kernel, out_shape, *args, from_hbm=False, aliases=None, **static):
@@ -484,12 +479,14 @@
     coeffs_near = exchange(coeffs, 1)
     coeffs_corner = exchange(coeffs_far, 1)
     adjoint = spread(adjoint)
-    solved = call(last_kernel, result(x_init.shape, f32), adjoint, estimate, vfac, **static)
-    residual = call(
-        residual_kernel, result(data.shape, f32),
+    misfit = call(
+        residual_kernel, shape(data.shape, f32),
         coeffs, coeffs_near, coeffs_far, coeffs_corner, ufac, data, **static,
     )
-    return (solved, residual)
+    return call(
+        last_kernel, (result(x_init.shape, f32), result(data.shape, f32)),
+        adjoint, estimate, vfac, misfit, **static,
+    )
 
 
 def solution(mesh):

time: 64.4 us -> 63.2 us (0.981)
  Pallas kernels: 8.93 us -> 8.23 us
    pallas_call x7, Pallas kernels: 8.93 us -> 8.23 us  [call(): pl.pallas_call(functools.partial(kernel, **static), out_shape=out_shape,...]
  transfers between devices with their start and end apart: 21 -> 21, of which waited for: 9 -> 9; matrix products, arithmetic and copies ran while one was open for 0% -> 0% of each run, Pallas kernels for 4% -> 3%
where the time goes in v8:
time: 63.2 us; the launch traced here: 62.9 us
  waiting for transfers between devices  21.3 us (34%)
  starting transfers between devices  21 us (33%)
  blocking collectives  11.7 us (19%)
  Pallas kernels  8.23 us (13%)
  between operations  0.72 us (1%)
    ppermute x20, waiting for transfers between devices, exchange(): return lax.ppermute(value, 'tile', [(s, s ^ bit) for s in range(tiles)])  21.1 us
    ppermute x20, starting transfers between devices, exchange(): return lax.ppermute(value, 'tile', [(s, s ^ bit) for s in range(tiles)])  17.5 us
    all_to_all x1, blocking collectives, spread(): lax.all_to_all(value, 'tile', split_axis=0, concat_axis=0, tiled=True)  11.7 us
    pallas_call x7, Pallas kernels, call(): pl.pallas_call(functools.partial(kernel, **static), out_shape=out_shape,...  8.23 us
    all_to_all x1, starting transfers between devices, spread(): lax.all_to_all(value, 'tile', split_axis=0, concat_axis=0, tiled=True)  3.5 us
  transfers between devices with their start and end apart: 21, of which 9 were waited for; matrix products, arithmetic and copies ran while one was open for 0% of the time, Pallas kernels for 3%

profile of v8, /device:TPU:0, one launch (start us, length us, event | category | flops | bytes accessed | tf_op | source)
XLA Modules:
  0.0 62.9 jit_solution(13460493513341079955)
XLA Ops:
  0.6 2.3 %shard_map.59 = (bf16[16,16,128]{2,1,0:T(8,128)(2,1)S(1)}, f32[2,128,256]{2,1,0:T(8,128)S(1)}, bf16[512,256]{1,0:T(8,128)(2,1)S(1)}, bf16[384,256]{1,0:T(8,128)(...) custom-call(f32[2,128,256]{2,1,0:T(8,128)} %data.1, ...), custom_call_target="tpu_custom_call" | custom-call | tf_op jit(solution)/shard_map/pallas_call | solution.py:377
  2.9 3.1 %collective-permute-start.1 = (bf16[512,256]{1,0:T(8,128)(2,1)S(1)}, bf16[512,256]{1,0:T(8,128)(2,1)S(1)}, u32[]{:S(2)}, u32[]{:S(2)}) collective-permute-start(bf16[512,256]{1,0:T(8,128)(2,1)S(1)} %get-tuple-element.31), channel_id=1, source_target_pairs={{0,2},{1,3},{2,0},{3,1},{4,6},{5,7},{6,4},{7,5},{8,10},{9,11},{10,... | collective-permute-start | bytes 786440 | tf_op jit(solution)/shard_map/ppermute | solution.py:401
  6.0 0.1 collective-permute-start.9
  6.1 7.1 %collective-permute-done.1.far.refs_7_ = bf16[512,256]{1,0:T(8,128)(2,1)S(1)} collective-permute-done((bf16[512,256]{1,0:T(8,128)(2,1)S(1)}, bf16[512,256]{1,0:T(8,128)(2,1)S(1)}, u32[]{:S(2)}, u32[]{:S(2)}) %collective-permute-start.1) | collective-permute-done | bytes 262176 | tf_op jit(solution)/shard_map/ppermute | solution.py:401
  13.1 0.5 collective-permute-start.6
  13.7 4.3 %collective-permute-done.9.refs_9_ = bf16[512,256]{1,0:T(8,128)(2,1)S(1)} collective-permute-done((bf16[512,256]{1,0:T(8,128)(2,1)S(1)}, bf16[512,256]{1,0:T(8,128)(2,1)S(1)}, u32[]{:S(2)}, u32[]{:S(2)}) %collective-permute-start.9) | collective-permute-done | bytes 262176 | tf_op jit(solution)/shard_map/ppermute | solution.py:401
  17.9 1.7 %collective-permute-start.8 = (bf16[512,128]{1,0:T(8,128)(2,1)S(1)}, bf16[512,128]{1,0:T(8,128)(2,1)S(1)}, u32[]{:S(2)}, u32[]{:S(2)}) collective-permute-start(bf16[512,128]{1,0:T(8,128)(2,1)S(1)} %get-tuple-element.39), channel_id=1, source_target_pairs={{0,2},{1,3},{2,0},{3,1},{4,6},{5,7},{6,4},{7,5},{8,10},{9,11},{10,... | collective-permute-start | bytes 393224 | tf_op jit(solution)/shard_map/ppermute | solution.py:401
  19.7 0.2 collective-permute-start.7
  19.9 11.7 %all_to_all.10.coeffs = bf16[16,16,128]{2,1,0:T(8,128)(2,1)S(1)} all-to-all(bf16[16,16,128]{2,1,0:T(8,128)(2,1)S(1)} %get-tuple-element.27), channel_id=1, replica_groups=mesh['freq'=2,'tile'=16] {'tile'}, dimensions={0} | all-to-all | bytes 131072 | tf_op jit(solution)/shard_map/all_to_all | solution.py:404
  31.6 0.8 %shard_map.60 = (bf16[4,16,128]{2,1,0:T(8,128)(2,1)S(1)}, bf16[4,16,128]{2,1,0:T(8,128)(2,1)S(1)}, bf16[4,16,128]{2,1,0:T(8,128)(2,1)S(1)}, bf16[4,16,128]{2,1,0:T(8,128)(2,1)S(1)}) custom-call(bf16[16,16,128]{2,1,0:T(8,128)(2,1)S(1)} %all_to_all.10.coeffs, f32[128,128]{1,0:T(8,128)S(1)} %get-tuple-element.28.own.refs_4_, ...), custom_call_target="tpu_custom_call" | custom-call | tf_op jit(solution)/shard_map/pallas_call | solution.py:377
  32.4 0.2 collective-permute-start.3
  32.6 1.0 %collective-permute-start.4 = (bf16[4,16,128]{2,1,0:T(8,128)(2,1)S(1)}, bf16[4,16,128]{2,1,0:T(8,128)(2,1)S(1)}, u32[]{:S(2)}, u32[]{:S(2)}) collective-permute-start(bf16[4,16,128]{2,1,0:T(8,128)(2,1)S(1)} %get-tuple-element.34), channel_id=1, source_target_pairs={{0,8},{1,9},{2,10},{3,11},{4,12},{5,13},{6,14},{7,15},{8,0},{9,1},... | collective-permute-start | bytes 49160 | tf_op jit(solution)/shard_map/ppermute | solution.py:401
  33.6 3.3 %collective-permute-start.5 = (bf16[4,16,128]{2,1,0:T(8,128)(2,1)S(1)}, bf16[4,16,128]{2,1,0:T(8,128)(2,1)S(1)}, u32[]{:S(2)}, u32[]{:S(2)}) collective-permute-start(bf16[4,16,128]{2,1,0:T(8,128)(2,1)S(1)} %get-tuple-element.35), channel_id=1, source_target_pairs={{0,12},{1,13},{2,14},{3,15},{4,8},{5,9},{6,10},{7,11},{8,4},{9,5},... | collective-permute-start | bytes 49160 | tf_op jit(solution)/shard_map/ppermute | solution.py:401
  36.8 0.4 collective-permute-done.4.refs_2_
  37.2 1.9 %collective-permute-done.5.refs_3_ = bf16[4,16,128]{2,1,0:T(8,128)(2,1)S(1)} collective-permute-done((bf16[4,16,128]{2,1,0:T(8,128)(2,1)S(1)}, bf16[4,16,128]{2,1,0:T(8,128)(2,1)S(1)}, u32[]{:S(2)}, u32[]{:S(2)}) %collective-permute-start.5) | collective-permute-done | bytes 16416 | tf_op jit(solution)/shard_map/ppermute | solution.py:401
  39.1 1.2 %shard_map.61 = (bf16[4,16,128]{2,1,0:T(8,128)(2,1)S(1)}, bf16[4,16,128]{2,1,0:T(8,128)(2,1)S(1)}, bf16[4,16,128]{2,1,0:T(8,128)(2,1)S(1)}, bf16[4,16,128]{2,1,0...) custom-call(bf16[4,16,128]{2,1,0:T(8,128)(2,1)S(1)} %get-tuple-element, ...), custom_call_target="tpu_custom_call" | custom-call | tf_op jit(solution)/shard_map/pallas_call | solution.py:377
  40.3 3.8 %collective-permute-start.12 = (bf16[4,16,128]{2,1,0:T(8,128)(2,1)S(1)}, bf16[4,16,128]{2,1,0:T(8,128)(2,1)S(1)}, u32[]{:S(2)}, u32[]{:S(2)}) collective-permute-start(bf16[4,16,128]{2,1,0:T(8,128)(2,1)S(1)} %get-tuple-element.43), channel_id=1, source_target_pairs={{0,8},{1,9},{2,10},{3,11},{4,12},{5,13},{6,14},{7,15},{8,0},{9,1},... | collective-permute-start | bytes 49160 | tf_op jit(solution)/shard_map/ppermute | solution.py:401
  44.2 0.6 collective-permute-start.13
  44.7 1.2 %collective-permute-done.12.refs_2_ = bf16[4,16,128]{2,1,0:T(8,128)(2,1)S(1)} collective-permute-done((bf16[4,16,128]{2,1,0:T(8,128)(2,1)S(1)}, bf16[4,16,128]{2,1,0:T(8,128)(2,1)S(1)}, u32[]{:S(2)}, u32[]{:S(2)}) %collective-permute-start.12) | collective-permute-done | bytes 16416 | tf_op jit(solution)/shard_map/ppermute | solution.py:401
  45.9 3.8 %collective-permute-done.13.refs_3_ = bf16[4,16,128]{2,1,0:T(8,128)(2,1)S(1)} collective-permute-done((bf16[4,16,128]{2,1,0:T(8,128)(2,1)S(1)}, bf16[4,16,128]{2,1,0:T(8,128)(2,1)S(1)}, u32[]{:S(2)}, u32[]{:S(2)}) %collective-permute-start.13) | collective-permute-done | bytes 16416 | tf_op jit(solution)/shard_map/ppermute | solution.py:401
  49.7 1.4 %shard_map.62 = (bf16[16,16,128]{2,1,0:T(8,128)(2,1)}, bf16[256,128]{1,0:T(8,128)(2,1)S(1)}) custom-call(bf16[4,16,128]{2,1,0:T(8,128)(2,1)S(1)} %get-tuple-element.41.refs_0_, bf16[4,16,128]{2,1,0:T(8,128)(2,1)S(1)} %collective-permute-done.11.refs_1_, bf16[4,16,128]{2,1,0:T(8,128)(2,1)S(1)} %collective-permute-done.12.refs_2_, ...), custom_call_target="tpu_custom_call" | custom-call | tf_op jit(solution)/shard_map/pallas_call | solution.py:377
  51.1 0.1 collective-permute-start.18
  51.3 3.5 %all-to-all-start.1 = ((bf16[16,16,128]{2,1,0:T(8,128)(2,1)}), bf16[16,16,128]{2,1,0:T(8,128)(2,1)S(1)}, u32[]{:S(2)}, u32[]{:S(2)}) async-start(bf16[16,16,128]{2,1,0:T(8,128)(2,1)} %get-tuple-element.45), calls=%async_computation.1 | async-start | bytes 131072 | tf_op jit(solution)/shard_map/all_to_all | solution.py:404
  54.8 1.9 %collective-permute-start.15 = (bf16[2,64,128]{2,1,0:T(8,128)(2,1)S(1)}, bf16[2,64,128]{2,1,0:T(8,128)(2,1)S(1)}, u32[]{:S(2)}, u32[]{:S(2)}) collective-permute-start(bf16[2,64,128]{2,1,0:T(8,128)(2,1)S(1)} %get-tuple-element.48), channel_id=1, source_target_pairs={{0,2},{1,3},{2,0},{3,1},{4,6},{5,7},{6,4},{7,5},{8,10},{9,11},{10,... | collective-permute-start | bytes 98312 | tf_op jit(solution)/shard_map/ppermute | solution.py:401
  56.6 0.5 collective-permute-start.19
  57.1 1.6 %collective-permute-done.15.adj_far = bf16[2,64,128]{2,1,0:T(8,128)(2,1)S(1)} collective-permute-done((bf16[2,64,128]{2,1,0:T(8,128)(2,1)S(1)}, bf16[2,64,128]{2,1,0:T(8,128)(2,1)S(1)}, u32[]{:S(2)}, u32[]{:S(2)}) %collective-permute-start.15) | collective-permute-done | bytes 32800 | tf_op jit(solution)/shard_map/ppermute | solution.py:401
  58.8 0.5 collective-permute-start.14
  59.3 0.8 %collective-permute-done.14.adj_near = bf16[64,128]{1,0:T(8,128)(2,1)S(1)} collective-permute-done((bf16[64,128]{1,0:T(8,128)(2,1)S(1)}, bf16[64,128]{1,0:T(8,128)(2,1)S(1)}, u32[]{:S(2)}, u32[]{:S(2)}) %collective-permute-start.14) | collective-permute-done | bytes 16416 | tf_op jit(solution)/shard_map/ppermute | solution.py:401
  60.1 0.8 %shard_map.63.x = f32[2,512,256]{2,1,0:T(8,128)S(1)} custom-call(bf16[64,128]{1,0:T(8,128)(2,1)S(1)} %get-tuple-element.46.adj_own, bf16[64,128]{1,0:T(8,128)(2,1)S(1)} %collective-permute-done.14.adj_near, bf16[2,64,128]{2,1,0:T(8,128)(2,1)S(1)} %collective-permute-done.15.adj_far, ...), custom_call_target="tpu_custom_call", output_to_operand_aliasing={{}: (4, {})} | custom-call | tf_op jit(solution)/shard_map/pallas_call | solution.py:377
  60.9 0.5 shard_map.64.misfit
  61.4 0.2 all-to-all-done.1.adjoint
  61.6 1.3 %shard_map.65 = (f32[2,512,256]{2,1,0:T(8,128)}, f32[2,128,256]{2,1,0:T(8,128)}) custom-call(bf16[16,16,128]{2,1,0:T(8,128)(2,1)S(1)} %all-to-all-done.1.adjoint, f32[2,512,256]{2,1,0:T(8,128)S(1)} %shard_map.63.x, bf16[2,4,16,512]{3,2,1,0:T(8,128)(2,1)S(1)} %get-tuple-element.37.refs_5_.vfac, f32[2,128,256]{2,1,0:T(8,128)S(1)} %shard_map.64.misfit), custom_call_target="tpu_custom_call" | custom-call | tf_op jit(solution)/shard_map/pallas_call | solution.py:377
  (18 shorter events, 0.1 us)
Async XLA Ops:
  2.9 10.2 %collective-permute-start.1 = (bf16[512,256]{1,0:T(8,128)(2,1)S(1)}, bf16[512,256]{1,0:T(8,128)(2,1)S(1)}, u32[]{:S(2)}, u32[]{:S(2)}) collective-permute-start(bf16[512,256]{1,0:T(8,128)(2,1)S(1)} %get-tuple-element.31), channel_id=1, source_target_pairs={{0,2},{1,3},{2,0},{3,1},{4,6},{5,7},{6,4},{7,5},{8,10},{9,11},{10,... | collective-permute-start | bytes 786440 | tf_op jit(solution)/shard_map/ppermute | solution.py:401
  6.0 11.9 %collective-permute-start.9 = (bf16[512,256]{1,0:T(8,128)(2,1)S(1)}, bf16[512,256]{1,0:T(8,128)(2,1)S(1)}, u32[]{:S(2)}, u32[]{:S(2)}) collective-permute-start(bf16[512,256]{1,0:T(8,128)(2,1)S(1)} %get-tuple-element.40), channel_id=1, source_target_pairs={{0,2},{1,3},{2,0},{3,1},{4,6},{5,7},{6,4},{7,5},{8,10},{9,11},{10,... | collective-permute-start | bytes 786440 | tf_op jit(solution)/shard_map/ppermute | solution.py:401
  6.1 13.6 %collective-permute-start = (bf16[384,256]{1,0:T(8,128)(2,1)S(1)}, bf16[384,256]{1,0:T(8,128)(2,1)S(1)}, u32[]{:S(2)}, u32[]{:S(2)}) collective-permute-start(bf16[384,256]{1,0:T(8,128)(2,1)S(1)} %get-tuple-element.30), channel_id=1, source_target_pairs={{0,1},{1,0},{2,3},{3,2},{4,5},{5,4},{6,7},{7,6},{8,9},{9,8},{10,11... | collective-permute-start | bytes 589832 | tf_op jit(solution)/shard_map/ppermute | solution.py:401
  13.1 18.4 %collective-permute-start.2 = (bf16[512,256]{1,0:T(8,128)(2,1)S(1)}, bf16[512,256]{1,0:T(8,128)(2,1)S(1)}, u32[]{:S(2)}, u32[]{:S(2)}) collective-permute-start(bf16[512,256]{1,0:T(8,128)(2,1)S(1)} %collective-permute-done.1.far.refs_7_), channel_id=1, source_target_pairs={{0,1},{1,0},{2,3},{3,2},{4,5},{5,4},{6,7},{7,6},{8,9},{9,8},{10,11... | collective-permute-start | bytes 786440 | tf_op jit(solution)/shard_map/ppermute | solution.py:401
  13.1 23.7 %collective-permute-start.6 = (bf16[512,256]{1,0:T(8,128)(2,1)S(1)}, bf16[512,256]{1,0:T(8,128)(2,1)S(1)}, u32[]{:S(2)}, u32[]{:S(2)}) collective-permute-start(bf16[512,256]{1,0:T(8,128)(2,1)S(1)} %get-tuple-element.38), channel_id=1, source_target_pairs={{0,1},{1,0},{2,3},{3,2},{4,5},{5,4},{6,7},{7,6},{8,9},{9,8},{10,11... | collective-permute-start | bytes 786440 | tf_op jit(solution)/shard_map/ppermute | solution.py:401
  17.9 18.9 %collective-permute-start.10 = (bf16[512,256]{1,0:T(8,128)(2,1)S(1)}, bf16[512,256]{1,0:T(8,128)(2,1)S(1)}, u32[]{:S(2)}, u32[]{:S(2)}) collective-permute-start(bf16[512,256]{1,0:T(8,128)(2,1)S(1)} %collective-permute-done.9.refs_9_), channel_id=1, source_target_pairs={{0,1},{1,0},{2,3},{3,2},{4,5},{5,4},{6,7},{7,6},{8,9},{9,8},{10,11... | collective-permute-start | bytes 786440 | tf_op jit(solution)/shard_map/ppermute | solution.py:401
  17.9 14.6 %collective-permute-start.8 = (bf16[512,128]{1,0:T(8,128)(2,1)S(1)}, bf16[512,128]{1,0:T(8,128)(2,1)S(1)}, u32[]{:S(2)}, u32[]{:S(2)}) collective-permute-start(bf16[512,128]{1,0:T(8,128)(2,1)S(1)} %get-tuple-element.39), channel_id=1, source_target_pairs={{0,2},{1,3},{2,0},{3,1},{4,6},{5,7},{6,4},{7,5},{8,10},{9,11},{10,... | collective-permute-start | bytes 393224 | tf_op jit(solution)/shard_map/ppermute | solution.py:401
  19.7 13.9 %collective-permute-start.7 = (bf16[2,4,16,512]{3,2,1,0:T(8,128)(2,1)S(1)}, bf16[2,4,16,512]{3,2,1,0:T(8,128)(2,1)S(1)}, u32[]{:S(2)}, u32[]{:S(2)}) collective-permute-start(bf16[2,4,16,512]{3,2,1,0:T(8,128)(2,1)S(1)} %get-tuple-element.37.refs_5_.vfac), channel_id=1, source_target_pairs={{0,1},{1,0},{2,3},{3,2},{4,5},{5,4},{6,7},{7,6},{8,9},{9,8},{10,11... | collective-permute-start | bytes 393224 | tf_op jit(solution)/shard_map/ppermute | solution.py:401
  32.4 4.5 %collective-permute-start.3 = (bf16[4,16,128]{2,1,0:T(8,128)(2,1)S(1)}, bf16[4,16,128]{2,1,0:T(8,128)(2,1)S(1)}, u32[]{:S(2)}, u32[]{:S(2)}) collective-permute-start(bf16[4,16,128]{2,1,0:T(8,128)(2,1)S(1)} %get-tuple-element.33), channel_id=1, source_target_pairs={{0,4},{1,5},{2,6},{3,7},{4,0},{5,1},{6,2},{7,3},{8,12},{9,13},{10,... | collective-permute-start | bytes 49160 | tf_op jit(solution)/shard_map/ppermute | solution.py:401
  32.6 4.6 %collective-permute-start.4 = (bf16[4,16,128]{2,1,0:T(8,128)(2,1)S(1)}, bf16[4,16,128]{2,1,0:T(8,128)(2,1)S(1)}, u32[]{:S(2)}, u32[]{:S(2)}) collective-permute-start(bf16[4,16,128]{2,1,0:T(8,128)(2,1)S(1)} %get-tuple-element.34), channel_id=1, source_target_pairs={{0,8},{1,9},{2,10},{3,11},{4,12},{5,13},{6,14},{7,15},{8,0},{9,1},... | collective-permute-start | bytes 49160 | tf_op jit(solution)/shard_map/ppermute | solution.py:401
  33.6 5.5 %collective-permute-start.5 = (bf16[4,16,128]{2,1,0:T(8,128)(2,1)S(1)}, bf16[4,16,128]{2,1,0:T(8,128)(2,1)S(1)}, u32[]{:S(2)}, u32[]{:S(2)}) collective-permute-start(bf16[4,16,128]{2,1,0:T(8,128)(2,1)S(1)} %get-tuple-element.35), channel_id=1, source_target_pairs={{0,12},{1,13},{2,14},{3,15},{4,8},{5,9},{6,10},{7,11},{8,4},{9,5},... | collective-permute-start | bytes 49160 | tf_op jit(solution)/shard_map/ppermute | solution.py:401
  40.3 4.5 %collective-permute-start.11 = (bf16[4,16,128]{2,1,0:T(8,128)(2,1)S(1)}, bf16[4,16,128]{2,1,0:T(8,128)(2,1)S(1)}, u32[]{:S(2)}, u32[]{:S(2)}) collective-permute-start(bf16[4,16,128]{2,1,0:T(8,128)(2,1)S(1)} %get-tuple-element.42), channel_id=1, source_target_pairs={{0,4},{1,5},{2,6},{3,7},{4,0},{5,1},{6,2},{7,3},{8,12},{9,13},{10,... | collective-permute-start | bytes 49160 | tf_op jit(solution)/shard_map/ppermute | solution.py:401
  40.3 5.5 %collective-permute-start.12 = (bf16[4,16,128]{2,1,0:T(8,128)(2,1)S(1)}, bf16[4,16,128]{2,1,0:T(8,128)(2,1)S(1)}, u32[]{:S(2)}, u32[]{:S(2)}) collective-permute-start(bf16[4,16,128]{2,1,0:T(8,128)(2,1)S(1)} %get-tuple-element.43), channel_id=1, source_target_pairs={{0,8},{1,9},{2,10},{3,11},{4,12},{5,13},{6,14},{7,15},{8,0},{9,1},... | collective-permute-start | bytes 49160 | tf_op jit(solution)/shard_map/ppermute | solution.py:401
  44.2 5.5 %collective-permute-start.13 = (bf16[4,16,128]{2,1,0:T(8,128)(2,1)S(1)}, bf16[4,16,128]{2,1,0:T(8,128)(2,1)S(1)}, u32[]{:S(2)}, u32[]{:S(2)}) collective-permute-start(bf16[4,16,128]{2,1,0:T(8,128)(2,1)S(1)} %get-tuple-element.44), channel_id=1, source_target_pairs={{0,12},{1,13},{2,14},{3,15},{4,8},{5,9},{6,10},{7,11},{8,4},{9,5},... | collective-permute-start | bytes 49160 | tf_op jit(solution)/shard_map/ppermute | solution.py:401
  51.1 5.5 %collective-permute-start.18 = (bf16[256,128]{1,0:T(8,128)(2,1)S(1)}, bf16[256,128]{1,0:T(8,128)(2,1)S(1)}, u32[]{:S(2)}, u32[]{:S(2)}) collective-permute-start(bf16[256,128]{1,0:T(8,128)(2,1)S(1)} %get-tuple-element.50.own), channel_id=1, source_target_pairs={{0,2},{1,3},{2,0},{3,1},{4,6},{5,7},{6,4},{7,5},{8,10},{9,11},{10,... | collective-permute-start | bytes 196616 | tf_op jit(solution)/shard_map/ppermute | solution.py:401
  51.3 10.4 %all-to-all-start.1 = ((bf16[16,16,128]{2,1,0:T(8,128)(2,1)}), bf16[16,16,128]{2,1,0:T(8,128)(2,1)S(1)}, u32[]{:S(2)}, u32[]{:S(2)}) async-start(bf16[16,16,128]{2,1,0:T(8,128)(2,1)} %get-tuple-element.45), calls=%async_computation.1 | async-start | bytes 131072 | tf_op jit(solution)/shard_map/all_to_all | solution.py:404
  54.8 4.0 %collective-permute-start.15 = (bf16[2,64,128]{2,1,0:T(8,128)(2,1)S(1)}, bf16[2,64,128]{2,1,0:T(8,128)(2,1)S(1)}, u32[]{:S(2)}, u32[]{:S(2)}) collective-permute-start(bf16[2,64,128]{2,1,0:T(8,128)(2,1)S(1)} %get-tuple-element.48), channel_id=1, source_target_pairs={{0,2},{1,3},{2,0},{3,1},{4,6},{5,7},{6,4},{7,5},{8,10},{9,11},{10,... | collective-permute-start | bytes 98312 | tf_op jit(solution)/shard_map/ppermute | solution.py:401
  56.6 4.3 %collective-permute-start.17 = (bf16[256,128]{1,0:T(8,128)(2,1)S(1)}, bf16[256,128]{1,0:T(8,128)(2,1)S(1)}, u32[]{:S(2)}, u32[]{:S(2)}) collective-permute-start(bf16[256,128]{1,0:T(8,128)(2,1)S(1)} %get-tuple-element.50.own), channel_id=1, source_target_pairs={{0,1},{1,0},{2,3},{3,2},{4,5},{5,4},{6,7},{7,6},{8,9},{9,8},{10,11... | collective-permute-start | bytes 196616 | tf_op jit(solution)/shard_map/ppermute | solution.py:401
  56.6 4.3 %collective-permute-start.19 = (bf16[256,128]{1,0:T(8,128)(2,1)S(1)}, bf16[256,128]{1,0:T(8,128)(2,1)S(1)}, u32[]{:S(2)}, u32[]{:S(2)}) collective-permute-start(bf16[256,128]{1,0:T(8,128)(2,1)S(1)} %collective-permute-done.18.far), channel_id=1, source_target_pairs={{0,1},{1,0},{2,3},{3,2},{4,5},{5,4},{6,7},{7,6},{8,9},{9,8},{10,11... | collective-permute-start | bytes 196616 | tf_op jit(solution)/shard_map/ppermute | solution.py:401
  58.8 1.4 %collective-permute-start.16 = (bf16[2,64,128]{2,1,0:T(8,128)(2,1)S(1)}, bf16[2,64,128]{2,1,0:T(8,128)(2,1)S(1)}, u32[]{:S(2)}, u32[]{:S(2)}) collective-permute-start(bf16[2,64,128]{2,1,0:T(8,128)(2,1)S(1)} %collective-permute-done.15.adj_far), channel_id=1, source_target_pairs={{0,1},{1,0},{2,3},{3,2},{4,5},{5,4},{6,7},{7,6},{8,9},{9,8},{10,11... | collective-permute-start | bytes 98312 | tf_op jit(solution)/shard_map/ppermute | solution.py:401
  58.8 1.3 %collective-permute-start.14 = (bf16[64,128]{1,0:T(8,128)(2,1)S(1)}, bf16[64,128]{1,0:T(8,128)(2,1)S(1)}, u32[]{:S(2)}, u32[]{:S(2)}) collective-permute-start(bf16[64,128]{1,0:T(8,128)(2,1)S(1)} %get-tuple-element.47), channel_id=1, source_target_pairs={{0,1},{1,0},{2,3},{3,2},{4,5},{5,4},{6,7},{7,6},{8,9},{9,8},{10,11... | collective-permute-start | bytes 49160 | tf_op jit(solution)/shard_map/ppermute | solution.py:401

commit v9 on v8

--- a/solution.py
+++ b/solution.py
@@ -82,7 +82,7 @@
     return vfac[:, :, :, cut].reshape(parts * rows * rank, -1)
 
 
-def first_kernel(data, x, ufac, vfac, out, kept, to_far, to_near, own, u_own, x_own, v_own, *columns, group, width):
+def first_kernel(data, x, ufac, vfac, out, to_far, to_near, own, u_own, x_own, v_own, *columns, group, width):
     rows = data.shape[1]
     sources = x.shape[1]
     lanes = 2 * width
@@ -108,7 +108,6 @@
         for s, block in enumerate(slices_of(waves[0], waves[1], width)):
             scratch[jnp.bitwise_xor(q, s)] = block
         own[...] = scratch[0]
-        kept[...] = waves[...]
         for ref, base, b in ((to_near, 0, 1), (to_far, 0, 2), (to_far, step, 3)):
             high, low = split(scratch[b])
             for g in range(folds):
@@ -416,11 +415,10 @@
         shape((sources, lanes), f32),
     )
     by_columns = tile_rows == 4
-    coeffs, data, to_far, to_near, own, ufac, estimate, vfac, *columns = call(
+    coeffs, to_far, to_near, own, ufac, estimate, vfac, *columns = call(
         first_kernel,
         (
             result(chunks.shape, bf16),
-            shape(data.shape, f32),
             shape((2 * rows + 2 * step, wide), bf16),
             shape((2 * rows + step, wide), bf16),
             shape((rows, lanes), f32),

time: 63.2 us -> 63.2 us (level)
  transfers between devices with their start and end apart: 21 -> 21, of which waited for: 9 -> 8; matrix products, arithmetic and copies ran while one was open for 0% -> 0% of each run, Pallas kernels for 3% -> 3%
where the time goes in v9:
time: 63.2 us; the launch traced here: 62.9 us
  waiting for transfers between devices  21.1 us (33%)
  starting transfers between devices  21 us (33%)
  blocking collectives  11.7 us (19%)
  Pallas kernels  8.22 us (13%)
  between operations  0.72 us (1%)
    ppermute x20, waiting for transfers between devices, exchange(): return lax.ppermute(value, 'tile', [(s, s ^ bit) for s in range(tiles)])  21.1 us
    ppermute x20, starting transfers between devices, exchange(): return lax.ppermute(value, 'tile', [(s, s ^ bit) for s in range(tiles)])  17.5 us
    all_to_all x1, blocking collectives, spread(): lax.all_to_all(value, 'tile', split_axis=0, concat_axis=0, tiled=True)  11.7 us
    pallas_call x7, Pallas kernels, call(): pl.pallas_call(functools.partial(kernel, **static), out_shape=out_shape,...  8.22 us
    all_to_all x1, starting transfers between devices, spread(): lax.all_to_all(value, 'tile', split_axis=0, concat_axis=0, tiled=True)  3.5 us
  transfers between devices with their start and end apart: 21, of which 8 were waited for; matrix products, arithmetic and copies ran while one was open for 0% of the time, Pallas kernels for 3%

profile of v9, /device:TPU:0, one launch (start us, length us, event | category | flops | bytes accessed | tf_op | source)
XLA Modules:
  0.0 62.9 jit_solution(5928784876060643812)
XLA Ops:
  0.6 2.3 %shard_map.59 = (bf16[16,16,128]{2,1,0:T(8,128)(2,1)S(1)}, bf16[512,256]{1,0:T(8,128)(2,1)S(1)}, bf16[384,256]{1,0:T(8,128)(2,1)S(1)}, f32[128,128]{1,0:T(8,128)...) custom-call(f32[2,128,256]{2,1,0:T(8,128)} %data.3, ...), custom_call_target="tpu_custom_call" | custom-call | tf_op jit(solution)/shard_map/pallas_call | solution.py:376
  2.9 3.1 %collective-permute-start.1 = (bf16[512,256]{1,0:T(8,128)(2,1)S(1)}, bf16[512,256]{1,0:T(8,128)(2,1)S(1)}, u32[]{:S(2)}, u32[]{:S(2)}) collective-permute-start(bf16[512,256]{1,0:T(8,128)(2,1)S(1)} %get-tuple-element.30), channel_id=1, source_target_pairs={{0,2},{1,3},{2,0},{3,1},{4,6},{5,7},{6,4},{7,5},{8,10},{9,11},{10,... | collective-permute-start | bytes 786440 | tf_op jit(solution)/shard_map/ppermute | solution.py:400
  6.0 0.1 collective-permute-start.9
  6.1 7.1 %collective-permute-done.1.far.refs_7_ = bf16[512,256]{1,0:T(8,128)(2,1)S(1)} collective-permute-done((bf16[512,256]{1,0:T(8,128)(2,1)S(1)}, bf16[512,256]{1,0:T(8,128)(2,1)S(1)}, u32[]{:S(2)}, u32[]{:S(2)}) %collective-permute-start.1) | collective-permute-done | bytes 262176 | tf_op jit(solution)/shard_map/ppermute | solution.py:400
  13.1 0.5 collective-permute-start.6
  13.6 4.3 %collective-permute-done.9.refs_9_ = bf16[512,256]{1,0:T(8,128)(2,1)S(1)} collective-permute-done((bf16[512,256]{1,0:T(8,128)(2,1)S(1)}, bf16[512,256]{1,0:T(8,128)(2,1)S(1)}, u32[]{:S(2)}, u32[]{:S(2)}) %collective-permute-start.9) | collective-permute-done | bytes 262176 | tf_op jit(solution)/shard_map/ppermute | solution.py:400
  17.9 1.7 %collective-permute-start.8 = (bf16[512,128]{1,0:T(8,128)(2,1)S(1)}, bf16[512,128]{1,0:T(8,128)(2,1)S(1)}, u32[]{:S(2)}, u32[]{:S(2)}) collective-permute-start(bf16[512,128]{1,0:T(8,128)(2,1)S(1)} %get-tuple-element.38), channel_id=1, source_target_pairs={{0,2},{1,3},{2,0},{3,1},{4,6},{5,7},{6,4},{7,5},{8,10},{9,11},{10,... | collective-permute-start | bytes 393224 | tf_op jit(solution)/shard_map/ppermute | solution.py:400
  19.6 0.2 collective-permute-start.7
  19.9 11.7 %all_to_all.10.coeffs = bf16[16,16,128]{2,1,0:T(8,128)(2,1)S(1)} all-to-all(bf16[16,16,128]{2,1,0:T(8,128)(2,1)S(1)} %get-tuple-element.26), channel_id=1, replica_groups=mesh['freq'=2,'tile'=16] {'tile'}, dimensions={0} | all-to-all | bytes 131072 | tf_op jit(solution)/shard_map/all_to_all | solution.py:403
  31.5 0.8 %shard_map.60 = (bf16[4,16,128]{2,1,0:T(8,128)(2,1)S(1)}, bf16[4,16,128]{2,1,0:T(8,128)(2,1)S(1)}, bf16[4,16,128]{2,1,0:T(8,128)(2,1)S(1)}, bf16[4,16,128]{2,1,0:T(8,128)(2,1)S(1)}) custom-call(bf16[16,16,128]{2,1,0:T(8,128)(2,1)S(1)} %all_to_all.10.coeffs, f32[128,128]{1,0:T(8,128)S(1)} %get-tuple-element.27.own.refs_4_, ...), custom_call_target="tpu_custom_call" | custom-call | tf_op jit(solution)/shard_map/pallas_call | solution.py:376
  32.4 0.2 collective-permute-start.3
  32.5 1.0 %collective-permute-start.4 = (bf16[4,16,128]{2,1,0:T(8,128)(2,1)S(1)}, bf16[4,16,128]{2,1,0:T(8,128)(2,1)S(1)}, u32[]{:S(2)}, u32[]{:S(2)}) collective-permute-start(bf16[4,16,128]{2,1,0:T(8,128)(2,1)S(1)} %get-tuple-element.33), channel_id=1, source_target_pairs={{0,8},{1,9},{2,10},{3,11},{4,12},{5,13},{6,14},{7,15},{8,0},{9,1},... | collective-permute-start | bytes 49160 | tf_op jit(solution)/shard_map/ppermute | solution.py:400
  33.5 3.3 %collective-permute-start.5 = (bf16[4,16,128]{2,1,0:T(8,128)(2,1)S(1)}, bf16[4,16,128]{2,1,0:T(8,128)(2,1)S(1)}, u32[]{:S(2)}, u32[]{:S(2)}) collective-permute-start(bf16[4,16,128]{2,1,0:T(8,128)(2,1)S(1)} %get-tuple-element.34), channel_id=1, source_target_pairs={{0,12},{1,13},{2,14},{3,15},{4,8},{5,9},{6,10},{7,11},{8,4},{9,5},... | collective-permute-start | bytes 49160 | tf_op jit(solution)/shard_map/ppermute | solution.py:400
  36.8 0.4 collective-permute-done.4.refs_2_
  37.2 1.9 %collective-permute-done.5.refs_3_ = bf16[4,16,128]{2,1,0:T(8,128)(2,1)S(1)} collective-permute-done((bf16[4,16,128]{2,1,0:T(8,128)(2,1)S(1)}, bf16[4,16,128]{2,1,0:T(8,128)(2,1)S(1)}, u32[]{:S(2)}, u32[]{:S(2)}) %collective-permute-start.5) | collective-permute-done | bytes 16416 | tf_op jit(solution)/shard_map/ppermute | solution.py:400
  39.1 1.2 %shard_map.61 = (bf16[4,16,128]{2,1,0:T(8,128)(2,1)S(1)}, bf16[4,16,128]{2,1,0:T(8,128)(2,1)S(1)}, bf16[4,16,128]{2,1,0:T(8,128)(2,1)S(1)}, bf16[4,16,128]{2,1,0...) custom-call(bf16[4,16,128]{2,1,0:T(8,128)(2,1)S(1)} %get-tuple-element, ...), custom_call_target="tpu_custom_call" | custom-call | tf_op jit(solution)/shard_map/pallas_call | solution.py:376
  40.3 3.8 %collective-permute-start.12 = (bf16[4,16,128]{2,1,0:T(8,128)(2,1)S(1)}, bf16[4,16,128]{2,1,0:T(8,128)(2,1)S(1)}, u32[]{:S(2)}, u32[]{:S(2)}) collective-permute-start(bf16[4,16,128]{2,1,0:T(8,128)(2,1)S(1)} %get-tuple-element.42), channel_id=1, source_target_pairs={{0,8},{1,9},{2,10},{3,11},{4,12},{5,13},{6,14},{7,15},{8,0},{9,1},... | collective-permute-start | bytes 49160 | tf_op jit(solution)/shard_map/ppermute | solution.py:400
  44.2 0.6 collective-permute-start.13
  44.7 1.2 %collective-permute-done.12.refs_2_ = bf16[4,16,128]{2,1,0:T(8,128)(2,1)S(1)} collective-permute-done((bf16[4,16,128]{2,1,0:T(8,128)(2,1)S(1)}, bf16[4,16,128]{2,1,0:T(8,128)(2,1)S(1)}, u32[]{:S(2)}, u32[]{:S(2)}) %collective-permute-start.12) | collective-permute-done | bytes 16416 | tf_op jit(solution)/shard_map/ppermute | solution.py:400
  45.9 3.8 %collective-permute-done.13.refs_3_ = bf16[4,16,128]{2,1,0:T(8,128)(2,1)S(1)} collective-permute-done((bf16[4,16,128]{2,1,0:T(8,128)(2,1)S(1)}, bf16[4,16,128]{2,1,0:T(8,128)(2,1)S(1)}, u32[]{:S(2)}, u32[]{:S(2)}) %collective-permute-start.13) | collective-permute-done | bytes 16416 | tf_op jit(solution)/shard_map/ppermute | solution.py:400
  49.7 1.4 %shard_map.62 = (bf16[16,16,128]{2,1,0:T(8,128)(2,1)}, bf16[256,128]{1,0:T(8,128)(2,1)S(1)}) custom-call(bf16[4,16,128]{2,1,0:T(8,128)(2,1)S(1)} %get-tuple-element.40.refs_0_, bf16[4,16,128]{2,1,0:T(8,128)(2,1)S(1)} %collective-permute-done.11.refs_1_, bf16[4,16,128]{2,1,0:T(8,128)(2,1)S(1)} %collective-permute-done.12.refs_2_, ...), custom_call_target="tpu_custom_call" | custom-call | tf_op jit(solution)/shard_map/pallas_call | solution.py:376
  51.1 0.1 collective-permute-start.18
  51.2 3.5 %all-to-all-start.1 = ((bf16[16,16,128]{2,1,0:T(8,128)(2,1)}), bf16[16,16,128]{2,1,0:T(8,128)(2,1)S(1)}, u32[]{:S(2)}, u32[]{:S(2)}) async-start(bf16[16,16,128]{2,1,0:T(8,128)(2,1)} %get-tuple-element.44), calls=%async_computation.1 | async-start | bytes 131072 | tf_op jit(solution)/shard_map/all_to_all | solution.py:403
  54.8 1.9 %collective-permute-start.15 = (bf16[2,64,128]{2,1,0:T(8,128)(2,1)S(1)}, bf16[2,64,128]{2,1,0:T(8,128)(2,1)S(1)}, u32[]{:S(2)}, u32[]{:S(2)}) collective-permute-start(bf16[2,64,128]{2,1,0:T(8,128)(2,1)S(1)} %get-tuple-element.47), channel_id=1, source_target_pairs={{0,2},{1,3},{2,0},{3,1},{4,6},{5,7},{6,4},{7,5},{8,10},{9,11},{10,... | collective-permute-start | bytes 98312 | tf_op jit(solution)/shard_map/ppermute | solution.py:400
  56.6 0.5 collective-permute-start.19
  57.1 1.6 %collective-permute-done.15.adj_far = bf16[2,64,128]{2,1,0:T(8,128)(2,1)S(1)} collective-permute-done((bf16[2,64,128]{2,1,0:T(8,128)(2,1)S(1)}, bf16[2,64,128]{2,1,0:T(8,128)(2,1)S(1)}, u32[]{:S(2)}, u32[]{:S(2)}) %collective-permute-start.15) | collective-permute-done | bytes 32800 | tf_op jit(solution)/shard_map/ppermute | solution.py:400
  58.8 0.5 collective-permute-start.14
  59.3 0.8 %collective-permute-done.14.adj_near = bf16[64,128]{1,0:T(8,128)(2,1)S(1)} collective-permute-done((bf16[64,128]{1,0:T(8,128)(2,1)S(1)}, bf16[64,128]{1,0:T(8,128)(2,1)S(1)}, u32[]{:S(2)}, u32[]{:S(2)}) %collective-permute-start.14) | collective-permute-done | bytes 16416 | tf_op jit(solution)/shard_map/ppermute | solution.py:400
  60.1 0.8 %shard_map.63.x = f32[2,512,256]{2,1,0:T(8,128)S(1)} custom-call(bf16[64,128]{1,0:T(8,128)(2,1)S(1)} %get-tuple-element.45.adj_own, bf16[64,128]{1,0:T(8,128)(2,1)S(1)} %collective-permute-done.14.adj_near, bf16[2,64,128]{2,1,0:T(8,128)(2,1)S(1)} %collective-permute-done.15.adj_far, ...), custom_call_target="tpu_custom_call", output_to_operand_aliasing={{}: (4, {})} | custom-call | tf_op jit(solution)/shard_map/pallas_call | solution.py:376
  60.9 0.2 copy-done
  61.1 0.5 shard_map.64.misfit
  61.6 1.3 %shard_map.65 = (f32[2,512,256]{2,1,0:T(8,128)}, f32[2,128,256]{2,1,0:T(8,128)}) custom-call(bf16[16,16,128]{2,1,0:T(8,128)(2,1)S(1)} %all-to-all-done.1.adjoint, f32[2,512,256]{2,1,0:T(8,128)S(1)} %shard_map.63.x, bf16[2,4,16,512]{3,2,1,0:T(8,128)(2,1)S(1)} %get-tuple-element.36.refs_5_.vfac, f32[2,128,256]{2,1,0:T(8,128)S(1)} %shard_map.64.misfit), custom_call_target="tpu_custom_call" | custom-call | tf_op jit(solution)/shard_map/pallas_call | solution.py:376
  (20 shorter events, 0.2 us)
Async XLA Ops:
  2.9 10.2 %collective-permute-start.1 = (bf16[512,256]{1,0:T(8,128)(2,1)S(1)}, bf16[512,256]{1,0:T(8,128)(2,1)S(1)}, u32[]{:S(2)}, u32[]{:S(2)}) collective-permute-start(bf16[512,256]{1,0:T(8,128)(2,1)S(1)} %get-tuple-element.30), channel_id=1, source_target_pairs={{0,2},{1,3},{2,0},{3,1},{4,6},{5,7},{6,4},{7,5},{8,10},{9,11},{10,... | collective-permute-start | bytes 786440 | tf_op jit(solution)/shard_map/ppermute | solution.py:400
  6.0 11.9 %collective-permute-start.9 = (bf16[512,256]{1,0:T(8,128)(2,1)S(1)}, bf16[512,256]{1,0:T(8,128)(2,1)S(1)}, u32[]{:S(2)}, u32[]{:S(2)}) collective-permute-start(bf16[512,256]{1,0:T(8,128)(2,1)S(1)} %get-tuple-element.39), channel_id=1, source_target_pairs={{0,2},{1,3},{2,0},{3,1},{4,6},{5,7},{6,4},{7,5},{8,10},{9,11},{10,... | collective-permute-start | bytes 786440 | tf_op jit(solution)/shard_map/ppermute | solution.py:400
  6.1 13.6 %collective-permute-start = (bf16[384,256]{1,0:T(8,128)(2,1)S(1)}, bf16[384,256]{1,0:T(8,128)(2,1)S(1)}, u32[]{:S(2)}, u32[]{:S(2)}) collective-permute-start(bf16[384,256]{1,0:T(8,128)(2,1)S(1)} %get-tuple-element.29), channel_id=1, source_target_pairs={{0,1},{1,0},{2,3},{3,2},{4,5},{5,4},{6,7},{7,6},{8,9},{9,8},{10,11... | collective-permute-start | bytes 589832 | tf_op jit(solution)/shard_map/ppermute | solution.py:400
  13.1 18.4 %collective-permute-start.2 = (bf16[512,256]{1,0:T(8,128)(2,1)S(1)}, bf16[512,256]{1,0:T(8,128)(2,1)S(1)}, u32[]{:S(2)}, u32[]{:S(2)}) collective-permute-start(bf16[512,256]{1,0:T(8,128)(2,1)S(1)} %collective-permute-done.1.far.refs_7_), channel_id=1, source_target_pairs={{0,1},{1,0},{2,3},{3,2},{4,5},{5,4},{6,7},{7,6},{8,9},{9,8},{10,11... | collective-permute-start | bytes 786440 | tf_op jit(solution)/shard_map/ppermute | solution.py:400
  13.1 23.7 %collective-permute-start.6 = (bf16[512,256]{1,0:T(8,128)(2,1)S(1)}, bf16[512,256]{1,0:T(8,128)(2,1)S(1)}, u32[]{:S(2)}, u32[]{:S(2)}) collective-permute-start(bf16[512,256]{1,0:T(8,128)(2,1)S(1)} %get-tuple-element.37), channel_id=1, source_target_pairs={{0,1},{1,0},{2,3},{3,2},{4,5},{5,4},{6,7},{7,6},{8,9},{9,8},{10,11... | collective-permute-start | bytes 786440 | tf_op jit(solution)/shard_map/ppermute | solution.py:400
  17.9 18.9 %collective-permute-start.10 = (bf16[512,256]{1,0:T(8,128)(2,1)S(1)}, bf16[512,256]{1,0:T(8,128)(2,1)S(1)}, u32[]{:S(2)}, u32[]{:S(2)}) collective-permute-start(bf16[512,256]{1,0:T(8,128)(2,1)S(1)} %collective-permute-done.9.refs_9_), channel_id=1, source_target_pairs={{0,1},{1,0},{2,3},{3,2},{4,5},{5,4},{6,7},{7,6},{8,9},{9,8},{10,11... | collective-permute-start | bytes 786440 | tf_op jit(solution)/shard_map/ppermute | solution.py:400
  17.9 14.6 %collective-permute-start.8 = (bf16[512,128]{1,0:T(8,128)(2,1)S(1)}, bf16[512,128]{1,0:T(8,128)(2,1)S(1)}, u32[]{:S(2)}, u32[]{:S(2)}) collective-permute-start(bf16[512,128]{1,0:T(8,128)(2,1)S(1)} %get-tuple-element.38), channel_id=1, source_target_pairs={{0,2},{1,3},{2,0},{3,1},{4,6},{5,7},{6,4},{7,5},{8,10},{9,11},{10,... | collective-permute-start | bytes 393224 | tf_op jit(solution)/shard_map/ppermute | solution.py:400
  19.6 13.9 %collective-permute-start.7 = (bf16[2,4,16,512]{3,2,1,0:T(8,128)(2,1)S(1)}, bf16[2,4,16,512]{3,2,1,0:T(8,128)(2,1)S(1)}, u32[]{:S(2)}, u32[]{:S(2)}) collective-permute-start(bf16[2,4,16,512]{3,2,1,0:T(8,128)(2,1)S(1)} %get-tuple-element.36.refs_5_.vfac), channel_id=1, source_target_pairs={{0,1},{1,0},{2,3},{3,2},{4,5},{5,4},{6,7},{7,6},{8,9},{9,8},{10,11... | collective-permute-start | bytes 393224 | tf_op jit(solution)/shard_map/ppermute | solution.py:400
  32.4 4.5 %collective-permute-start.3 = (bf16[4,16,128]{2,1,0:T(8,128)(2,1)S(1)}, bf16[4,16,128]{2,1,0:T(8,128)(2,1)S(1)}, u32[]{:S(2)}, u32[]{:S(2)}) collective-permute-start(bf16[4,16,128]{2,1,0:T(8,128)(2,1)S(1)} %get-tuple-element.32), channel_id=1, source_target_pairs={{0,4},{1,5},{2,6},{3,7},{4,0},{5,1},{6,2},{7,3},{8,12},{9,13},{10,... | collective-permute-start | bytes 49160 | tf_op jit(solution)/shard_map/ppermute | solution.py:400
  32.5 4.6 %collective-permute-start.4 = (bf16[4,16,128]{2,1,0:T(8,128)(2,1)S(1)}, bf16[4,16,128]{2,1,0:T(8,128)(2,1)S(1)}, u32[]{:S(2)}, u32[]{:S(2)}) collective-permute-start(bf16[4,16,128]{2,1,0:T(8,128)(2,1)S(1)} %get-tuple-element.33), channel_id=1, source_target_pairs={{0,8},{1,9},{2,10},{3,11},{4,12},{5,13},{6,14},{7,15},{8,0},{9,1},... | collective-permute-start | bytes 49160 | tf_op jit(solution)/shard_map/ppermute | solution.py:400
  33.5 5.5 %collective-permute-start.5 = (bf16[4,16,128]{2,1,0:T(8,128)(2,1)S(1)}, bf16[4,16,128]{2,1,0:T(8,128)(2,1)S(1)}, u32[]{:S(2)}, u32[]{:S(2)}) collective-permute-start(bf16[4,16,128]{2,1,0:T(8,128)(2,1)S(1)} %get-tuple-element.34), channel_id=1, source_target_pairs={{0,12},{1,13},{2,14},{3,15},{4,8},{5,9},{6,10},{7,11},{8,4},{9,5},... | collective-permute-start | bytes 49160 | tf_op jit(solution)/shard_map/ppermute | solution.py:400
  40.3 4.5 %collective-permute-start.11 = (bf16[4,16,128]{2,1,0:T(8,128)(2,1)S(1)}, bf16[4,16,128]{2,1,0:T(8,128)(2,1)S(1)}, u32[]{:S(2)}, u32[]{:S(2)}) collective-permute-start(bf16[4,16,128]{2,1,0:T(8,128)(2,1)S(1)} %get-tuple-element.41), channel_id=1, source_target_pairs={{0,4},{1,5},{2,6},{3,7},{4,0},{5,1},{6,2},{7,3},{8,12},{9,13},{10,... | collective-permute-start | bytes 49160 | tf_op jit(solution)/shard_map/ppermute | solution.py:400
  40.3 5.5 %collective-permute-start.12 = (bf16[4,16,128]{2,1,0:T(8,128)(2,1)S(1)}, bf16[4,16,128]{2,1,0:T(8,128)(2,1)S(1)}, u32[]{:S(2)}, u32[]{:S(2)}) collective-permute-start(bf16[4,16,128]{2,1,0:T(8,128)(2,1)S(1)} %get-tuple-element.42), channel_id=1, source_target_pairs={{0,8},{1,9},{2,10},{3,11},{4,12},{5,13},{6,14},{7,15},{8,0},{9,1},... | collective-permute-start | bytes 49160 | tf_op jit(solution)/shard_map/ppermute | solution.py:400
  44.2 5.5 %collective-permute-start.13 = (bf16[4,16,128]{2,1,0:T(8,128)(2,1)S(1)}, bf16[4,16,128]{2,1,0:T(8,128)(2,1)S(1)}, u32[]{:S(2)}, u32[]{:S(2)}) collective-permute-start(bf16[4,16,128]{2,1,0:T(8,128)(2,1)S(1)} %get-tuple-element.43), channel_id=1, source_target_pairs={{0,12},{1,13},{2,14},{3,15},{4,8},{5,9},{6,10},{7,11},{8,4},{9,5},... | collective-permute-start | bytes 49160 | tf_op jit(solution)/shard_map/ppermute | solution.py:400
  51.1 5.5 %collective-permute-start.18 = (bf16[256,128]{1,0:T(8,128)(2,1)S(1)}, bf16[256,128]{1,0:T(8,128)(2,1)S(1)}, u32[]{:S(2)}, u32[]{:S(2)}) collective-permute-start(bf16[256,128]{1,0:T(8,128)(2,1)S(1)} %get-tuple-element.49.own), channel_id=1, source_target_pairs={{0,2},{1,3},{2,0},{3,1},{4,6},{5,7},{6,4},{7,5},{8,10},{9,11},{10,... | collective-permute-start | bytes 196616 | tf_op jit(solution)/shard_map/ppermute | solution.py:400
  51.2 10.4 %all-to-all-start.1 = ((bf16[16,16,128]{2,1,0:T(8,128)(2,1)}), bf16[16,16,128]{2,1,0:T(8,128)(2,1)S(1)}, u32[]{:S(2)}, u32[]{:S(2)}) async-start(bf16[16,16,128]{2,1,0:T(8,128)(2,1)} %get-tuple-element.44), calls=%async_computation.1 | async-start | bytes 131072 | tf_op jit(solution)/shard_map/all_to_all | solution.py:403
  54.8 4.0 %collective-permute-start.15 = (bf16[2,64,128]{2,1,0:T(8,128)(2,1)S(1)}, bf16[2,64,128]{2,1,0:T(8,128)(2,1)S(1)}, u32[]{:S(2)}, u32[]{:S(2)}) collective-permute-start(bf16[2,64,128]{2,1,0:T(8,128)(2,1)S(1)} %get-tuple-element.47), channel_id=1, source_target_pairs={{0,2},{1,3},{2,0},{3,1},{4,6},{5,7},{6,4},{7,5},{8,10},{9,11},{10,... | collective-permute-start | bytes 98312 | tf_op jit(solution)/shard_map/ppermute | solution.py:400
  56.6 4.3 %collective-permute-start.17 = (bf16[256,128]{1,0:T(8,128)(2,1)S(1)}, bf16[256,128]{1,0:T(8,128)(2,1)S(1)}, u32[]{:S(2)}, u32[]{:S(2)}) collective-permute-start(bf16[256,128]{1,0:T(8,128)(2,1)S(1)} %get-tuple-element.49.own), channel_id=1, source_target_pairs={{0,1},{1,0},{2,3},{3,2},{4,5},{5,4},{6,7},{7,6},{8,9},{9,8},{10,11... | collective-permute-start | bytes 196616 | tf_op jit(solution)/shard_map/ppermute | solution.py:400
  56.6 4.3 %collective-permute-start.19 = (bf16[256,128]{1,0:T(8,128)(2,1)S(1)}, bf16[256,128]{1,0:T(8,128)(2,1)S(1)}, u32[]{:S(2)}, u32[]{:S(2)}) collective-permute-start(bf16[256,128]{1,0:T(8,128)(2,1)S(1)} %collective-permute-done.18.far), channel_id=1, source_target_pairs={{0,1},{1,0},{2,3},{3,2},{4,5},{5,4},{6,7},{7,6},{8,9},{9,8},{10,11... | collective-permute-start | bytes 196616 | tf_op jit(solution)/shard_map/ppermute | solution.py:400
  58.8 1.4 %collective-permute-start.16 = (bf16[2,64,128]{2,1,0:T(8,128)(2,1)S(1)}, bf16[2,64,128]{2,1,0:T(8,128)(2,1)S(1)}, u32[]{:S(2)}, u32[]{:S(2)}) collective-permute-start(bf16[2,64,128]{2,1,0:T(8,128)(2,1)S(1)} %collective-permute-done.15.adj_far), channel_id=1, source_target_pairs={{0,1},{1,0},{2,3},{3,2},{4,5},{5,4},{6,7},{7,6},{8,9},{9,8},{10,11... | collective-permute-start | bytes 98312 | tf_op jit(solution)/shard_map/ppermute | solution.py:400
  58.8 1.3 %collective-permute-start.14 = (bf16[64,128]{1,0:T(8,128)(2,1)S(1)}, bf16[64,128]{1,0:T(8,128)(2,1)S(1)}, u32[]{:S(2)}, u32[]{:S(2)}) collective-permute-start(bf16[64,128]{1,0:T(8,128)(2,1)S(1)} %get-tuple-element.46), channel_id=1, source_target_pairs={{0,1},{1,0},{2,3},{3,2},{4,5},{5,4},{6,7},{7,6},{8,9},{9,8},{10,11... | collective-permute-start | bytes 49160 | tf_op jit(solution)/shard_map/ppermute | solution.py:400
  60.1 1.0 %copy-start = (f32[2,128,256]{2,1,0:T(8,128)S(1)}, f32[2,128,256]{2,1,0:T(8,128)}, u32[]{:S(2)}) copy-start(f32[2,128,256]{2,1,0:T(8,128)} %data.3) | copy-start | bytes 786436

commit v10 on v9

--- a/solution.py
+++ b/solution.py
@@ -82,6 +82,13 @@
     return vfac[:, :, :, cut].reshape(parts * rows * rank, -1)
 
 
+def half_blocks(x, which, parity, lanes):
+    cut = pl.ds(pl.multiple_of(which * lanes, lanes), lanes)
+    even, odd = interleave(x[0, :, cut], x[1, :, cut])
+    first = jnp.broadcast_to(parity, even.shape) == 0
+    return jnp.where(first, even, odd), jnp.where(first, odd, even)
+
+
 def first_kernel(data, x, ufac, vfac, out, to_far, to_near, own, u_own, x_own, v_own, *columns, group, width):
     rows = data.shape[1]
     sources = x.shape[1]
@@ -90,7 +97,7 @@
     step = rows // folds
     q = group_index(group)
 
-    def run(stage, waves, scratch, quarters, sems):
+    def run(stage, waves, scratch, sems):
         x_copy = pltpu.make_async_copy(x, x_own, sems.at[0])
         v_copy = pltpu.make_async_copy(vfac, v_own, sems.at[1])
         wave_copy = pltpu.make_async_copy(data, waves, sems.at[2])
@@ -120,18 +127,18 @@
             to_near[step + rows * part:step + rows * (part + 1)] = u_own[part]
             to_far[2 * step + rows * part:2 * step + rows * (part + 1)] = u_own[part]
         if columns:
-            shared_x, far_x, near_x, block_x = columns
+            shared_x, far_x, near_x = columns
             tall = 2 * v_own.shape[1] * v_own.shape[2]
-            for s, block in enumerate(slices_of(x_own[0], x_own[1], width)):
-                quarters[jnp.bitwise_xor(q, s)] = block
-            block_x[...] = quarters[0]
-            high, low = split(quarters[1])
+            side, parity = lax.div(q, 2), lax.rem(q, 2)
+            same, other = half_blocks(x_own, 1 - side, parity, lanes)
+            far_x[...] = same.astype(bf16)
+            half = sources // 2
+            shared_x[:half, :lanes] = other[:half].astype(bf16)
+            shared_x[:half, lanes:] = other[half:].astype(bf16)
+            _, other = half_blocks(x_own, side, parity, lanes)
+            high, low = split(other)
             near_x[:, :lanes] = high
             near_x[:, lanes:] = low
-            far_x[...] = quarters[2].astype(bf16)
-            half = sources // 2
-            shared_x[:half, :lanes] = quarters[3, :half].astype(bf16)
-            shared_x[:half, lanes:] = quarters[3, half:].astype(bf16)
             for h in range(sources // (2 * lanes)):
                 cut = slice(h * 2 * lanes, (h + 1) * 2 * lanes)
                 shared_x[half + h * tall:half + (h + 1) * tall] = flat_factors(v_own, cut)
@@ -142,7 +149,6 @@
         pltpu.VMEM(out.shape, bf16),
         pltpu.VMEM(data.shape, f32),
         pltpu.VMEM((group, rows, lanes), f32),
-        pltpu.VMEM((group, sources, lanes), f32),
         pltpu.SemaphoreType.DMA((5,)),
     )
 
@@ -171,7 +177,7 @@
     total = None
     for wave, (ur, ui) in blocks:
         misfit = wave - (dot(ur, c) + dot(ui, ci))
-        mt = misfit.T.astype(bf16)
+        mt = misfit.astype(bf16).T
         mr, mi = mt[:width], mt[width:]
         turned = jnp.concatenate([mi, -mr], axis=0)
         term = dot(mt, ur) + dot(turned, ui)
@@ -225,7 +231,7 @@
     outs, (adj_own, adj_near, adj_far) = refs[:count], refs[count:]
     q = group_index(group)
     z = row_index(group)
-    sources, lanes = x_own.shape
+    sources, lanes = near.shape[0], near.shape[1] // 2
     rank = pieces[0].shape[1]
     side = count * rank
     tall = 2 * side
@@ -243,7 +249,7 @@
                 adj[k, jnp.bitwise_xor(z, b)] = piece[jnp.bitwise_xor(q, k)]
         exact = near[...].astype(f32)
         columns = (
-            (x_own[...], flat_factors(v_own)),
+            (half_blocks(x_own, lax.div(q, 2), lax.rem(q, 2), lanes)[0], flat_factors(v_own)),
             (exact[:, :lanes] + exact[:, lanes:], flat_factors(v_near)),
             (far[...].astype(f32), factors(shared)),
             (
@@ -262,8 +268,7 @@
             turned = times_i(a.astype(f32)).astype(bf16)
             s = x + STEP * dot(vcat, jnp.concatenate([a, turned], axis=0), ((0,), (0,)))
             square = s * s
-            magnitude = jnp.sqrt(square + swap_halves(square))
-            factor = jnp.maximum(magnitude - THRESHOLD, 0.0) / jnp.maximum(magnitude, THRESHOLD)
+            factor = shrink_factor(square + swap_halves(square))
             t = dot(vcat, (s * factor).astype(bf16))
             c = (t[:side] - times_i(t[side:])).astype(bf16)
             for i in range(count):
@@ -308,9 +313,12 @@
     return sides_of([a[:, s].reshape(rows * rank, lanes) for s in range(group)])
 
 
+def shrink_factor(square):
+    return jnp.where(square > THRESHOLD * THRESHOLD, 1.0 - THRESHOLD * lax.rsqrt(square), 0.0)
+
+
 def shrink(sr, si):
-    magnitude = jnp.sqrt(sr * sr + si * si)
-    factor = jnp.maximum(magnitude - THRESHOLD, 0.0) / jnp.maximum(magnitude, THRESHOLD)
+    factor = shrink_factor(sr * sr + si * si)
     return sr * factor, si * factor
 
 
@@ -412,7 +420,6 @@
         shape((sources // 2 + tall * sources // (2 * lanes), 2 * lanes), bf16),
         shape((sources, lanes), bf16),
         shape((sources, 2 * lanes), bf16),
-        shape((sources, lanes), f32),
     )
     by_columns = tile_rows == 4
     coeffs, to_far, to_near, own, ufac, estimate, vfac, *columns = call(
@@ -443,7 +450,7 @@
             order = {b: exchange(pieces[b], b * group) for b in range(tile_rows - 1, 0, -1)}
             return [pieces[0]] + [order[b] for b in range(1, tile_rows)]
 
-        x_shared, x_far, x_near, x_own = columns
+        x_shared, x_far, x_near = columns
         x_shared = exchange(x_shared, 2)
         x_far = exchange(x_far, 2)
         x_near = exchange(x_near, 1)
@@ -454,7 +461,7 @@
         *pieces, adj_own, adj_near, adj_far = call(
             middle_columns_kernel,
             (piece,) * tile_rows + (shape(side, bf16), shape(side, bf16), shape((2,) + side, bf16)),
-            *pieces, x_own, vfac, x_near, v_near, x_far, x_shared, x_corner, **counted,
+            *pieces, estimate, vfac, x_near, v_near, x_far, x_shared, x_corner, **counted,
         )
         pieces = along_rows(pieces)
         adj_far = exchange(adj_far, 2)

time: 63.2 us -> 62.9 us (level)
  no operation moved by 1% of the time
where the time goes in v10:
time: 62.9 us; the launch traced here: 62.6 us
  waiting for transfers between devices  21.1 us (34%)
  starting transfers between devices  21 us (33%)
  blocking collectives  11.7 us (19%)
  Pallas kernels  7.84 us (12%)
  between operations  0.72 us (1%)
    ppermute x20, waiting for transfers between devices, exchange(): return lax.ppermute(value, 'tile', [(s, s ^ bit) for s in range(tiles)])  21.1 us
    ppermute x20, starting transfers between devices, exchange(): return lax.ppermute(value, 'tile', [(s, s ^ bit) for s in range(tiles)])  17.5 us
    all_to_all x1, blocking collectives, spread(): lax.all_to_all(value, 'tile', split_axis=0, concat_axis=0, tiled=True)  11.7 us
    pallas_call x7, Pallas kernels, call(): pl.pallas_call(functools.partial(kernel, **static), out_shape=out_shape,...  7.84 us
    all_to_all x1, starting transfers between devices, spread(): lax.all_to_all(value, 'tile', split_axis=0, concat_axis=0, tiled=True)  3.5 us
  transfers between devices with their start and end apart: 21, of which 8 were waited for; matrix products, arithmetic and copies ran while one was open for 0% of the time, Pallas kernels for 3%

profile of v10, /device:TPU:0, one launch (start us, length us, event | category | flops | bytes accessed | tf_op | source)
XLA Modules:
  0.0 62.6 jit_solution(2245208754669193354)
XLA Ops:
  0.6 2.1 %shard_map.59 = (bf16[16,16,128]{2,1,0:T(8,128)(2,1)S(1)}, bf16[512,256]{1,0:T(8,128)(2,1)S(1)}, bf16[384,256]{1,0:T(8,128)(2,1)S(1)}, f32[128,128]{1,0:T(8,128)...) custom-call(f32[2,128,256]{2,1,0:T(8,128)} %data.3, ...), custom_call_target="tpu_custom_call" | custom-call | tf_op jit(solution)/shard_map/pallas_call | solution.py:384
  2.7 3.1 %collective-permute-start.1 = (bf16[512,256]{1,0:T(8,128)(2,1)S(1)}, bf16[512,256]{1,0:T(8,128)(2,1)S(1)}, u32[]{:S(2)}, u32[]{:S(2)}) collective-permute-start(bf16[512,256]{1,0:T(8,128)(2,1)S(1)} %get-tuple-element.29), channel_id=1, source_target_pairs={{0,2},{1,3},{2,0},{3,1},{4,6},{5,7},{6,4},{7,5},{8,10},{9,11},{10,... | collective-permute-start | bytes 786440 | tf_op jit(solution)/shard_map/ppermute | solution.py:408
  5.8 0.1 collective-permute-start.9
  5.9 7.1 %collective-permute-done.1.far.refs_7_ = bf16[512,256]{1,0:T(8,128)(2,1)S(1)} collective-permute-done((bf16[512,256]{1,0:T(8,128)(2,1)S(1)}, bf16[512,256]{1,0:T(8,128)(2,1)S(1)}, u32[]{:S(2)}, u32[]{:S(2)}) %collective-permute-start.1) | collective-permute-done | bytes 262176 | tf_op jit(solution)/shard_map/ppermute | solution.py:408
  13.0 0.5 collective-permute-start.6
  13.5 4.3 %collective-permute-done.9.refs_9_ = bf16[512,256]{1,0:T(8,128)(2,1)S(1)} collective-permute-done((bf16[512,256]{1,0:T(8,128)(2,1)S(1)}, bf16[512,256]{1,0:T(8,128)(2,1)S(1)}, u32[]{:S(2)}, u32[]{:S(2)}) %collective-permute-start.9) | collective-permute-done | bytes 262176 | tf_op jit(solution)/shard_map/ppermute | solution.py:408
  17.7 1.7 %collective-permute-start.8 = (bf16[512,128]{1,0:T(8,128)(2,1)S(1)}, bf16[512,128]{1,0:T(8,128)(2,1)S(1)}, u32[]{:S(2)}, u32[]{:S(2)}) collective-permute-start(bf16[512,128]{1,0:T(8,128)(2,1)S(1)} %get-tuple-element.37), channel_id=1, source_target_pairs={{0,2},{1,3},{2,0},{3,1},{4,6},{5,7},{6,4},{7,5},{8,10},{9,11},{10,... | collective-permute-start | bytes 393224 | tf_op jit(solution)/shard_map/ppermute | solution.py:408
  19.5 0.2 collective-permute-start.7
  19.7 11.7 %all_to_all.10.coeffs = bf16[16,16,128]{2,1,0:T(8,128)(2,1)S(1)} all-to-all(bf16[16,16,128]{2,1,0:T(8,128)(2,1)S(1)} %get-tuple-element.25), channel_id=1, replica_groups=mesh['freq'=2,'tile'=16] {'tile'}, dimensions={0} | all-to-all | bytes 131072 | tf_op jit(solution)/shard_map/all_to_all | solution.py:411
  31.4 0.8 %shard_map.60 = (bf16[4,16,128]{2,1,0:T(8,128)(2,1)S(1)}, bf16[4,16,128]{2,1,0:T(8,128)(2,1)S(1)}, bf16[4,16,128]{2,1,0:T(8,128)(2,1)S(1)}, bf16[4,16,128]{2,1,0:T(8,128)(2,1)S(1)}) custom-call(bf16[16,16,128]{2,1,0:T(8,128)(2,1)S(1)} %all_to_all.10.coeffs, f32[128,128]{1,0:T(8,128)S(1)} %get-tuple-element.26.own.refs_4_, ...), custom_call_target="tpu_custom_call" | custom-call | tf_op jit(solution)/shard_map/pallas_call | solution.py:384
  32.2 0.2 collective-permute-start.3
  32.4 1.0 %collective-permute-start.4 = (bf16[4,16,128]{2,1,0:T(8,128)(2,1)S(1)}, bf16[4,16,128]{2,1,0:T(8,128)(2,1)S(1)}, u32[]{:S(2)}, u32[]{:S(2)}) collective-permute-start(bf16[4,16,128]{2,1,0:T(8,128)(2,1)S(1)} %get-tuple-element.32), channel_id=1, source_target_pairs={{0,8},{1,9},{2,10},{3,11},{4,12},{5,13},{6,14},{7,15},{8,0},{9,1},... | collective-permute-start | bytes 49160 | tf_op jit(solution)/shard_map/ppermute | solution.py:408
  33.4 3.3 %collective-permute-start.5 = (bf16[4,16,128]{2,1,0:T(8,128)(2,1)S(1)}, bf16[4,16,128]{2,1,0:T(8,128)(2,1)S(1)}, u32[]{:S(2)}, u32[]{:S(2)}) collective-permute-start(bf16[4,16,128]{2,1,0:T(8,128)(2,1)S(1)} %get-tuple-element.33), channel_id=1, source_target_pairs={{0,12},{1,13},{2,14},{3,15},{4,8},{5,9},{6,10},{7,11},{8,4},{9,5},... | collective-permute-start | bytes 49160 | tf_op jit(solution)/shard_map/ppermute | solution.py:408
  36.7 0.4 collective-permute-done.4.refs_2_
  37.0 1.9 %collective-permute-done.5.refs_3_ = bf16[4,16,128]{2,1,0:T(8,128)(2,1)S(1)} collective-permute-done((bf16[4,16,128]{2,1,0:T(8,128)(2,1)S(1)}, bf16[4,16,128]{2,1,0:T(8,128)(2,1)S(1)}, u32[]{:S(2)}, u32[]{:S(2)}) %collective-permute-start.5) | collective-permute-done | bytes 16416 | tf_op jit(solution)/shard_map/ppermute | solution.py:408
  38.9 1.1 %shard_map.61 = (bf16[4,16,128]{2,1,0:T(8,128)(2,1)S(1)}, bf16[4,16,128]{2,1,0:T(8,128)(2,1)S(1)}, bf16[4,16,128]{2,1,0:T(8,128)(2,1)S(1)}, bf16[4,16,128]{2,1,0...) custom-call(bf16[4,16,128]{2,1,0:T(8,128)(2,1)S(1)} %get-tuple-element, ...), custom_call_target="tpu_custom_call" | custom-call | tf_op jit(solution)/shard_map/pallas_call | solution.py:384
  40.1 3.8 %collective-permute-start.12 = (bf16[4,16,128]{2,1,0:T(8,128)(2,1)S(1)}, bf16[4,16,128]{2,1,0:T(8,128)(2,1)S(1)}, u32[]{:S(2)}, u32[]{:S(2)}) collective-permute-start(bf16[4,16,128]{2,1,0:T(8,128)(2,1)S(1)} %get-tuple-element.41), channel_id=1, source_target_pairs={{0,8},{1,9},{2,10},{3,11},{4,12},{5,13},{6,14},{7,15},{8,0},{9,1},... | collective-permute-start | bytes 49160 | tf_op jit(solution)/shard_map/ppermute | solution.py:408
  43.9 0.6 collective-permute-start.13
  44.4 1.2 %collective-permute-done.12.refs_2_ = bf16[4,16,128]{2,1,0:T(8,128)(2,1)S(1)} collective-permute-done((bf16[4,16,128]{2,1,0:T(8,128)(2,1)S(1)}, bf16[4,16,128]{2,1,0:T(8,128)(2,1)S(1)}, u32[]{:S(2)}, u32[]{:S(2)}) %collective-permute-start.12) | collective-permute-done | bytes 16416 | tf_op jit(solution)/shard_map/ppermute | solution.py:408
  45.6 3.8 %collective-permute-done.13.refs_3_ = bf16[4,16,128]{2,1,0:T(8,128)(2,1)S(1)} collective-permute-done((bf16[4,16,128]{2,1,0:T(8,128)(2,1)S(1)}, bf16[4,16,128]{2,1,0:T(8,128)(2,1)S(1)}, u32[]{:S(2)}, u32[]{:S(2)}) %collective-permute-start.13) | collective-permute-done | bytes 16416 | tf_op jit(solution)/shard_map/ppermute | solution.py:408
  49.4 1.4 %shard_map.62 = (bf16[16,16,128]{2,1,0:T(8,128)(2,1)}, bf16[256,128]{1,0:T(8,128)(2,1)S(1)}) custom-call(bf16[4,16,128]{2,1,0:T(8,128)(2,1)S(1)} %get-tuple-element.39.refs_0_, bf16[4,16,128]{2,1,0:T(8,128)(2,1)S(1)} %collective-permute-done.11.refs_1_, bf16[4,16,128]{2,1,0:T(8,128)(2,1)S(1)} %collective-permute-done.12.refs_2_, ...), custom_call_target="tpu_custom_call" | custom-call | tf_op jit(solution)/shard_map/pallas_call | solution.py:384
  50.8 0.1 collective-permute-start.18
  51.0 3.5 %all-to-all-start.1 = ((bf16[16,16,128]{2,1,0:T(8,128)(2,1)}), bf16[16,16,128]{2,1,0:T(8,128)(2,1)S(1)}, u32[]{:S(2)}, u32[]{:S(2)}) async-start(bf16[16,16,128]{2,1,0:T(8,128)(2,1)} %get-tuple-element.43), calls=%async_computation.1 | async-start | bytes 131072 | tf_op jit(solution)/shard_map/all_to_all | solution.py:411
  54.5 1.9 %collective-permute-start.15 = (bf16[2,64,128]{2,1,0:T(8,128)(2,1)S(1)}, bf16[2,64,128]{2,1,0:T(8,128)(2,1)S(1)}, u32[]{:S(2)}, u32[]{:S(2)}) collective-permute-start(bf16[2,64,128]{2,1,0:T(8,128)(2,1)S(1)} %get-tuple-element.46), channel_id=1, source_target_pairs={{0,2},{1,3},{2,0},{3,1},{4,6},{5,7},{6,4},{7,5},{8,10},{9,11},{10,... | collective-permute-start | bytes 98312 | tf_op jit(solution)/shard_map/ppermute | solution.py:408
  56.4 0.5 collective-permute-start.19
  56.9 1.6 %collective-permute-done.15.adj_far = bf16[2,64,128]{2,1,0:T(8,128)(2,1)S(1)} collective-permute-done((bf16[2,64,128]{2,1,0:T(8,128)(2,1)S(1)}, bf16[2,64,128]{2,1,0:T(8,128)(2,1)S(1)}, u32[]{:S(2)}, u32[]{:S(2)}) %collective-permute-start.15) | collective-permute-done | bytes 32800 | tf_op jit(solution)/shard_map/ppermute | solution.py:408
  58.5 0.5 collective-permute-start.14
  59.0 0.8 %collective-permute-done.14.adj_near = bf16[64,128]{1,0:T(8,128)(2,1)S(1)} collective-permute-done((bf16[64,128]{1,0:T(8,128)(2,1)S(1)}, bf16[64,128]{1,0:T(8,128)(2,1)S(1)}, u32[]{:S(2)}, u32[]{:S(2)}) %collective-permute-start.14) | collective-permute-done | bytes 16416 | tf_op jit(solution)/shard_map/ppermute | solution.py:408
  59.8 0.7 %shard_map.63.x = f32[2,512,256]{2,1,0:T(8,128)S(1)} custom-call(bf16[64,128]{1,0:T(8,128)(2,1)S(1)} %get-tuple-element.44.adj_own, bf16[64,128]{1,0:T(8,128)(2,1)S(1)} %collective-permute-done.14.adj_near, bf16[2,64,128]{2,1,0:T(8,128)(2,1)S(1)} %collective-permute-done.15.adj_far, ...), custom_call_target="tpu_custom_call", output_to_operand_aliasing={{}: (4, {})} | custom-call | tf_op jit(solution)/shard_map/pallas_call | solution.py:384
  60.6 0.2 copy-done
  60.8 0.5 shard_map.64.misfit
  61.3 1.3 %shard_map.65 = (f32[2,512,256]{2,1,0:T(8,128)}, f32[2,128,256]{2,1,0:T(8,128)}) custom-call(bf16[16,16,128]{2,1,0:T(8,128)(2,1)S(1)} %all-to-all-done.1.adjoint, f32[2,512,256]{2,1,0:T(8,128)S(1)} %shard_map.63.x, bf16[2,4,16,512]{3,2,1,0:T(8,128)(2,1)S(1)} %get-tuple-element.35.refs_5_.vfac, f32[2,128,256]{2,1,0:T(8,128)S(1)} %shard_map.64.misfit), custom_call_target="tpu_custom_call" | custom-call | tf_op jit(solution)/shard_map/pallas_call | solution.py:384
  (20 shorter events, 0.2 us)
Async XLA Ops:
  2.7 10.2 %collective-permute-start.1 = (bf16[512,256]{1,0:T(8,128)(2,1)S(1)}, bf16[512,256]{1,0:T(8,128)(2,1)S(1)}, u32[]{:S(2)}, u32[]{:S(2)}) collective-permute-start(bf16[512,256]{1,0:T(8,128)(2,1)S(1)} %get-tuple-element.29), channel_id=1, source_target_pairs={{0,2},{1,3},{2,0},{3,1},{4,6},{5,7},{6,4},{7,5},{8,10},{9,11},{10,... | collective-permute-start | bytes 786440 | tf_op jit(solution)/shard_map/ppermute | solution.py:408
  5.8 11.9 %collective-permute-start.9 = (bf16[512,256]{1,0:T(8,128)(2,1)S(1)}, bf16[512,256]{1,0:T(8,128)(2,1)S(1)}, u32[]{:S(2)}, u32[]{:S(2)}) collective-permute-start(bf16[512,256]{1,0:T(8,128)(2,1)S(1)} %get-tuple-element.38), channel_id=1, source_target_pairs={{0,2},{1,3},{2,0},{3,1},{4,6},{5,7},{6,4},{7,5},{8,10},{9,11},{10,... | collective-permute-start | bytes 786440 | tf_op jit(solution)/shard_map/ppermute | solution.py:408
  5.9 13.6 %collective-permute-start = (bf16[384,256]{1,0:T(8,128)(2,1)S(1)}, bf16[384,256]{1,0:T(8,128)(2,1)S(1)}, u32[]{:S(2)}, u32[]{:S(2)}) collective-permute-start(bf16[384,256]{1,0:T(8,128)(2,1)S(1)} %get-tuple-element.28), channel_id=1, source_target_pairs={{0,1},{1,0},{2,3},{3,2},{4,5},{5,4},{6,7},{7,6},{8,9},{9,8},{10,11... | collective-permute-start | bytes 589832 | tf_op jit(solution)/shard_map/ppermute | solution.py:408
  13.0 18.4 %collective-permute-start.2 = (bf16[512,256]{1,0:T(8,128)(2,1)S(1)}, bf16[512,256]{1,0:T(8,128)(2,1)S(1)}, u32[]{:S(2)}, u32[]{:S(2)}) collective-permute-start(bf16[512,256]{1,0:T(8,128)(2,1)S(1)} %collective-permute-done.1.far.refs_7_), channel_id=1, source_target_pairs={{0,1},{1,0},{2,3},{3,2},{4,5},{5,4},{6,7},{7,6},{8,9},{9,8},{10,11... | collective-permute-start | bytes 786440 | tf_op jit(solution)/shard_map/ppermute | solution.py:408
  13.0 23.7 %collective-permute-start.6 = (bf16[512,256]{1,0:T(8,128)(2,1)S(1)}, bf16[512,256]{1,0:T(8,128)(2,1)S(1)}, u32[]{:S(2)}, u32[]{:S(2)}) collective-permute-start(bf16[512,256]{1,0:T(8,128)(2,1)S(1)} %get-tuple-element.36), channel_id=1, source_target_pairs={{0,1},{1,0},{2,3},{3,2},{4,5},{5,4},{6,7},{7,6},{8,9},{9,8},{10,11... | collective-permute-start | bytes 786440 | tf_op jit(solution)/shard_map/ppermute | solution.py:408
  17.7 18.9 %collective-permute-start.10 = (bf16[512,256]{1,0:T(8,128)(2,1)S(1)}, bf16[512,256]{1,0:T(8,128)(2,1)S(1)}, u32[]{:S(2)}, u32[]{:S(2)}) collective-permute-start(bf16[512,256]{1,0:T(8,128)(2,1)S(1)} %collective-permute-done.9.refs_9_), channel_id=1, source_target_pairs={{0,1},{1,0},{2,3},{3,2},{4,5},{5,4},{6,7},{7,6},{8,9},{9,8},{10,11... | collective-permute-start | bytes 786440 | tf_op jit(solution)/shard_map/ppermute | solution.py:408
  17.7 14.6 %collective-permute-start.8 = (bf16[512,128]{1,0:T(8,128)(2,1)S(1)}, bf16[512,128]{1,0:T(8,128)(2,1)S(1)}, u32[]{:S(2)}, u32[]{:S(2)}) collective-permute-start(bf16[512,128]{1,0:T(8,128)(2,1)S(1)} %get-tuple-element.37), channel_id=1, source_target_pairs={{0,2},{1,3},{2,0},{3,1},{4,6},{5,7},{6,4},{7,5},{8,10},{9,11},{10,... | collective-permute-start | bytes 393224 | tf_op jit(solution)/shard_map/ppermute | solution.py:408
  19.5 13.9 %collective-permute-start.7 = (bf16[2,4,16,512]{3,2,1,0:T(8,128)(2,1)S(1)}, bf16[2,4,16,512]{3,2,1,0:T(8,128)(2,1)S(1)}, u32[]{:S(2)}, u32[]{:S(2)}) collective-permute-start(bf16[2,4,16,512]{3,2,1,0:T(8,128)(2,1)S(1)} %get-tuple-element.35.refs_5_.vfac), channel_id=1, source_target_pairs={{0,1},{1,0},{2,3},{3,2},{4,5},{5,4},{6,7},{7,6},{8,9},{9,8},{10,11... | collective-permute-start | bytes 393224 | tf_op jit(solution)/shard_map/ppermute | solution.py:408
  32.2 4.5 %collective-permute-start.3 = (bf16[4,16,128]{2,1,0:T(8,128)(2,1)S(1)}, bf16[4,16,128]{2,1,0:T(8,128)(2,1)S(1)}, u32[]{:S(2)}, u32[]{:S(2)}) collective-permute-start(bf16[4,16,128]{2,1,0:T(8,128)(2,1)S(1)} %get-tuple-element.31), channel_id=1, source_target_pairs={{0,4},{1,5},{2,6},{3,7},{4,0},{5,1},{6,2},{7,3},{8,12},{9,13},{10,... | collective-permute-start | bytes 49160 | tf_op jit(solution)/shard_map/ppermute | solution.py:408
  32.4 4.6 %collective-permute-start.4 = (bf16[4,16,128]{2,1,0:T(8,128)(2,1)S(1)}, bf16[4,16,128]{2,1,0:T(8,128)(2,1)S(1)}, u32[]{:S(2)}, u32[]{:S(2)}) collective-permute-start(bf16[4,16,128]{2,1,0:T(8,128)(2,1)S(1)} %get-tuple-element.32), channel_id=1, source_target_pairs={{0,8},{1,9},{2,10},{3,11},{4,12},{5,13},{6,14},{7,15},{8,0},{9,1},... | collective-permute-start | bytes 49160 | tf_op jit(solution)/shard_map/ppermute | solution.py:408
  33.4 5.5 %collective-permute-start.5 = (bf16[4,16,128]{2,1,0:T(8,128)(2,1)S(1)}, bf16[4,16,128]{2,1,0:T(8,128)(2,1)S(1)}, u32[]{:S(2)}, u32[]{:S(2)}) collective-permute-start(bf16[4,16,128]{2,1,0:T(8,128)(2,1)S(1)} %get-tuple-element.33), channel_id=1, source_target_pairs={{0,12},{1,13},{2,14},{3,15},{4,8},{5,9},{6,10},{7,11},{8,4},{9,5},... | collective-permute-start | bytes 49160 | tf_op jit(solution)/shard_map/ppermute | solution.py:408
  40.0 4.5 %collective-permute-start.11 = (bf16[4,16,128]{2,1,0:T(8,128)(2,1)S(1)}, bf16[4,16,128]{2,1,0:T(8,128)(2,1)S(1)}, u32[]{:S(2)}, u32[]{:S(2)}) collective-permute-start(bf16[4,16,128]{2,1,0:T(8,128)(2,1)S(1)} %get-tuple-element.40), channel_id=1, source_target_pairs={{0,4},{1,5},{2,6},{3,7},{4,0},{5,1},{6,2},{7,3},{8,12},{9,13},{10,... | collective-permute-start | bytes 49160 | tf_op jit(solution)/shard_map/ppermute | solution.py:408
  40.1 5.5 %collective-permute-start.12 = (bf16[4,16,128]{2,1,0:T(8,128)(2,1)S(1)}, bf16[4,16,128]{2,1,0:T(8,128)(2,1)S(1)}, u32[]{:S(2)}, u32[]{:S(2)}) collective-permute-start(bf16[4,16,128]{2,1,0:T(8,128)(2,1)S(1)} %get-tuple-element.41), channel_id=1, source_target_pairs={{0,8},{1,9},{2,10},{3,11},{4,12},{5,13},{6,14},{7,15},{8,0},{9,1},... | collective-permute-start | bytes 49160 | tf_op jit(solution)/shard_map/ppermute | solution.py:408
  43.9 5.5 %collective-permute-start.13 = (bf16[4,16,128]{2,1,0:T(8,128)(2,1)S(1)}, bf16[4,16,128]{2,1,0:T(8,128)(2,1)S(1)}, u32[]{:S(2)}, u32[]{:S(2)}) collective-permute-start(bf16[4,16,128]{2,1,0:T(8,128)(2,1)S(1)} %get-tuple-element.42), channel_id=1, source_target_pairs={{0,12},{1,13},{2,14},{3,15},{4,8},{5,9},{6,10},{7,11},{8,4},{9,5},... | collective-permute-start | bytes 49160 | tf_op jit(solution)/shard_map/ppermute | solution.py:408
  50.8 5.5 %collective-permute-start.18 = (bf16[256,128]{1,0:T(8,128)(2,1)S(1)}, bf16[256,128]{1,0:T(8,128)(2,1)S(1)}, u32[]{:S(2)}, u32[]{:S(2)}) collective-permute-start(bf16[256,128]{1,0:T(8,128)(2,1)S(1)} %get-tuple-element.47.own), channel_id=1, source_target_pairs={{0,2},{1,3},{2,0},{3,1},{4,6},{5,7},{6,4},{7,5},{8,10},{9,11},{10,... | collective-permute-start | bytes 196616 | tf_op jit(solution)/shard_map/ppermute | solution.py:408
  51.0 10.4 %all-to-all-start.1 = ((bf16[16,16,128]{2,1,0:T(8,128)(2,1)}), bf16[16,16,128]{2,1,0:T(8,128)(2,1)S(1)}, u32[]{:S(2)}, u32[]{:S(2)}) async-start(bf16[16,16,128]{2,1,0:T(8,128)(2,1)} %get-tuple-element.43), calls=%async_computation.1 | async-start | bytes 131072 | tf_op jit(solution)/shard_map/all_to_all | solution.py:411
  54.5 4.0 %collective-permute-start.15 = (bf16[2,64,128]{2,1,0:T(8,128)(2,1)S(1)}, bf16[2,64,128]{2,1,0:T(8,128)(2,1)S(1)}, u32[]{:S(2)}, u32[]{:S(2)}) collective-permute-start(bf16[2,64,128]{2,1,0:T(8,128)(2,1)S(1)} %get-tuple-element.46), channel_id=1, source_target_pairs={{0,2},{1,3},{2,0},{3,1},{4,6},{5,7},{6,4},{7,5},{8,10},{9,11},{10,... | collective-permute-start | bytes 98312 | tf_op jit(solution)/shard_map/ppermute | solution.py:408
  56.4 4.2 %collective-permute-start.17 = (bf16[256,128]{1,0:T(8,128)(2,1)S(1)}, bf16[256,128]{1,0:T(8,128)(2,1)S(1)}, u32[]{:S(2)}, u32[]{:S(2)}) collective-permute-start(bf16[256,128]{1,0:T(8,128)(2,1)S(1)} %get-tuple-element.47.own), channel_id=1, source_target_pairs={{0,1},{1,0},{2,3},{3,2},{4,5},{5,4},{6,7},{7,6},{8,9},{9,8},{10,11... | collective-permute-start | bytes 196616 | tf_op jit(solution)/shard_map/ppermute | solution.py:408
  56.4 4.2 %collective-permute-start.19 = (bf16[256,128]{1,0:T(8,128)(2,1)S(1)}, bf16[256,128]{1,0:T(8,128)(2,1)S(1)}, u32[]{:S(2)}, u32[]{:S(2)}) collective-permute-start(bf16[256,128]{1,0:T(8,128)(2,1)S(1)} %collective-permute-done.18.far), channel_id=1, source_target_pairs={{0,1},{1,0},{2,3},{3,2},{4,5},{5,4},{6,7},{7,6},{8,9},{9,8},{10,11... | collective-permute-start | bytes 196616 | tf_op jit(solution)/shard_map/ppermute | solution.py:408
  58.5 1.4 %collective-permute-start.16 = (bf16[2,64,128]{2,1,0:T(8,128)(2,1)S(1)}, bf16[2,64,128]{2,1,0:T(8,128)(2,1)S(1)}, u32[]{:S(2)}, u32[]{:S(2)}) collective-permute-start(bf16[2,64,128]{2,1,0:T(8,128)(2,1)S(1)} %collective-permute-done.15.adj_far), channel_id=1, source_target_pairs={{0,1},{1,0},{2,3},{3,2},{4,5},{5,4},{6,7},{7,6},{8,9},{9,8},{10,11... | collective-permute-start | bytes 98312 | tf_op jit(solution)/shard_map/ppermute | solution.py:408
  58.5 1.3 %collective-permute-start.14 = (bf16[64,128]{1,0:T(8,128)(2,1)S(1)}, bf16[64,128]{1,0:T(8,128)(2,1)S(1)}, u32[]{:S(2)}, u32[]{:S(2)}) collective-permute-start(bf16[64,128]{1,0:T(8,128)(2,1)S(1)} %get-tuple-element.45), channel_id=1, source_target_pairs={{0,1},{1,0},{2,3},{3,2},{4,5},{5,4},{6,7},{7,6},{8,9},{9,8},{10,11... | collective-permute-start | bytes 49160 | tf_op jit(solution)/shard_map/ppermute | solution.py:408
  59.8 1.0 %copy-start = (f32[2,128,256]{2,1,0:T(8,128)S(1)}, f32[2,128,256]{2,1,0:T(8,128)}, u32[]{:S(2)}) copy-start(f32[2,128,256]{2,1,0:T(8,128)} %data.3) | copy-start | bytes 786436
